TPU v7x, 32 devices: a whole 2x2x4 slice. The times are simulated.
32 devices in a mesh: fsdp: 8 (over z, core), tp: 4 (over y, x).
Axes of the slice: x: 2, y: 2, z: 4, core: 2. Of those that a mesh axis runs over, the one named last changes fastest.
Arguments:
- tokens_in: bfloat16 [16384, 1536], P(('fsdp', 'tp')), may hold values from -6 to 6
- cotangent: bfloat16 [16384, 1536], P(('fsdp', 'tp')), may hold values from -6 to 6
- piece_starts: int32 [16, 2], P('fsdp'), may hold values from 0 to 768, as said below
- adapter_ids: int32 [16], P('fsdp'), may hold values from 0 to 7, as said below
- gain_att: bfloat16 [1, 1536], P(None, ('fsdp', 'tp')), may hold values from 0.5 to 1.5
- w_in: bfloat16 [1, 1536, 4, 1536], P(None, 'fsdp', None, 'tp'), may hold values from -0.15625 to 0.15625
- w_forget: bfloat16 [1, 1536, 24], P(None, 'fsdp', 'tp'), may hold values from -0.078125 to 0.078125
- bias_forget: bfloat16 [1, 24], P(None, 'tp'), may hold values from 2.5 to 8
- w_out: bfloat16 [1, 1536, 1536], P(None, 'tp', 'fsdp'), may hold values from -0.625 to 0.625
- gain_mlp: bfloat16 [1, 1536], P(None, ('fsdp', 'tp')), may hold values from 0.5 to 1.5
- w_gate_up: bfloat16 [1, 1536, 2, 4096], P(None, 'fsdp', None, 'tp'), may hold values from -0.15625 to 0.15625
- w_down: bfloat16 [1, 4096, 1536], P(None, 'tp', 'fsdp'), may hold values from -0.1875 to 0.1875
- adapt_in_a: bfloat16 [1, 1536, 640], P(None, ('fsdp', 'tp')), may hold values from -0.15625 to 0.15625
- adapt_in_b: bfloat16 [1, 4, 128, 1536], P(None, None, 'fsdp', 'tp'), may hold values from -1.5 to 1.5
- adapt_forget_b: bfloat16 [1, 128, 24], P(None, 'fsdp', 'tp'), may hold values from -0.75 to 0.75
- adapt_out_a: bfloat16 [1, 1536, 128], P(None, 'tp', 'fsdp'), may hold values from -0.625 to 0.625
- adapt_out_b: bfloat16 [1, 128, 1536], P(None, None, ('fsdp', 'tp')), may hold values from -1.5 to 1.5
- adapt_mlp_a: bfloat16 [1, 1536, 256], P(None, ('fsdp', 'tp')), may hold values from -0.15625 to 0.15625
- adapt_gu_b: bfloat16 [1, 2, 128, 4096], P(None, None, 'fsdp', 'tp'), may hold values from -1.5 to 1.5
- adapt_down_a: bfloat16 [1, 4096, 128], P(None, 'tp', 'fsdp'), may hold values from -0.1875 to 0.1875
- adapt_down_b: bfloat16 [1, 128, 1536], P(None, None, ('fsdp', 'tp')), may hold values from -1.5 to 1.5
Outputs:
- activations: bfloat16 [16384, 1536], P(('fsdp', 'tp'))
- input_grad: float32 [16384, 1536], P(('fsdp', 'tp'))
- grad_in_a: float32 [1, 1536, 640], P(None, ('fsdp', 'tp'))
- grad_in_b: float32 [1, 4, 128, 1536], P(None, None, 'fsdp', 'tp')
- grad_forget_b: float32 [1, 128, 24], P(None, 'fsdp', 'tp')
- grad_out_a: float32 [1, 1536, 128], P(None, 'tp', 'fsdp')
- grad_out_b: float32 [1, 128, 1536], P(None, None, ('fsdp', 'tp'))
- grad_mlp_a: float32 [1, 1536, 256], P(None, ('fsdp', 'tp'))
- grad_gu_b: float32 [1, 2, 128, 4096], P(None, None, 'fsdp', 'tp')
- grad_down_a: float32 [1, 4096, 128], P(None, 'tp', 'fsdp')
- grad_down_b: float32 [1, 128, 1536], P(None, None, ('fsdp', 'tp'))
Inputs may be any that keep to these rules, and one draw needn't show every extreme that they name: `piece_starts`: each sequence has 2 picture pieces of 256 positions, given by their first positions in increasing order; they do not intersect and lie inside the sequence. `adapter_ids`: every one of the 8 adapters is used by some sequence.
All inputs are finite; a program needn't handle non-finite values.
Results may differ from a plain program's by a relative error of at most 0.023.
Values may be sent and summed in bfloat16 or wider, within the bound.
No kernel may reach another device: no remote copies, remote signals or barrier semaphores. Data moves between devices by JAX's collectives and lax.ppermute only.
A program may use at most 256 MiB of HBM per device.

v0:
```python
import jax
import jax.numpy as jnp
from jax import lax
from jax.sharding import PartitionSpec as P

HEAD = 64
RANK = 16
PIECE = 256
PIECES = 2
LEN = 1024


epsilon = 1e-06
masked_score = -1e30


def rms_rows(hidden, gain_vec):
    inv_rms = lax.rsqrt(jnp.mean(hidden * hidden, axis=-1, keepdims=True) + epsilon)
    return ((hidden * inv_rms * gain_vec).astype(jnp.bfloat16), inv_rms)


def rms_back(hidden, inv_rms, gain_vec, grad_normed):
    weighted = grad_normed * gain_vec
    return inv_rms * weighted - hidden * inv_rms**3 * jnp.mean(
        weighted * hidden, axis=-1, keepdims=True
    )


def log_gate(logits):
    return -jnp.log1p(jnp.exp(-logits))


def allowed_pairs(starts):
    positions = jnp.arange(LEN)
    inside = (positions[:, None] >= starts[None, :]) & (
        positions[:, None] < starts[None, :] + PIECE
    )
    labels = jnp.sum(inside.astype(jnp.int32) * (jnp.arange(PIECES)[None, :] + 1), axis=1)
    return (positions[None, :] <= positions[:, None]) | (labels[:, None] == labels[None, :]) & (
        labels[:, None] > 0
    )


def earlier_mask():
    positions = jnp.arange(LEN)
    return positions[None, :] <= positions[:, None]


def adapter_mask(adapter_ids, row_count, row_start, adapter_width):
    seq_index = (row_start + jnp.arange(row_count)) // LEN
    seq_match = seq_index[:, None] == jnp.arange(adapter_ids.shape[0])[None, :]
    token_ids = jnp.sum(jnp.where(seq_match, adapter_ids[None, :], 0), axis=1)
    mask_one = ((jnp.arange(adapter_width) // RANK)[None, :] == token_ids[:, None]).astype(
        jnp.bfloat16
    )
    return (mask_one, seq_match.astype(jnp.bfloat16))


def heads_first(values_in, heads_here):
    return values_in.reshape(-1, LEN, heads_here, HEAD).transpose(0, 2, 1, 3)


def rows_back(values_in, group_rows):
    return values_in.transpose(0, 2, 1, 3).reshape(group_rows, -1)


def scores_of(queries, key_rows, cum_t, allowed):
    scores = jnp.einsum(
        "hid,hjd->hij", queries, key_rows, preferred_element_type=jnp.float32
    ) * HEAD ** (-0.5)
    decay = jnp.where(
        earlier_mask()[None],
        cum_t[:, :, None] - cum_t[:, None, :],
        cum_t[:, None, :] - cum_t[:, :, None],
    )
    return jnp.where(allowed[None], scores + decay, masked_score)


def attend_forward(packed):
    queries, key_rows, values, cum_t, allowed = packed
    scores = scores_of(queries, key_rows, cum_t, allowed)
    row_max = jnp.max(scores, axis=-1, keepdims=True)
    weights = jnp.exp(scores - row_max)
    totals = jnp.sum(weights, axis=-1, keepdims=True)
    prob_bf = (weights / totals).astype(jnp.bfloat16)
    mixed_out = jnp.einsum("hij,hjd->hid", prob_bf, values, preferred_element_type=jnp.float32)
    return (mixed_out, row_max, totals)


def attend_back(packed):
    queries, key_rows, values, cum_t, allowed, row_max, totals, grad_mixed = packed
    scores = scores_of(queries, key_rows, cum_t, allowed)
    probs = jnp.exp(scores - row_max) / totals
    prob_bf = probs.astype(jnp.bfloat16)
    grad_probs = jnp.einsum("hid,hjd->hij", grad_mixed, values, preferred_element_type=jnp.float32)
    grad_scores = (
        probs * (grad_probs - jnp.sum(probs * grad_probs, axis=-1, keepdims=True))
    ).astype(jnp.bfloat16)
    grad_query = jnp.einsum(
        "hij,hjd->hid", grad_scores, key_rows, preferred_element_type=jnp.float32
    ) * HEAD ** (-0.5)
    grad_key = jnp.einsum(
        "hij,hid->hjd", grad_scores, queries, preferred_element_type=jnp.float32
    ) * HEAD ** (-0.5)
    grad_value = jnp.einsum("hij,hid->hjd", prob_bf, grad_mixed, preferred_element_type=jnp.float32)
    signed = jnp.where(earlier_mask()[None], 1.0, -1.0) * grad_scores.astype(jnp.float32)
    grad_cum = jnp.sum(signed, axis=-1) - jnp.sum(signed, axis=-2)
    return (grad_query, grad_key, grad_value, grad_cum)


def attention_forward(hidden, frozen, shared, bias_vec, masks, allowed):
    w_in, w_forget, w_out, b_in, b_forget, a_out = frozen[:6]
    gain_vec, a_in, b_out = shared[:3]
    mask_one, mask_two, mask_five, seq_hot = masks
    normed, inv_rms = rms_rows(hidden, gain_vec.astype(jnp.float32))
    low_in = (
        jnp.dot(normed, a_in, preferred_element_type=jnp.float32).astype(jnp.bfloat16) * mask_five
    )
    normed_all, low_all = (
        lax.all_gather(normed, "tp", axis=0, tiled=True),
        lax.all_gather(low_in, "tp", axis=0, tiled=True),
    )
    group_rows = normed_all.shape[0]
    heads_here = w_forget.shape[1]
    low_parts = low_all.reshape(group_rows, 5, -1)
    projected = jnp.einsum("td,dkh->tkh", normed_all, w_in, preferred_element_type=jnp.float32)
    projected = projected + jnp.einsum(
        "tkr,krh->tkh", low_parts[:, :4], b_in, preferred_element_type=jnp.float32
    )
    forget_logits = (
        jnp.dot(normed_all, w_forget, preferred_element_type=jnp.float32)
        + jnp.dot(low_parts[:, 4], b_forget, preferred_element_type=jnp.float32)
        + bias_vec.astype(jnp.float32)
    )
    queries = heads_first(projected[:, 0].astype(jnp.bfloat16), heads_here)
    key_rows = heads_first(projected[:, 1].astype(jnp.bfloat16), heads_here)
    values = heads_first(projected[:, 2].astype(jnp.bfloat16), heads_here)
    out_gate = jax.nn.sigmoid(projected[:, 3])
    cum_t = jnp.cumsum(log_gate(forget_logits).reshape(-1, LEN, heads_here), axis=1).transpose(
        0, 2, 1
    )
    mixed_out, row_max, totals = lax.map(
        attend_forward, (queries, key_rows, values, cum_t, allowed)
    )
    mixed_rows = rows_back(mixed_out, group_rows)
    merged = (mixed_rows * out_gate).astype(jnp.bfloat16)
    out_part = jnp.dot(merged, w_out, preferred_element_type=jnp.float32)
    low_part = jnp.dot(merged, a_out, preferred_element_type=jnp.float32)
    branch, low_sum = (
        lax.psum_scatter(out_part, "tp", scatter_dimension=0, tiled=True),
        lax.psum_scatter(low_part, "tp", scatter_dimension=0, tiled=True),
    )
    low_out = low_sum.astype(jnp.bfloat16) * mask_one
    branch = branch + jnp.dot(low_out, b_out, preferred_element_type=jnp.float32)
    kept = (
        hidden,
        inv_rms,
        normed,
        low_parts,
        queries,
        key_rows,
        values,
        out_gate,
        mixed_rows,
        forget_logits,
        cum_t,
        row_max,
        totals,
        merged,
        low_out,
    )
    return (hidden + branch, kept)


def attention_backward(grad_rows, frozen, shared, kept, masks, allowed):
    w_in, w_forget, w_out, b_in, b_forget, a_out = frozen[:6]
    gain_vec, a_in, b_out = shared[:3]
    mask_one, mask_two, mask_five, seq_hot = masks
    (
        hidden,
        inv_rms,
        normed,
        low_parts,
        queries,
        key_rows,
        values,
        out_gate,
        mixed_rows,
        forget_logits,
        cum_t,
        row_max,
        totals,
        merged,
        low_out,
    ) = kept
    group_rows = mixed_rows.shape[0]
    heads_here = w_forget.shape[1]
    grad_branch = grad_rows.astype(jnp.bfloat16)
    grad_out_b = jnp.dot(low_out.T, grad_branch, preferred_element_type=jnp.float32)
    grad_low = (
        jnp.dot(grad_branch, b_out.T, preferred_element_type=jnp.float32) * mask_one
    ).astype(jnp.bfloat16)
    branch_all, low_all = (
        lax.all_gather(grad_branch, "tp", axis=0, tiled=True),
        lax.all_gather(grad_low, "tp", axis=0, tiled=True),
    )
    grad_merged = jnp.dot(branch_all, w_out.T, preferred_element_type=jnp.float32) + jnp.dot(
        low_all, a_out.T, preferred_element_type=jnp.float32
    )
    grad_out_a = jnp.dot(merged.T, low_all, preferred_element_type=jnp.float32)
    grad_mixed = heads_first((grad_merged * out_gate).astype(jnp.bfloat16), heads_here)
    grad_gate = (grad_merged * mixed_rows * out_gate * (1.0 - out_gate)).astype(jnp.bfloat16)
    grad_query, grad_key, grad_value, grad_cum = lax.map(
        attend_back, (queries, key_rows, values, cum_t, allowed, row_max, totals, grad_mixed)
    )
    grad_log = (
        jnp.flip(jnp.cumsum(jnp.flip(grad_cum, 2), axis=2), 2)
        .transpose(0, 2, 1)
        .reshape(group_rows, heads_here)
    )
    grad_logits = (grad_log * jax.nn.sigmoid(-forget_logits)).astype(jnp.bfloat16)
    grad_proj = jnp.stack(
        [
            rows_back(grad_query, group_rows).astype(jnp.bfloat16),
            rows_back(grad_key, group_rows).astype(jnp.bfloat16),
            rows_back(grad_value, group_rows).astype(jnp.bfloat16),
            grad_gate,
        ],
        axis=1,
    )
    grad_normed = jnp.einsum(
        "tkh,dkh->td", grad_proj, w_in, preferred_element_type=jnp.float32
    ) + jnp.dot(grad_logits, w_forget.T, preferred_element_type=jnp.float32)
    grad_parts = jnp.concatenate(
        [
            jnp.einsum("tkh,krh->tkr", grad_proj, b_in, preferred_element_type=jnp.float32),
            jnp.dot(grad_logits, b_forget.T, preferred_element_type=jnp.float32)[:, None, :],
        ],
        axis=1,
    ).reshape(group_rows, -1)
    grad_in_b = jnp.einsum(
        "tkr,tkh->krh", low_parts[:, :4], grad_proj, preferred_element_type=jnp.float32
    )
    grad_forget_b = jnp.dot(low_parts[:, 4].T, grad_logits, preferred_element_type=jnp.float32)
    grad_normed, grad_low_in = (
        lax.psum_scatter(
            grad_normed.astype(jnp.bfloat16), "tp", scatter_dimension=0, tiled=True
        ).astype(jnp.float32),
        lax.psum_scatter(
            grad_parts.astype(jnp.bfloat16), "tp", scatter_dimension=0, tiled=True
        ).astype(jnp.float32),
    )
    grad_low_in = (grad_low_in * mask_five).astype(jnp.bfloat16)
    grad_in_a = jnp.dot(normed.T, grad_low_in, preferred_element_type=jnp.float32)
    grad_normed = grad_normed + jnp.dot(grad_low_in, a_in.T, preferred_element_type=jnp.float32)
    grad_rows = grad_rows + rms_back(hidden, inv_rms, gain_vec.astype(jnp.float32), grad_normed)
    return (grad_rows, (grad_in_b, grad_forget_b, grad_out_a), (grad_in_a, grad_out_b))


def mlp_forward(hidden, frozen, shared, masks):
    w_gate_up, w_down, b_gu, a_down = frozen[6:]
    gain_vec, a_mlp, b_down = shared[3:]
    mask_one, mask_two, mask_five, seq_hot = masks
    normed, inv_rms = rms_rows(hidden, gain_vec.astype(jnp.float32))
    low_in = (
        jnp.dot(normed, a_mlp, preferred_element_type=jnp.float32).astype(jnp.bfloat16) * mask_two
    )
    normed_all, low_all = (
        lax.all_gather(normed, "tp", axis=0, tiled=True),
        lax.all_gather(low_in, "tp", axis=0, tiled=True),
    )
    group_rows = normed_all.shape[0]
    low_parts = low_all.reshape(group_rows, 2, -1)
    pre_act = jnp.einsum("td,dkf->tkf", normed_all, w_gate_up, preferred_element_type=jnp.float32)
    pre_act = pre_act + jnp.einsum(
        "tkr,krf->tkf", low_parts, b_gu, preferred_element_type=jnp.float32
    )
    gate_pre = pre_act[:, 0]
    inner_act = (gate_pre * jax.nn.sigmoid(gate_pre) * pre_act[:, 1]).astype(jnp.bfloat16)
    out_part = jnp.dot(inner_act, w_down, preferred_element_type=jnp.float32)
    low_part = jnp.dot(inner_act, a_down, preferred_element_type=jnp.float32)
    branch, low_sum = (
        lax.psum_scatter(
            out_part.astype(jnp.bfloat16), "tp", scatter_dimension=0, tiled=True
        ).astype(jnp.float32),
        lax.psum_scatter(
            low_part.astype(jnp.bfloat16), "tp", scatter_dimension=0, tiled=True
        ).astype(jnp.float32),
    )
    low_out = low_sum.astype(jnp.bfloat16) * mask_one
    branch = branch + jnp.dot(low_out, b_down, preferred_element_type=jnp.float32)
    kept = (hidden, inv_rms, normed, low_parts, pre_act, inner_act, low_out)
    return (hidden + branch, kept)


def mlp_backward(grad_rows, frozen, shared, kept, masks):
    w_gate_up, w_down, b_gu, a_down = frozen[6:]
    gain_vec, a_mlp, b_down = shared[3:]
    mask_one, mask_two, mask_five, seq_hot = masks
    hidden, inv_rms, normed, low_parts, pre_act, inner_act, low_out = kept
    group_rows = pre_act.shape[0]
    grad_branch = grad_rows.astype(jnp.bfloat16)
    grad_down_b = jnp.dot(low_out.T, grad_branch, preferred_element_type=jnp.float32)
    grad_low = (
        jnp.dot(grad_branch, b_down.T, preferred_element_type=jnp.float32) * mask_one
    ).astype(jnp.bfloat16)
    branch_all, low_all = (
        lax.all_gather(grad_branch, "tp", axis=0, tiled=True),
        lax.all_gather(grad_low, "tp", axis=0, tiled=True),
    )
    grad_inner = jnp.dot(branch_all, w_down.T, preferred_element_type=jnp.float32) + jnp.dot(
        low_all, a_down.T, preferred_element_type=jnp.float32
    )
    grad_down_a = jnp.dot(inner_act.T, low_all, preferred_element_type=jnp.float32)
    gate_pre = pre_act[:, 0]
    up_act = pre_act[:, 1]
    sigmoid_g = jax.nn.sigmoid(gate_pre)
    grad_gate = grad_inner * up_act * sigmoid_g * (1.0 + gate_pre * (1.0 - sigmoid_g))
    grad_up = grad_inner * gate_pre * sigmoid_g
    grad_pre = jnp.stack([grad_gate, grad_up], axis=1).astype(jnp.bfloat16)
    grad_normed = jnp.einsum("tkf,dkf->td", grad_pre, w_gate_up, preferred_element_type=jnp.float32)
    grad_parts = jnp.einsum(
        "tkf,krf->tkr", grad_pre, b_gu, preferred_element_type=jnp.float32
    ).reshape(group_rows, -1)
    grad_gu_b = jnp.einsum("tkr,tkf->krf", low_parts, grad_pre, preferred_element_type=jnp.float32)
    grad_normed, grad_low_in = (
        lax.psum_scatter(grad_normed, "tp", scatter_dimension=0, tiled=True),
        lax.psum_scatter(grad_parts, "tp", scatter_dimension=0, tiled=True),
    )
    grad_low_in = (grad_low_in * mask_two).astype(jnp.bfloat16)
    grad_mlp_a = jnp.dot(normed.T, grad_low_in, preferred_element_type=jnp.float32)
    grad_normed = grad_normed + jnp.dot(grad_low_in, a_mlp.T, preferred_element_type=jnp.float32)
    grad_rows = grad_rows + rms_back(hidden, inv_rms, gain_vec.astype(jnp.float32), grad_normed)
    return (grad_rows, (grad_gu_b, grad_down_a), (grad_mlp_a, grad_down_b))


def stack_layers(per_layer):
    return jax.tree.map(lambda *stacked: jnp.stack(stacked), *per_layer)


def on_device(
    tokens_in,
    cotangent,
    piece_starts,
    adapter_ids,
    gain_att,
    w_in,
    w_forget,
    bias_forget,
    w_out,
    gain_mlp,
    w_gate_up,
    w_down,
    adapt_in_a,
    adapt_in_b,
    adapt_forget_b,
    adapt_out_a,
    adapt_out_b,
    adapt_mlp_a,
    adapt_gu_b,
    adapt_down_a,
    adapt_down_b,
):
    row_count = tokens_in.shape[0]
    adapter_width = adapt_out_b.shape[1]
    layer_count = w_in.shape[0]
    mask_one, seq_hot = adapter_mask(
        adapter_ids, row_count, lax.axis_index("tp") * row_count, adapter_width
    )
    masks = (
        mask_one,
        jnp.concatenate([mask_one] * 2, axis=1),
        jnp.concatenate([mask_one] * 5, axis=1),
        seq_hot,
    )
    allowed = jax.vmap(allowed_pairs)(piece_starts)

    def frozen_pieces(layer_index):
        return (
            lax.all_gather(w_in[layer_index], "fsdp", axis=0, tiled=True),
            lax.all_gather(w_forget[layer_index], "fsdp", axis=0, tiled=True),
            lax.all_gather(w_out[layer_index], "fsdp", axis=1, tiled=True),
            lax.all_gather(adapt_in_b[layer_index], "fsdp", axis=1, tiled=True),
            lax.all_gather(adapt_forget_b[layer_index], "fsdp", axis=0, tiled=True),
            lax.all_gather(adapt_out_a[layer_index], "fsdp", axis=1, tiled=True),
            lax.all_gather(w_gate_up[layer_index], "fsdp", axis=0, tiled=True),
            lax.all_gather(w_down[layer_index], "fsdp", axis=1, tiled=True),
            lax.all_gather(adapt_gu_b[layer_index], "fsdp", axis=1, tiled=True),
            lax.all_gather(adapt_down_a[layer_index], "fsdp", axis=1, tiled=True),
        )

    def shared_pieces(layer_index):
        return (
            lax.all_gather(gain_att[layer_index], ("fsdp", "tp"), axis=0, tiled=True),
            lax.all_gather(adapt_in_a[layer_index], ("fsdp", "tp"), axis=0, tiled=True),
            lax.all_gather(adapt_out_b[layer_index], ("fsdp", "tp"), axis=1, tiled=True),
            lax.all_gather(gain_mlp[layer_index], ("fsdp", "tp"), axis=0, tiled=True),
            lax.all_gather(adapt_mlp_a[layer_index], ("fsdp", "tp"), axis=0, tiled=True),
            lax.all_gather(adapt_down_b[layer_index], ("fsdp", "tp"), axis=1, tiled=True),
        )

    hidden = tokens_in.astype(jnp.float32)
    layer_index = 0
    frozen = frozen_pieces(layer_index)
    shared = shared_pieces(layer_index)
    hidden, kept_att = attention_forward(
        hidden, frozen, shared, bias_forget[layer_index], masks, allowed
    )
    hidden, kept_mlp = mlp_forward(hidden, frozen, shared, masks)
    saved_list = [(frozen, shared, kept_att, kept_mlp)]
    result = hidden.astype(jnp.bfloat16)
    grad_rows = cotangent.astype(jnp.float32)
    parts_fsdp = [None] * layer_count
    parts_all = [None] * layer_count
    for layer_index in reversed(range(layer_count)):
        frozen, shared, kept_att, kept_mlp = saved_list[layer_index]
        frozen = frozen_pieces(layer_index)
        shared = shared_pieces(layer_index)
        grad_rows, mlp_fsdp, mlp_all = mlp_backward(grad_rows, frozen, shared, kept_mlp, masks)
        grad_rows, att_fsdp, att_all = attention_backward(
            grad_rows, frozen, shared, kept_att, masks, allowed
        )
        parts_fsdp[layer_index] = att_fsdp + mlp_fsdp
        parts_all[layer_index] = (att_all[0], att_all[1], mlp_all[0], mlp_all[1])
    layer_index = 0
    part_in_b, part_forget_b, part_out_a, part_gu_b, part_down_a = parts_fsdp[layer_index]
    reduced_fsdp = [
        (
            lax.psum_scatter(
                part_in_b.astype(jnp.bfloat16), "fsdp", scatter_dimension=1, tiled=True
            ).astype(jnp.float32),
            lax.psum_scatter(
                part_forget_b.astype(jnp.bfloat16), "fsdp", scatter_dimension=0, tiled=True
            ).astype(jnp.float32),
            lax.psum_scatter(
                part_out_a.astype(jnp.bfloat16), "fsdp", scatter_dimension=1, tiled=True
            ).astype(jnp.float32),
            lax.psum_scatter(
                part_gu_b.astype(jnp.bfloat16), "fsdp", scatter_dimension=1, tiled=True
            ).astype(jnp.float32),
            lax.psum_scatter(
                part_down_a.astype(jnp.bfloat16), "fsdp", scatter_dimension=1, tiled=True
            ).astype(jnp.float32),
        )
    ]
    summed_fsdp = stack_layers(reduced_fsdp)
    layer_index = 0
    part_in_a, part_out_b, part_mlp_a, part_down_b = parts_all[layer_index]
    reduced_all = [
        (
            lax.psum_scatter(part_in_a, ("fsdp", "tp"), scatter_dimension=0, tiled=True),
            lax.psum_scatter(part_out_b, ("fsdp", "tp"), scatter_dimension=1, tiled=True),
            lax.psum_scatter(part_mlp_a, ("fsdp", "tp"), scatter_dimension=0, tiled=True),
            lax.psum_scatter(part_down_b, ("fsdp", "tp"), scatter_dimension=1, tiled=True),
        )
    ]
    summed_all = stack_layers(reduced_all)
    grad_in_b, grad_forget_b, grad_out_a, grad_gu_b, grad_down_a = summed_fsdp
    grad_in_a, grad_out_b, grad_mlp_a, grad_down_b = summed_all
    return (
        result,
        grad_rows,
        grad_in_a,
        grad_in_b,
        grad_forget_b,
        grad_out_a,
        grad_out_b,
        grad_mlp_a,
        grad_gu_b,
        grad_down_a,
        grad_down_b,
    )


def solution(mesh):
    return jax.shard_map(
        on_device,
        mesh=mesh,
        in_specs=(
            P(("fsdp", "tp"), None),
            P(("fsdp", "tp"), None),
            P("fsdp", None),
            P("fsdp"),
            P(None, ("fsdp", "tp")),
            P(None, "fsdp", None, "tp"),
            P(None, "fsdp", "tp"),
            P(None, "tp"),
            P(None, "tp", "fsdp"),
            P(None, ("fsdp", "tp")),
            P(None, "fsdp", None, "tp"),
            P(None, "tp", "fsdp"),
            P(None, ("fsdp", "tp"), None),
            P(None, None, "fsdp", "tp"),
            P(None, "fsdp", "tp"),
            P(None, "tp", "fsdp"),
            P(None, None, ("fsdp", "tp")),
            P(None, ("fsdp", "tp"), None),
            P(None, None, "fsdp", "tp"),
            P(None, "tp", "fsdp"),
            P(None, None, ("fsdp", "tp")),
        ),
        out_specs=(
            P(("fsdp", "tp"), None),
            P(("fsdp", "tp"), None),
            P(None, ("fsdp", "tp"), None),
            P(None, None, "fsdp", "tp"),
            P(None, "fsdp", "tp"),
            P(None, "tp", "fsdp"),
            P(None, None, ("fsdp", "tp")),
            P(None, ("fsdp", "tp"), None),
            P(None, None, "fsdp", "tp"),
            P(None, "tp", "fsdp"),
            P(None, None, ("fsdp", "tp")),
        ),
        check_vma=False,
    )
```

profile of v0, /device:TPU:0, one launch (start us, length us, event | category | flops | bytes accessed | tf_op | source)
XLA Modules:
  0.0 2117.3 jit_solution(17654208218768773041)
XLA Ops:
  9.7 42.2 %all-reduce.2 = (bf16[1536]{0:T(1024)(128)(2,1)S(1)}, bf16[1536]{0:T(1024)(128)(2,1)}) all-reduce(bf16[1536]{0:T(1024)(128)(2,1)S(1)} %dynamic-update-slice, bf16[1536]{0:T(1024)(128)(2,1)S(1)} %dynamic-update-slice.1), channel_id=2, replica_groups=mesh['fsdp'=8,'tp'=4] {'fsdp','tp'}, use_global_device_ids=true, to_apply=%add | all-reduce | flops 3072 | bytes 12288
  153.3 31.4 %all-gather.28.cloned.1.call-done = bf16[2048,1536]{1,0:T(8,128)(2,1)} async-done(((bf16[512,1536]{1,0:T(8,128)(2,1)}), bf16[2048,1536]{1,0:T(8,128)(2,1)}) %all-gather.28.cloned.1.call-update) | async-done | bytes 6291472 | tf_op jit(solution)/shard_map/all_gather | solution.py:120
  196.0 41.6 %all-gather.40.cloned.1.call-done = bf16[1,1536,4,384]{3,1,2,0:T(8,128)(2,1)} async-done(((bf16[1,192,4,384]{3,1,2,0:T(8,128)(2,1)}), bf16[1,1536,4,384]{3,1,2,0:T(8,128)(2,1)}) %all-gather.40.cloned.1.call-update) | async-done | bytes 4718608 | tf_op jit(solution)/shard_map/all_gather | solution.py:380
  286.2 75.9 %while.32 = (s32[]{:T(128)}, f32[2,6,1024,64]{2,3,1,0:T(8,128)}, f32[2,6,1024,1]{2,1,3,0:T(8,128)}, f32[2,6,1024,1]{2,1,3,0:T(8,128)}, pred[2,1024,1024]{1,2,0:T...) while((s32[]{:T(128)}, f32[2,6,1024,64]{2,3,1,0:T(8,128)}, ...), condition=%wide.region_8.9_spmd.clone, body=%wide.region_5.8_spmd.sunk.clone | while | flops 1687146496 | bytes 129083648 | solution.py:142
  385.7 69.5 %all-gather.8 = bf16[1,128,1536]{1,2,0:T(8,128)(2,1)S(1)} all-gather(bf16[1,128,48]{1,2,0:T(8,128)(2,1)S(1)} %copy-done.77), channel_id=10, replica_groups=mesh['fsdp'=8,'tp'=4] {'fsdp','tp'}, dimensions={2}, use_global_device_ids=true | all-gather | bytes 405504 | tf_op jit(solution)/shard_map/all_gather | solution.py:396
  456.1 76.2 %all-gather.11 = bf16[1,1536,256]{2,1,0:T(8,128)(2,1)} all-gather(bf16[1,48,256]{2,1,0:T(8,128)(2,1)S(1)} %copy-done.73), channel_id=13, replica_groups=mesh['fsdp'=8,'tp'=4] {'fsdp','tp'}, dimensions={1}, use_global_device_ids=true | all-gather | bytes 811008 | tf_op jit(solution)/shard_map/all_gather | solution.py:398
  558.9 71.1 %all-gather.15 = bf16[1,128,1536]{1,2,0:T(8,128)(2,1)S(1)} all-gather(bf16[1,128,48]{1,2,0:T(8,128)(2,1)} %param.45), channel_id=17, replica_groups=mesh['fsdp'=8,'tp'=4] {'fsdp','tp'}, dimensions={2}, use_global_device_ids=true | all-gather | bytes 405504 | tf_op jit(solution)/shard_map/all_gather | solution.py:399
  694.2 64.1 %all-gather.46.cloned.1.call-done = bf16[1,1536,2,1024]{3,1,2,0:T(8,128)(2,1)} async-done(((bf16[1,192,2,1024]{3,1,2,0:T(8,128)(2,1)}), bf16[1,1536,2,1024]{3,1,2,0:T(8,128)(2,1)}) %all-gather.46.cloned.1.call-update) | async-done | bytes 6291472 | tf_op jit(solution)/shard_map/all_gather | solution.py:386
  758.3 70.4 %all-gather.32.cloned.1.call-done = bf16[2048,1536]{1,0:T(8,128)(2,1)} async-done(((bf16[512,1536]{1,0:T(8,128)(2,1)}), bf16[2048,1536]{1,0:T(8,128)(2,1)}) %all-gather.32.cloned.1.call-update) | async-done | bytes 6291472 | tf_op jit(solution)/shard_map/all_gather | solution.py:269
  922.6 123.6 %reduce-scatter.28.cloned.1.call-done = f32[512,1536]{1,0:T(8,128)} async-done(((f32[2048,1536]{1,0:T(8,128)}), f32[512,1536]{1,0:T(8,128)}) %reduce-scatter.28.cloned.1.call-update) | async-done | bytes 3145744 | tf_op jit(solution)/shard_map/reduce_scatter | solution.py:327
  1076.0 51.0 %all-gather.38.cloned.1.call-done = bf16[2048,1536]{1,0:T(8,128)(2,1)} async-done(((bf16[512,1536]{1,0:T(8,128)(2,1)}), bf16[2048,1536]{1,0:T(8,128)(2,1)}) %all-gather.38.cloned.1.call-update) | async-done | bytes 6291472 | tf_op jit(solution)/shard_map/all_gather | solution.py:204
  1147.6 171.5 %while.33 = (s32[]{:T(128)}, bf16[2,6,1024,64]{2,3,1,0:T(8,128)(2,1)}, bf16[2,6,1024,64]{2,3,1,0:T(8,128)(2,1)}, bf16[2,6,1024,64]{2,3,1,0:T(8,128)(2,1)}, f32[2...) while((s32[]{:T(128)}, ...), condition=%wide.region_21.22_spmd.clone, body=%wide.region_17.21_spmd.sunk.clone | while | flops 4143697920 | bytes 250828080 | solution.py:213
  1160.2 22.5 %multiply_reduce_fusion.5 = (f32[6,1024]{1,0:T(8,128)S(1)}, f32[6,1024,1024]{1,2,0:T(8,128)}) fusion(f32[6,1024,1024]{1,2,0:T(8,128)} %fusion.207, f32[6,1024]{1,0:T(8,128)S(1)} %get-tuple-element.558, f32[6,1024]{1,0:T(8,128)S(1)} %get-tuple-element.559, f32[6,1024]{1,0:T(8,128)S(1)} %dynamic-slice_bitcast_fusion.19, ...), kind=kOutput, calls=%fused_computation.23.clone.1.clone | convolution fusion | flops 868214784 | bytes 54158336 | tf_op jit(solution)/shard_map/while/body/eval_jaxpr/hid,hjd->hij/dot_general | solution.py:68
  1245.7 22.5 %multiply_reduce_fusion.5 = (f32[6,1024]{1,0:T(8,128)S(1)}, f32[6,1024,1024]{1,2,0:T(8,128)}) fusion(f32[6,1024,1024]{1,2,0:T(8,128)} %fusion.207, f32[6,1024]{1,0:T(8,128)S(1)} %get-tuple-element.558, f32[6,1024]{1,0:T(8,128)S(1)} %get-tuple-element.559, f32[6,1024]{1,0:T(8,128)S(1)} %dynamic-slice_bitcast_fusion.19, ...), kind=kOutput, calls=%fused_computation.23.clone.1.clone | convolution fusion | flops 868214784 | bytes 54158336 | tf_op jit(solution)/shard_map/while/body/eval_jaxpr/hid,hjd->hij/dot_general | solution.py:68
  1426.7 30.3 %reduce-scatter.46.cloned.1.call-done = bf16[2,16,1024]{2,1,0:T(8,128)(2,1)} async-done(((bf16[2,128,1024]{2,1,0:T(8,128)(2,1)}), bf16[2,16,1024]{2,1,0:T(8,128)(2,1)}) %reduce-scatter.46.cloned.1.call-update) | async-done | bytes 65552 | tf_op jit(solution)/shard_map/reduce_scatter | solution.py:438
  1458.5 69.5 %reduce-scatter.24.cloned.1.call-done = bf16[512,1536]{1,0:T(8,128)(2,1)} async-done(((bf16[2048,1536]{1,0:T(8,128)(2,1)}), bf16[512,1536]{1,0:T(8,128)(2,1)}) %reduce-scatter.24.cloned.1.call-update) | async-done | bytes 1572880 | tf_op jit(solution)/shard_map/reduce_scatter | solution.py:283
  1531.3 30.1 %reduce-scatter.40.cloned.1.call-done = bf16[384,16]{0,1:T(8,128)(2,1)} async-done(((bf16[384,128]{0,1:T(8,128)(2,1)}), bf16[384,16]{0,1:T(8,128)(2,1)}) %reduce-scatter.40.cloned.1.call-update) | async-done | bytes 12304 | tf_op jit(solution)/shard_map/reduce_scatter | solution.py:435
  1562.7 29.6 %reduce-scatter.52.cloned.1.call-done = bf16[16,6]{1,0:T(8,128)(2,1)} async-done(((bf16[128,6]{1,0:T(8,128)(2,1)}), bf16[16,6]{1,0:T(8,128)(2,1)}) %reduce-scatter.52.cloned.1.call-update) | async-done | bytes 208
  1593.7 30.3 %reduce-scatter.38.cloned.1.call-done = bf16[4,16,384]{2,1,0:T(8,128)(2,1)} async-done(((bf16[4,128,384]{2,1,0:T(8,128)(2,1)}), bf16[4,16,384]{2,1,0:T(8,128)(2,1)}) %reduce-scatter.38.cloned.1.call-update) | async-done | bytes 49168 | tf_op jit(solution)/shard_map/reduce_scatter | solution.py:429
  1625.5 69.5 %reduce-scatter.32.cloned.1.call-done = bf16[512,1536]{1,0:T(8,128)(2,1)} async-done(((bf16[2048,1536]{1,0:T(8,128)(2,1)}), bf16[512,1536]{1,0:T(8,128)(2,1)}) %reduce-scatter.32.cloned.1.call-update) | async-done | bytes 1572880 | tf_op jit(solution)/shard_map/reduce_scatter | solution.py:246
  1702.1 94.8 %reduce-scatter.50.cloned.1.call-done = f32[128,48]{0,1:T(8,128)} async-done(((f32[128,1536]{0,1:T(8,128)}), f32[128,48]{0,1:T(8,128)}) %reduce-scatter.50.cloned.1.call-update) | async-done | bytes 24592 | tf_op jit(solution)/shard_map/reduce_scatter | solution.py:454
  1797.0 102.7 %reduce-scatter.44.cloned.1.call-done = f32[48,256]{1,0:T(8,128)} async-done(((f32[1536,256]{1,0:T(8,128)}), f32[48,256]{1,0:T(8,128)}) %reduce-scatter.44.cloned.1.call-update) | async-done | bytes 49168 | tf_op jit(solution)/shard_map/reduce_scatter | solution.py:453
  1899.7 100.8 %reduce-scatter.42.cloned.1.call-done = f32[128,48]{0,1:T(8,128)} async-done(((f32[128,1536]{0,1:T(8,128)}), f32[128,48]{0,1:T(8,128)}) %reduce-scatter.42.cloned.1.call-update) | async-done | bytes 24592 | tf_op jit(solution)/shard_map/reduce_scatter | solution.py:452
  2000.5 109.8 %reduce-scatter.36.cloned.1.call-done = f32[48,640]{1,0:T(8,128)} async-done(((f32[1536,640]{1,0:T(8,128)}), f32[48,640]{1,0:T(8,128)}) %reduce-scatter.36.cloned.1.call-update) | async-done | bytes 122896 | tf_op jit(solution)/shard_map/reduce_scatter | solution.py:451
  (457 shorter events, 746.7 us)
Async XLA Ops:
  7.9 132.3 %all-gather.30.cloned.1.call-start = ((), (), s32[]{:S(2)}) async-start(), calls=%async_computation.18 | async-start | bytes 3276800 | tf_op jit(solution)/shard_map/all_gather | solution.py:121
  74.5 163.1 %all-gather.40.cloned.1.call-start = ((), (), s32[]{:S(2)}) async-start(), calls=%async_computation.39 | async-start | bytes 5308416 | tf_op jit(solution)/shard_map/all_gather | solution.py:380
  75.5 300.9 %all-gather.44.cloned.1.call-start = ((), (), s32[]{:S(2)}) async-start(), calls=%async_computation.41 | async-start | bytes 1327104 | tf_op jit(solution)/shard_map/all_gather | solution.py:382
  76.1 456.2 %reduce-scatter.22.cloned.1.call-start = ((), (), s32[]{:S(2)}) async-start(), calls=%async_computation.20 | async-start | bytes 1310720 | tf_op jit(solution)/shard_map/reduce_scatter | solution.py:151
  376.3 170.1 %reduce-scatter.20.cloned.1.call-start = ((), (), s32[]{:S(2)}) async-start(), calls=%async_computation.19 | async-start | bytes 15728640 | tf_op jit(solution)/shard_map/reduce_scatter | solution.py:150
  384.2 294.4 %all-gather.48.cloned.1.call-start = ((), (), s32[]{:S(2)}) async-start(), calls=%async_computation.43 | async-start | bytes 3538944 | tf_op jit(solution)/shard_map/all_gather | solution.py:387
  384.9 293.7 %all-gather.36.cloned.1.call-start = ((), (), s32[]{:S(2)}) async-start(), calls=%async_computation.25 | async-start | bytes 7864320 | tf_op jit(solution)/shard_map/all_gather | solution.py:308
  385.7 306.3 %all-gather.34.cloned.1.call-start = ((), (), s32[]{:S(2)}) async-start(), calls=%async_computation.22 | async-start | bytes 1310720 | tf_op jit(solution)/shard_map/all_gather | solution.py:270
  555.9 202.4 %all-gather.46.cloned.1.call-start = ((), (), s32[]{:S(2)}) async-start(), calls=%async_computation.42 | async-start | bytes 7077888 | tf_op jit(solution)/shard_map/all_gather | solution.py:386
  558.3 270.4 %all-gather.32.cloned.1.call-start = ((), (), s32[]{:S(2)}) async-start(), calls=%async_computation.21 | async-start | bytes 7864320 | tf_op jit(solution)/shard_map/all_gather | solution.py:269
  558.8 363.7 %reduce-scatter.30.cloned.1.call-start = ((), (), s32[]{:S(2)}) async-start(), calls=%async_computation.27 | async-start | bytes 2621440 | tf_op jit(solution)/shard_map/reduce_scatter | solution.py:328
  887.2 158.9 %reduce-scatter.28.cloned.1.call-start = ((), (), s32[]{:S(2)}) async-start(), calls=%async_computation.26 | async-start | bytes 15728640 | tf_op jit(solution)/shard_map/reduce_scatter | solution.py:327
  907.0 220.0 %all-gather.38.cloned.1.call-start = ((), (), s32[]{:S(2)}) async-start(), calls=%async_computation.28 | async-start | bytes 7864320 | tf_op jit(solution)/shard_map/all_gather | solution.py:204
  1053.2 348.5 %reduce-scatter.26.cloned.1.call-start = ((), (), s32[]{:S(2)}) async-start(), calls=%async_computation.24 | async-start | bytes 655360 | tf_op jit(solution)/shard_map/reduce_scatter | solution.py:286
  1059.5 351.5 %reduce-scatter.34.cloned.1.call-start = ((), (), s32[]{:S(2)}) async-start(), calls=%async_computation.30 | async-start | bytes 3276800 | tf_op jit(solution)/shard_map/reduce_scatter | solution.py:249
  1362.1 165.9 %reduce-scatter.24.cloned.1.call-start = ((), (), s32[]{:S(2)}) async-start(), calls=%async_computation.23 | async-start | bytes 7864320 | tf_op jit(solution)/shard_map/reduce_scatter | solution.py:283
  1373.9 187.5 %reduce-scatter.40.cloned.1.call-start = ((), (), s32[]{:S(2)}) async-start(), calls=%async_computation.33 | async-start | bytes 110592 | tf_op jit(solution)/shard_map/reduce_scatter | solution.py:435
  1377.5 214.8 %reduce-scatter.52.cloned.1.call-start = ((), (), s32[]{:S(2)}) async-start(), calls=%async_computation.44 | async-start | bytes 36864
  1378.6 245.4 %reduce-scatter.38.cloned.1.call-start = ((), (), s32[]{:S(2)}) async-start(), calls=%async_computation.32 | async-start | bytes 442368 | tf_op jit(solution)/shard_map/reduce_scatter | solution.py:429
  1383.0 312.0 %reduce-scatter.32.cloned.1.call-start = ((), (), s32[]{:S(2)}) async-start(), calls=%async_computation.29 | async-start | bytes 7864320 | tf_op jit(solution)/shard_map/reduce_scatter | solution.py:246
  1401.6 395.3 %reduce-scatter.50.cloned.1.call-start = ((), (), s32[]{:S(2)}) async-start(), calls=%async_computation.38 | async-start | bytes 811008 | tf_op jit(solution)/shard_map/reduce_scatter | solution.py:454
  1405.7 493.9 %reduce-scatter.44.cloned.1.call-start = ((), (), s32[]{:S(2)}) async-start(), calls=%async_computation.35 | async-start | bytes 1622016 | tf_op jit(solution)/shard_map/reduce_scatter | solution.py:453
  1408.8 591.7 %reduce-scatter.42.cloned.1.call-start = ((), (), s32[]{:S(2)}) async-start(), calls=%async_computation.34 | async-start | bytes 811008 | tf_op jit(solution)/shard_map/reduce_scatter | solution.py:452
  1411.0 699.3 %reduce-scatter.36.cloned.1.call-start = ((), (), s32[]{:S(2)}) async-start(), calls=%async_computation.31 | async-start | bytes 4055040 | tf_op jit(solution)/shard_map/reduce_scatter | solution.py:451
  (105 other events, 2854.4 us)
Sparse Core Ops, SparseCore 0:
  10.9 58.7 all-gather.41
  73.9 38.2 all-gather.29
  114.6 70.0 all-gather.27
  186.1 51.3 all-gather.39
  406.6 139.7 reduce-scatter.19
  548.0 38.5 all-gather.47
  588.5 75.5 all-gather.35
  693.6 64.6 all-gather.45
  760.0 68.6 all-gather.31
  887.4 35.1 reduce-scatter.29
  925.5 120.6 reduce-scatter.27
  1053.3 73.5 all-gather.37
  1352.7 39.5 reduce-scatter.33
  1394.4 30.8 reduce-scatter.47
  1427.5 29.4 reduce-scatter.45
  1459.8 68.1 reduce-scatter.23
  1530.8 30.4 reduce-scatter.39
  1563.6 28.6 reduce-scatter.51
  1594.6 29.3 reduce-scatter.37
  1626.8 68.0 reduce-scatter.31
  1700.7 96.2 reduce-scatter.49
  1802.6 96.9 reduce-scatter.43
  1905.2 95.2 reduce-scatter.41
  2006.5 103.7 reduce-scatter.35
  (4 shorter events, 99.6 us)
where the time goes:
time: 2120 us
  waiting for transfers between devices  1110 us (52%)
  matrix products  398 us (19%)
  blocking collectives  380 us (18%)
  local copies, waits for them, and re-layouts  112 us (5%)
  other arithmetic  103 us (5%)
    reduce_scatter x1, waiting for transfers between devices, mlp_backward(): lax.psum_scatter(grad_normed, 'tp', scatter_dimension=0, tiled=True)  124 us
    reduce_scatter x1, waiting for transfers between devices, on_device(): lax.psum_scatter(part_in_a, ('fsdp', 'tp'), scatter_dimension=0, tiled=True)  110 us
    reduce_scatter x1, waiting for transfers between devices, on_device(): lax.psum_scatter(part_mlp_a, ('fsdp', 'tp'), scatter_dimension=0, tiled=T...  103 us
    reduce_scatter x1, waiting for transfers between devices, on_device(): lax.psum_scatter(part_out_b, ('fsdp', 'tp'), scatter_dimension=1, tiled=T...  101 us
    reduce_scatter x1, waiting for transfers between devices, on_device(): lax.psum_scatter(part_down_b, ('fsdp', 'tp'), scatter_dimension=1, tiled=...  94.8 us
    all_gather x1, blocking collectives, shared_pieces(): lax.all_gather(adapt_mlp_a[layer_index], ('fsdp', 'tp'), axis=0, tiled=True)  76.2 us
    all_gather x1, blocking collectives, shared_pieces(): lax.all_gather(adapt_down_b[layer_index], ('fsdp', 'tp'), axis=1, tiled=T...  71.1 us
    dot_general x4, matrix products, scores_of(): jnp.einsum('hid,hjd->hij', queries, key_rows, preferred_element_type=jnp....  70.6 us
  transfers between devices with their start and end apart: 28, of which 21 were waited for; matrix products, arithmetic and copies ran while one was open for 25% of the time, Pallas kernels for 0%

commit v1 on v0

v1 whole, which is shorter than its diff:
```python
import functools

import jax
import jax.numpy as jnp
from jax import lax
from jax.experimental import pallas as pl
from jax.experimental.pallas import tpu as pltpu
from jax.sharding import Mesh, PartitionSpec as P

HEAD = 64
RANK = 16
PIECE = 256
PIECES = 2
LEN = 1024
epsilon = 1e-06
masked_score = -1e30
LANES = 128
BLOCK = 256
VMEM_LIMIT = 60 * 1024 * 1024

f32 = jnp.float32
bf16 = jnp.bfloat16
ANY = pl.BlockSpec(memory_space=pl.ANY)
WHOLE = pl.BlockSpec(memory_space=pltpu.VMEM)


def mm(left, right, dims):
    return lax.dot_general(left, right, ((dims[0], dims[1]), ((), ())), preferred_element_type=f32)


def shift(value, axis, size, step):
    return lax.ppermute(value, axis, [(i, (i + step) % size) for i in range(size)])


def split3(value):
    high = value.astype(bf16)
    rest = value - high.astype(f32)
    mid = rest.astype(bf16)
    low = (rest - mid.astype(f32)).astype(bf16)
    return high, mid, low


def split_columns(value):
    high = lax.reduce_precision(value, 8, 7)
    mid = lax.reduce_precision(value - high, 8, 7)
    return jnp.concatenate([high, mid, value - high - mid], 1).astype(bf16)


def in_order(pieces, index, size):
    if size == 1:
        return pieces[0]
    if size == 2:
        return jnp.where(
            index == 0, jnp.concatenate(pieces, 0), jnp.concatenate(pieces[::-1], 0)
        )
    rows = pieces[0].shape[0]
    out = jnp.zeros((size * rows,) + pieces[0].shape[1:], pieces[0].dtype)
    for d, piece in enumerate(pieces):
        out = lax.dynamic_update_slice_in_dim(out, piece, ((index - d) % size) * rows, 0)
    return out


def assemble_kernel(count, axis, width, at_ref, *refs):
    pieces, out, buf, sem = refs[:count], refs[count], refs[count + 1], refs[count + 2]
    copies = []
    for d in range(count):
        where = pl.multiple_of(lax.rem(at_ref[0] - d + count, count) * width, width)
        spot = (slice(None),) * axis + (pl.ds(where, width),)
        copies.append(pltpu.make_async_copy(pieces[d], buf.at[spot], sem.at[d]))
    for copy in copies:
        copy.start()
    for copy in copies:
        copy.wait()
    last = pltpu.make_async_copy(buf, out, sem.at[count])
    last.start()
    last.wait()


def assemble(pieces, index, axis):
    count = len(pieces)
    shape = list(pieces[0].shape)
    width = shape[axis]
    shape[axis] = width * count
    size = 2 * functools.reduce(lambda a, b: a * b, shape)
    return pl.pallas_call(
        functools.partial(assemble_kernel, count, axis, width),
        out_shape=jax.ShapeDtypeStruct(tuple(shape), pieces[0].dtype),
        grid_spec=pltpu.PrefetchScalarGridSpec(
            num_scalar_prefetch=1,
            grid=(1,),
            in_specs=[ANY] * count,
            out_specs=ANY,
            scratch_shapes=[
                pltpu.VMEM(tuple(shape), pieces[0].dtype),
                pltpu.SemaphoreType.DMA((count + 1,)),
            ],
        ),
        cost_estimate=pl.CostEstimate(flops=0, bytes_accessed=2 * size, transcendentals=0),
        compiler_params=pltpu.CompilerParams(vmem_limit_bytes=VMEM_LIMIT),
        name="assemble",
    )(jnp.reshape(index, (1,)).astype(jnp.int32), *pieces)


def out_weight_kernel(blocks, cols, at_ref, *refs):
    mine, other = refs[:blocks], refs[blocks : 2 * blocks]
    out, buf, sem = refs[2 * blocks :]
    core = at_ref[0]
    copies = []
    for i in range(blocks):
        for k, source in enumerate((mine[i], other[i])):
            spot = buf.at[:, lax.rem(core + k, 2), :, pl.ds(i * cols, cols)]
            copies.append(pltpu.make_async_copy(source, spot, sem.at[2 * i + k]))
    for copy in copies:
        copy.start()
    for copy in copies:
        copy.wait()
    last = pltpu.make_async_copy(buf, out, sem.at[2 * blocks])
    last.start()
    last.wait()


def out_weight(mine, other, core):
    blocks = len(mine)
    nz, rows, cols = mine[0].shape
    if cols % LANES:
        mine, other = jnp.concatenate(mine, 2), jnp.concatenate(other, 2)
        return jnp.where(core == 0, jnp.stack([mine, other], 1), jnp.stack([other, mine], 1))
    shape = (nz, 2, rows, blocks * cols)
    size = 2 * nz * 2 * rows * blocks * cols
    return pl.pallas_call(
        functools.partial(out_weight_kernel, blocks, cols),
        out_shape=jax.ShapeDtypeStruct(shape, bf16),
        grid_spec=pltpu.PrefetchScalarGridSpec(
            num_scalar_prefetch=1,
            grid=(1,),
            in_specs=[ANY] * (2 * blocks),
            out_specs=ANY,
            scratch_shapes=[
                pltpu.VMEM(shape, bf16),
                pltpu.SemaphoreType.DMA((2 * blocks + 1,)),
            ],
        ),
        cost_estimate=pl.CostEstimate(flops=0, bytes_accessed=2 * size, transcendentals=0),
        compiler_params=pltpu.CompilerParams(vmem_limit_bytes=VMEM_LIMIT),
        name="out_weight",
    )(jnp.reshape(core, (1,)).astype(jnp.int32), *mine, *other)


def mlp_kernel(units, first, width, *refs):
    own, oth = refs[:units], refs[units : 2 * units]
    refs = refs[2 * units :]
    xm_ref, gz_ref, low_ref, bu_ref = refs[:4]
    refs = refs[4:]
    if not first:
        prior, refs = refs[:3], refs[3:]
    out_ref, dx_ref, small_ref, grad_ref, wbuf, sem = refs
    for u in range(units):
        for half, source in enumerate((own[u], oth[u])):
            pltpu.make_async_copy(
                source, wbuf.at[u, :, :, pl.ds(half * width, width)], sem.at[u, half]
            ).start()
    if first:
        out_ref[...] = jnp.zeros_like(out_ref)
        dx_ref[...] = jnp.zeros_like(dx_ref)
        small_ref[...] = jnp.zeros_like(small_ref)
    else:
        out_ref[...] = prior[0][...]
        dx_ref[...] = prior[1][...]
        small_ref[...] = prior[2][...]
    low_all = low_ref[...]
    lane = lax.broadcasted_iota(jnp.int32, low_all.shape, 1) // RANK
    zero = jnp.zeros_like(low_all)
    low_e, low_u, low_d = (jnp.where(lane == i, low_all, zero) for i in range(3))

    def step(u, carry):
        for half in range(2):
            spot = wbuf.at[u, :, :, pl.ds(half * width, width)]
            pltpu.make_async_copy(spot, spot, sem.at[u, half]).wait()
        bu = bu_ref[u]
        gate = mm(xm_ref[...], wbuf[u, 0], ((1,), (0,))) + mm(low_e, bu, ((1,), (0,)))
        up = mm(xm_ref[...], wbuf[u, 1], ((1,), (0,))) + mm(low_u, bu, ((1,), (0,)))
        dh = mm(gz_ref[...], wbuf[u, 2], ((1,), (0,))) + mm(low_d, bu, ((1,), (0,)))
        sig = jax.nn.sigmoid(gate)
        act = gate * sig
        inner = (act * up).astype(bf16)
        dgate = (dh * up * sig * (1.0 + gate * (1.0 - sig))).astype(bf16)
        dup = (dh * act).astype(bf16)
        out_ref[...] += mm(inner, wbuf[u, 2], ((1,), (1,)))
        dx_ref[...] += mm(dgate, wbuf[u, 0], ((1,), (1,))) + mm(dup, wbuf[u, 1], ((1,), (1,)))
        s_e = mm(dgate, bu, ((1,), (1,)))
        s_u = mm(dup, bu, ((1,), (1,)))
        s_d = mm(inner, bu, ((1,), (1,)))
        small_ref[...] += jnp.where(lane == 0, s_e, jnp.where(lane == 1, s_u, s_d))
        grad_ref[u] = (
            mm(low_e, dgate, ((0,), (0,)))
            + mm(low_u, dup, ((0,), (0,)))
            + mm(low_d, inner, ((0,), (0,)))
        ).astype(bf16)
        return carry

    lax.fori_loop(0, units, step, 0)


def mlp_call(own, oth, xm, gz, low, bu, prior):
    units = len(own)
    three, depth, width = own[0].shape
    rows = xm.shape[0]
    first = prior is None
    lanes = low.shape[1]
    flops = units * 2 * rows * depth * 2 * width * 6
    return pl.pallas_call(
        functools.partial(mlp_kernel, units, first, width),
        out_shape=(
            jax.ShapeDtypeStruct((rows, depth), f32),
            jax.ShapeDtypeStruct((rows, depth), f32),
            jax.ShapeDtypeStruct((rows, lanes), f32),
            jax.ShapeDtypeStruct((units, lanes, 2 * width), bf16),
        ),
        in_specs=[ANY] * (2 * units) + [WHOLE] * (4 + (0 if first else 3)),
        out_specs=(WHOLE,) * 4,
        scratch_shapes=[
            pltpu.VMEM((units, three, depth, 2 * width), bf16),
            pltpu.SemaphoreType.DMA((units, 2)),
        ],
        cost_estimate=pl.CostEstimate(
            flops=flops,
            bytes_accessed=units * 3 * depth * 2 * width * 2 + rows * depth * 20,
            transcendentals=units * rows * 2 * width,
        ),
        compiler_params=pltpu.CompilerParams(vmem_limit_bytes=VMEM_LIMIT),
        name="feed_forward",
    )(*own, *oth, xm, gz, low, bu, *(() if first else prior))


def decay_lanes(cum, negate):
    high, mid, low = (part.astype(f32) for part in split3(cum))
    lane = lax.broadcasted_iota(jnp.int32, cum.shape, 1) % HEAD
    one = jnp.ones_like(cum)
    if negate:
        picks = (-high, -mid, -low, one, one, one)
    else:
        picks = (one, one, one, high, mid, low)
    out = jnp.zeros_like(cum)
    for i, pick in enumerate(picks):
        out = jnp.where(lane == i, pick, out)
    return out.astype(bf16)


def pair_masks(row, col, starts):
    def label(position, none):
        out = jnp.full(position.shape, none, jnp.int32)
        for i in range(PIECES):
            inside = (position >= starts[i]) & (position < starts[i] + PIECE)
            out = jnp.where(inside, i + 1, out)
        return out

    lower = col <= row
    return lower, lower | (label(row, -1) == label(col, -2))


def hi_fix(scores, decay, lower, allowed):
    return jnp.where(lower, scores, jnp.where(allowed, scores - 2.0 * decay, masked_score))


def block_ranges(i, rows, length):
    low = i * rows
    return low, min(low + rows + PIECE, length)


def attend_kernel(length, starts_ref, q_ref, k_ref, v_ref, gate_ref, cum_ref, y_ref, o_ref, lse_ref, keys):
    starts = [starts_ref[i] for i in range(PIECES)]
    cum = cum_ref[...]
    keys[:, :LANES] = k_ref[0]
    keys[:, LANES:] = decay_lanes(cum, True)
    values = v_ref[0].astype(bf16)
    for i in range(length // BLOCK):
        low, top = block_ranges(i, BLOCK, length)
        rows = slice(low, low + BLOCK)
        lane = lax.broadcasted_iota(jnp.int32, (BLOCK, LANES), 1)
        queries = q_ref[0, rows, :] * jnp.asarray(HEAD**-0.5, bf16)
        aug = decay_lanes(cum_ref[rows, :], False)
        row = low + lax.broadcasted_iota(jnp.int32, (BLOCK, 1), 0)
        col = low + lax.broadcasted_iota(jnp.int32, (1, top - low), 1)
        lower, allowed = pair_masks(row, col, starts)
        mixed, lse = [], []
        for h in range(2):
            mine = (lane // HEAD) == h
            zero = jnp.zeros_like(queries)
            aug_h = jnp.where(mine, aug, zero)
            left = jnp.concatenate([jnp.where(mine, queries, zero), aug_h], 1)
            s_hi = mm(left, keys[low:top, :], ((1,), (1,)))
            decay = mm(aug_h, keys[low:top, LANES:], ((1,), (1,)))
            s_hi = hi_fix(s_hi, decay, lower, allowed)
            top_score = jnp.max(s_hi, axis=1, keepdims=True)
            if low:
                s_lo = mm(left, keys[:low, :], ((1,), (1,)))
                top_score = jnp.maximum(top_score, jnp.max(s_lo, axis=1, keepdims=True))
                p_lo = jnp.exp(s_lo - top_score)
            p_hi = jnp.exp(s_hi - top_score)
            total = jnp.sum(p_hi, axis=1, keepdims=True)
            out = mm(p_hi.astype(bf16), values[low:top, :], ((1,), (0,)))
            if low:
                total = total + jnp.sum(p_lo, axis=1, keepdims=True)
                out = out + mm(p_lo.astype(bf16), values[:low, :], ((1,), (0,)))
            mixed.append(out / total)
            lse.append(top_score + jnp.log(total))
        out = jnp.where(lane < HEAD, mixed[0], mixed[1])
        o_ref[rows, :] = out
        lse_ref[rows, :] = jnp.where(lane < HEAD, lse[0], lse[1])
        y_ref[rows, :] = (out * jax.nn.sigmoid(gate_ref[0, rows, :])).astype(bf16)


def prefetch_call(kernel, grid, in_specs, out_specs, out_shape, scratch, cost, name, scalars):
    return pl.pallas_call(
        kernel,
        out_shape=out_shape,
        grid_spec=pltpu.PrefetchScalarGridSpec(
            num_scalar_prefetch=1,
            grid=grid,
            in_specs=in_specs,
            out_specs=out_specs,
            scratch_shapes=scratch,
        ),
        cost_estimate=cost,
        compiler_params=pltpu.CompilerParams(vmem_limit_bytes=VMEM_LIMIT),
        name=name,
    )


def attend(scalars, qk, vg, cum):
    _, length, width = qk.shape
    pairs = width // LANES
    block = (1, length, LANES)
    flat = pl.BlockSpec((length, LANES), lambda p, s: (0, p))
    first = lambda p, s: (s[PIECES], 0, p)
    second = lambda p, s: (1 - s[PIECES], 0, p)
    area = length * length * pairs * 2
    return prefetch_call(
        functools.partial(attend_kernel, length),
        (pairs,),
        [
            pl.BlockSpec(block, first),
            pl.BlockSpec(block, second),
            pl.BlockSpec(block, first),
            pl.BlockSpec(block, second),
            flat,
        ],
        [flat, flat, flat],
        (
            jax.ShapeDtypeStruct((length, width), bf16),
            jax.ShapeDtypeStruct((length, width), f32),
            jax.ShapeDtypeStruct((length, width), f32),
        ),
        [pltpu.VMEM((length, 2 * LANES), bf16)],
        pl.CostEstimate(
            flops=area * 600, bytes_accessed=length * width * 26, transcendentals=area
        ),
        "attend",
        scalars,
    )(scalars, qk, qk, vg, vg, cum)


def attend_back_kernel(
    length, starts_ref, q_ref, k_ref, v_ref, gate_ref, cum_ref, o_ref, lse_ref, dy_ref,
    dq_ref, dk_ref, dv_ref, dgate_ref, dcum_ref, keys, summed, vals, dkeys, dvals, dcol,
):
    starts = [starts_ref[i] for i in range(PIECES)]
    lane_all = lax.broadcasted_iota(jnp.int32, (length, LANES), 1)
    spot_all = lane_all % HEAD
    keys[:, :LANES] = k_ref[0]
    keys[:, LANES:] = jnp.where(
        (spot_all >= 6) & (spot_all < 9), jnp.asarray(1.0, bf16), decay_lanes(cum_ref[...], True)
    )
    for h in range(2):
        summed[h] = jnp.where(lane_all // HEAD == h, k_ref[0], jnp.asarray(1.0, bf16))
    vals[...] = v_ref[0].astype(bf16)
    dkeys[...] = jnp.zeros_like(dkeys)
    dvals[...] = jnp.zeros_like(dvals)
    for i in range(length // BLOCK):
        low, top = block_ranges(i, BLOCK, length)
        rows = slice(low, low + BLOCK)
        lane = lax.broadcasted_iota(jnp.int32, (BLOCK, LANES), 1)
        queries = q_ref[0, rows, :] * jnp.asarray(HEAD**-0.5, bf16)
        aug = decay_lanes(cum_ref[rows, :], False)
        gate = jax.nn.sigmoid(gate_ref[0, rows, :])
        mixed = o_ref[rows, :]
        dy = dy_ref[rows, :].astype(f32)
        dmix = (dy * gate).astype(bf16)
        dgate_ref[rows, :] = (dy * mixed * gate * (1.0 - gate)).astype(bf16)
        lse_parts = split3(-lse_ref[rows, :])
        row = low + lax.broadcasted_iota(jnp.int32, (BLOCK, 1), 0)
        col = low + lax.broadcasted_iota(jnp.int32, (1, top - low), 1)
        lower, allowed = pair_masks(row, col, starts)
        grads, sums = [], []
        for h in range(2):
            mine = (lane // HEAD) == h
            zero = jnp.zeros_like(queries)
            spot = lane % HEAD
            aug_h = jnp.where(mine, aug, zero)
            shifted = aug_h
            for j in range(3):
                shifted = jnp.where(mine & (spot == 6 + j), lse_parts[j], shifted)
            left = jnp.concatenate([jnp.where(mine, queries, zero), shifted], 1)
            dmix_h = jnp.where(mine, dmix, zero)
            plain = jnp.concatenate([left[:, :LANES], aug_h], 1)
            grad_q, delta, kept = None, None, []
            for start, stop in ((0, low), (low, top)):
                if start == stop:
                    continue
                scores = mm(left, keys[start:stop, :], ((1,), (1,)))
                if start == low:
                    decay = mm(aug_h, keys[start:stop, LANES:], ((1,), (1,)))
                    scores = hi_fix(scores, decay, lower, allowed)
                probs = jnp.exp(scores)
                dprobs = mm(dmix_h, vals[start:stop, :], ((1,), (1,)))
                part = jnp.sum(probs * dprobs, axis=1, keepdims=True)
                delta = part if delta is None else delta + part
                kept.append((start, stop, probs, dprobs))
            for start, stop, probs, dprobs in kept:
                dscores = (probs * (dprobs - delta)).astype(bf16)
                part = mm(dscores, summed[h, start:stop, :], ((1,), (0,)))
                grad_q = part if grad_q is None else grad_q + part
                dkeys[start:stop, :] += mm(dscores, plain, ((0,), (0,)))
                dvals[start:stop, :] += mm(probs.astype(bf16), dmix_h, ((0,), (0,)))
                if start == low:
                    late = jnp.where(lower, jnp.zeros_like(dscores), dscores)
                    ones = jnp.where(mine, jnp.ones_like(zero), zero)
                    dkeys[start:stop, LANES:] += mm(late, ones * jnp.asarray(-2.0, bf16), ((0,), (0,)))
                    fix = -2.0 * jnp.sum(late.astype(f32), axis=1, keepdims=True)
            grads.append(grad_q)
            sums.append(fix + grad_q[:, (1 - h) * HEAD : (1 - h) * HEAD + 1])
        dq_ref[rows, :] = (jnp.where(lane < HEAD, grads[0], grads[1]) * HEAD**-0.5).astype(bf16)
        dcol[rows, :] = jnp.where(lane < HEAD, sums[0], sums[1])
    dk_ref[...] = dkeys[:, :LANES].astype(bf16)
    dv_ref[...] = dvals[...].astype(bf16)
    cols = dkeys[:, LANES:]
    dcum_ref[...] = dcol[...] - jnp.where(lane_all < HEAD, cols[:, 0:1], cols[:, HEAD : HEAD + 1])


def attend_back(scalars, qk, vg, cum, mixed, lse, dy):
    _, length, width = qk.shape
    pairs = width // LANES
    block = (1, length, LANES)
    flat = pl.BlockSpec((length, LANES), lambda p, s: (0, p))
    first = lambda p, s: (s[PIECES], 0, p)
    second = lambda p, s: (1 - s[PIECES], 0, p)
    area = length * length * pairs * 2
    out = jax.ShapeDtypeStruct((length, width), bf16)
    return prefetch_call(
        functools.partial(attend_back_kernel, length),
        (pairs,),
        [
            pl.BlockSpec(block, first),
            pl.BlockSpec(block, second),
            pl.BlockSpec(block, first),
            pl.BlockSpec(block, second),
            flat,
            flat,
            flat,
            flat,
        ],
        [flat] * 5,
        (out, out, out, out, jax.ShapeDtypeStruct((length, width), f32)),
        [
            pltpu.VMEM((length, 2 * LANES), bf16),
            pltpu.VMEM((2, length, LANES), bf16),
            pltpu.VMEM((length, LANES), bf16),
            pltpu.VMEM((length, 2 * LANES), f32),
            pltpu.VMEM((length, LANES), f32),
            pltpu.VMEM((length, LANES), f32),
        ],
        pl.CostEstimate(
            flops=area * 1500, bytes_accessed=length * width * 34, transcendentals=area
        ),
        "attend_back",
        scalars,
    )(scalars, qk, qk, vg, vg, cum, mixed, lse, dy)


def norm_scale(hidden):
    return lax.rsqrt(jnp.mean(hidden * hidden, axis=-1, keepdims=True) + epsilon)


def norm_back(hidden, inv_rms, gain, grad):
    weighted = grad * gain
    return inv_rms * weighted - hidden * inv_rms**3 * jnp.mean(
        weighted * hidden, axis=-1, keepdims=True
    )


def on_device(
    sizes, tokens_in, cotangent, piece_starts, adapter_ids, gain_att, w_in, w_forget, bias_forget,
    w_out, gain_mlp, w_gate_up, w_down, adapt_in_a, adapt_in_b, adapt_forget_b, adapt_out_a,
    adapt_out_b, adapt_mlp_a, adapt_gu_b, adapt_down_a, adapt_down_b,
):
    nz, ny, nx = sizes
    z, c, y, x = (lax.axis_index(name) for name in "zcyx")
    everyone, fsdp = ("z", "c", "y", "x"), ("z", "c")
    n_fsdp, n_tp = 2 * nz, ny * nx
    count = n_fsdp * n_tp
    rows, depth = tokens_in.shape
    length = rows * nx
    ranks = adapt_out_b.shape[1]
    adapters = ranks // RANK
    d_part = depth // count
    d_fsdp = depth // n_fsdp
    cols_t = w_out.shape[1]
    ff_t = w_down.shape[1]
    heads_t = w_forget.shape[2]
    rank_part = ranks // n_fsdp

    small = jnp.concatenate(
        [
            gain_att[0],
            gain_mlp[0],
            w_forget[0].reshape(-1),
            adapt_forget_b[0].reshape(-1),
            bias_forget[0],
            adapter_ids.astype(bf16),
        ]
    )
    small = lax.all_to_all(
        jnp.broadcast_to(small[None], (count, small.shape[0])), everyone, 0, 0, tiled=True
    )
    cuts = [d_part, d_part, d_fsdp * heads_t, rank_part * heads_t, heads_t, ny]
    at, parts = 0, []
    for cut in cuts:
        parts.append(small[:, at : at + cut])
        at += cut
    gain_a = parts[0].reshape(1, depth).astype(f32)
    gain_m = parts[1].reshape(1, depth).astype(f32)

    def heads_full(part, lead):
        return (
            part.reshape(n_fsdp, n_tp, lead, heads_t).transpose(0, 2, 1, 3).reshape(-1, n_tp * heads_t)
        )

    forget_w = heads_full(parts[2], d_fsdp)
    forget_b = heads_full(parts[3], rank_part)
    forget_bias = parts[4].reshape(n_fsdp, n_tp * heads_t)[:1]
    ids_all = parts[5].reshape(n_fsdp, n_tp, ny)[:, 0].astype(jnp.int32)
    my_id = lax.dynamic_index_in_dim(adapter_ids, y, 0, keepdims=False)
    seq_of = jnp.broadcast_to(ids_all[:, :, None], (n_fsdp, ny, nx)).reshape(count)
    seq_hot = (seq_of[:, None] == jnp.arange(adapters)[None, :]).astype(bf16)

    def z_gather(value, axis):
        return assemble([shift(value, "z", nz, d) if d else value for d in range(nz)], z, axis)

    def core_split(half0, half1):
        keep, send = jnp.where(c == 0, half0, half1), jnp.where(c == 0, half1, half0)
        got = shift(send, "c", 2, 1)
        axis = keep.ndim - 2
        return jnp.where(
            c == 0, jnp.concatenate([keep, got], axis), jnp.concatenate([got, keep], axis)
        )

    def other_core(value):
        return shift(value, "c", 2, 1)

    w4 = w_in[0]
    half0 = jnp.stack([w4[:, 0], w4[:, 2]])
    half1 = jnp.stack([w4[:, 1], w4[:, 3]])
    w4 = core_split(half0, half1)
    chunks = []
    for j in range(2):
        mine = z_gather(w4[j], 0)
        mine = [shift(mine, "y", ny, d) if d else mine for d in range(ny)]
        chunks.append((mine, [other_core(piece) for piece in mine]))

    wo = jnp.swapaxes(w_out[0], 0, 1)
    wo = z_gather(wo[None], 0)
    wo_mine = {}
    for dx in range(nx):
        moved = shift(wo, "x", nx, dx) if dx else wo
        for dy in range(ny):
            wo_mine[dx, dy] = shift(moved, "y", ny, dy) if dy else moved
    wo_keys = [(dx, dy) for dx in range(nx) for dy in range(ny)]
    wo_mine = [wo_mine[key] for key in wo_keys]
    wo_all = out_weight(wo_mine, [other_core(piece) for piece in wo_mine], c)
    wo_all = wo_all.reshape(depth, n_tp * cols_t)

    w3 = jnp.stack([w_gate_up[0][:, 0], w_gate_up[0][:, 1], jnp.swapaxes(w_down[0], 0, 1)])
    w3 = core_split(w3[..., : ff_t // 2], w3[..., ff_t // 2 :])
    n_chunk = max(1, ff_t // 2 // LANES)
    width = ff_t // 2 // n_chunk
    ff_units = []
    for k in range(n_chunk):
        mine = z_gather(w3[..., k * width : (k + 1) * width], 1)
        placed = {}
        if k % 2 == 0:
            for dx in range(nx):
                moved = shift(mine, "x", nx, dx) if dx else mine
                for dy in range(ny):
                    placed[dy, dx] = shift(moved, "y", ny, dy) if dy else moved
        else:
            for dy in range(ny):
                moved = shift(mine, "y", ny, dy) if dy else mine
                for dx in range(nx):
                    placed[dy, dx] = shift(moved, "x", nx, dx) if dx else moved
        order = [placed[dy, dx] for dy in range(ny) for dx in range(nx)]
        ff_units.append((order, [other_core(piece) for piece in order]))

    sub_c, sub_f = cols_t // n_fsdp, ff_t // n_fsdp
    spread = jnp.concatenate(
        [
            adapt_in_b[0].reshape(4, rank_part, n_fsdp, sub_c).transpose(2, 1, 0, 3).reshape(
                n_fsdp, rank_part, 4 * sub_c
            ),
            adapt_out_a[0].reshape(n_fsdp, sub_c, rank_part).transpose(0, 2, 1),
            adapt_gu_b[0].reshape(2, rank_part, n_fsdp, sub_f).transpose(2, 1, 0, 3).reshape(
                n_fsdp, rank_part, 2 * sub_f
            ),
            adapt_down_a[0].reshape(n_fsdp, sub_f, rank_part).transpose(0, 2, 1),
        ],
        axis=2,
    )
    n_cols = spread.shape[2]
    spread = lax.all_to_all(spread, fsdp, 0, 0, tiled=True)
    table_b = spread.reshape(adapters, RANK * n_cols)
    table_a = jnp.concatenate(
        [
            adapt_in_a[0].reshape(d_part, 5, adapters, RANK).transpose(2, 0, 1, 3).reshape(
                adapters, d_part, 5 * RANK
            ),
            adapt_mlp_a[0].reshape(d_part, 2, adapters, RANK).transpose(2, 0, 1, 3).reshape(
                adapters, d_part, 2 * RANK
            ),
            adapt_out_b[0].reshape(adapters, RANK, d_part).transpose(0, 2, 1),
            adapt_down_b[0].reshape(adapters, RANK, d_part).transpose(0, 2, 1),
        ],
        axis=2,
    )
    n_a = d_part * 9 * RANK
    table = jnp.concatenate([table_a.reshape(adapters, n_a), table_b], axis=1)
    chosen = mm(seq_hot, table, ((1,), (0,))).astype(bf16)
    chosen = lax.all_to_all(chosen, everyone, 0, 0, tiled=True)
    map_a = chosen[:, :n_a].reshape(depth, 9 * RANK)
    in_a, mlp_a = map_a[:, : 5 * RANK], map_a[:, 5 * RANK : 7 * RANK]
    out_b, down_b = map_a[:, 7 * RANK : 8 * RANK], map_a[:, 8 * RANK :]

    share = n_fsdp // 2
    r = jnp.arange(count)
    r_c, r_s = r // (share * n_tp), (r // n_tp) % share
    r_y, r_x = (r // nx) % ny, r % nx
    r_true = (((c - r_c) % 2) * share + r_s) * n_tp + ((y - r_y) % ny) * nx + (x - r_x) % nx
    reorder = (r_true[:, None] == r[None, :]).astype(bf16)
    map_b = mm(reorder, chosen[:, n_a:], ((1,), (0,))).astype(bf16)
    map_b = map_b.reshape(2, share, ny, nx, RANK, n_cols)
    cut_b = [4 * sub_c, sub_c, 2 * sub_f, sub_f]
    at, pieces_b = 0, []
    for cut in cut_b:
        pieces_b.append(map_b[..., at : at + cut])
        at += cut
    in_b = pieces_b[0][:, :, :, 0].reshape(2, share, ny, RANK, 4, sub_c)
    half_order_y = in_b.transpose(4, 3, 2, 0, 1, 5)
    in_b = jnp.where(c == 0, half_order_y, jnp.flip(half_order_y, 3)).reshape(4, RANK, ny * cols_t)
    out_a = pieces_b[1].transpose(4, 3, 2, 0, 1, 5)
    out_a = jnp.where(c == 0, out_a, jnp.flip(out_a, 3)).reshape(RANK, n_tp * cols_t)
    per = share // n_chunk
    gu_b = (
        pieces_b[2]
        .reshape(2, n_chunk, per, ny, nx, RANK, 2, sub_f)
        .transpose(1, 3, 4, 6, 5, 0, 2, 7)
        .reshape(n_chunk, n_tp, 2 * RANK, 2 * width)
    )
    down_a = (
        pieces_b[3]
        .reshape(2, n_chunk, per, ny, nx, RANK, sub_f)
        .transpose(1, 3, 4, 5, 0, 2, 6)
        .reshape(n_chunk, n_tp, RANK, 2 * width)
    )
    unit_b = jnp.concatenate([gu_b, down_a, jnp.zeros_like(down_a)], axis=2)

    hidden = tokens_in.astype(f32)
    inv_att = norm_scale(hidden)
    normed = (hidden * inv_att * gain_a).astype(bf16)
    normed_all = in_order([shift(normed, "x", nx, d) if d else normed for d in range(nx)], x, nx)
    low_in = mm(normed_all, in_a, ((1,), (0,))).astype(bf16)
    la = [low_in[:, j * RANK : (j + 1) * RANK] for j in range(5)]
    local_heads = ny * heads_t
    lh = jnp.arange(local_heads)
    true_head = (((y - lh // heads_t) % ny) * nx + x) * heads_t + lh % heads_t
    head_pick = (jnp.arange(n_tp * heads_t)[:, None] == true_head[None, :]).astype(bf16)
    wf = mm(forget_w, head_pick, ((1,), (0,))).astype(bf16)
    bf = mm(forget_b, head_pick, ((1,), (0,))).astype(bf16)
    bf = lax.dynamic_slice_in_dim(bf, my_id * RANK, RANK, 0)
    bias = mm(forget_bias, head_pick, ((1,), (0,)))
    logits = mm(normed_all, wf, ((1,), (0,))) + mm(la[4], bf, ((1,), (0,))) + bias
    log_gate = -jnp.log1p(jnp.exp(-logits))
    order = jnp.arange(length)
    earlier = (order[None, :] <= order[:, None]).astype(bf16)
    cum = mm(earlier, split_columns(log_gate), ((1,), (0,)))
    cum = cum[:, :local_heads] + cum[:, local_heads : 2 * local_heads] + cum[:, 2 * local_heads :]
    cum = jnp.repeat(cum, HEAD, axis=1)

    def core_pick(first, second):
        return jnp.where(c == 0, first, second), jnp.where(c == 0, second, first)

    def project(j, out_type):
        mine, other = chunks[j]
        la_pair = core_pick(la[2 * j], la[2 * j + 1])
        in_b_pair = core_pick(in_b[2 * j], in_b[2 * j + 1])
        out = []
        for pieces, low, up in zip((mine, other), la_pair, in_b_pair):
            weight = jnp.concatenate(pieces, 1)
            out.append(
                (mm(normed_all, weight, ((1,), (0,))) + mm(low, up, ((1,), (0,)))).astype(out_type)
            )
        return jnp.stack(out)

    qk = project(0, bf16)
    vg = project(1, f32)
    my_starts = lax.dynamic_index_in_dim(piece_starts, y, 0, keepdims=False)
    scalars = jnp.concatenate([my_starts, c[None].astype(jnp.int32)])
    merged, mixed, lse = attend(scalars, qk, vg, cum)

    def row_block(value, index):
        return lax.dynamic_slice_in_dim(value, index * rows, rows, 0)

    merged_full = jnp.concatenate(
        [
            shift(row_block(merged, (x + d) % nx), "x", nx, d) if d else row_block(merged, x)
            for d in range(nx)
        ],
        axis=1,
    )
    low_out = mm(merged_full, out_a, ((1,), (1,))).astype(bf16)
    hidden1 = (
        hidden + mm(merged_full, wo_all, ((1,), (1,))) + mm(low_out, out_b, ((1,), (1,)))
    )

    inv_mlp = norm_scale(hidden1)
    normed_m = (hidden1 * inv_mlp * gain_m).astype(bf16)
    low_m = mm(normed_m, mlp_a, ((1,), (0,))).astype(bf16)
    grad_down = mm(cotangent, down_b, ((1,), (0,))).astype(bf16)
    low_all = jnp.concatenate([low_m, grad_down, jnp.zeros_like(grad_down)], axis=1)
    state, unit_grads = None, []
    for k in range(n_chunk):
        own, oth = ff_units[k]
        *state, unit_grad = mlp_call(own, oth, normed_m, cotangent, low_all, unit_b[k], state)
        unit_grads.append(unit_grad)
    ff_out, grad_m, small_m = state
    low_down = small_m[:, 2 * RANK : 3 * RANK].astype(bf16)
    result = (hidden1 + ff_out + mm(low_down, down_b, ((1,), (1,)))).astype(bf16)
    grad_low_m = small_m[:, : 2 * RANK].astype(bf16)
    grad_m = grad_m + mm(grad_low_m, mlp_a, ((1,), (1,)))
    grad1 = cotangent.astype(f32) + norm_back(hidden1, inv_mlp, gain_m, grad_m)

    grad_y = grad1.astype(bf16)
    grad_low_out = mm(grad_y, out_b, ((1,), (0,))).astype(bf16)
    grad_merged = (
        mm(grad_y, wo_all, ((1,), (0,))) + mm(grad_low_out, out_a, ((1,), (0,)))
    ).astype(bf16)
    block = ny * cols_t
    grad_rows = []
    for d in range(nx):
        part = grad_merged[:, d * block : (d + 1) * block]
        grad_rows.append(shift(part, "x", nx, -d) if d else part)
    grad_rows = [grad_rows[-d % nx] for d in range(nx)]
    grad_rows = in_order(grad_rows, x, nx)
    dq, dk, dv, dgate, dcum = attend_back(scalars, qk, vg, cum, mixed, lse, grad_rows)
    dcum = dcum[:, ::HEAD]
    dlog = mm(earlier, split_columns(dcum), ((0,), (0,)))
    dlog = dlog[:, :local_heads] + dlog[:, local_heads : 2 * local_heads] + dlog[:, 2 * local_heads :]
    dforget = (dlog * jax.nn.sigmoid(-logits)).astype(bf16)

    grad_x, grad_la, grad_in_b = 0.0, [], []
    pair_grads = ((dq, dk), (dv, dgate))
    for j in range(2):
        mine, other = chunks[j]
        for pieces, grad in zip((mine, other), core_pick(*pair_grads[j])):
            weight = jnp.concatenate(pieces, 1)
            grad_x = grad_x + mm(grad, weight, ((1,), (1,)))
        for i in range(2):
            grad = pair_grads[j][i]
            grad_la.append(mm(grad, in_b[2 * j + i], ((1,), (1,))))
            grad_in_b.append(mm(la[2 * j + i], grad, ((0,), (0,))))
    grad_x = grad_x + mm(dforget, wf, ((1,), (1,)))
    grad_la.append(mm(dforget, bf, ((1,), (1,))))
    grad_la = jnp.concatenate(grad_la, 1).astype(bf16)
    grad_forget_b = mm(la[4], dforget, ((0,), (0,)))
    grad_x = grad_x.astype(bf16)

    def scatter_rows(value):
        total = row_block(value, x).astype(f32)
        for d in range(1, nx):
            total = total + shift(row_block(value, (x + d) % nx), "x", nx, d).astype(f32)
        return total

    grad_low_in = scatter_rows(grad_la).astype(bf16)
    grad_normed = scatter_rows(grad_x) + mm(grad_low_in, in_a, ((1,), (1,)))
    input_grad = grad1 + norm_back(hidden, inv_att, gain_a, grad_normed)

    part_a = jnp.concatenate(
        [
            mm(normed, grad_low_in, ((0,), (0,))),
            mm(normed_m, grad_low_m, ((0,), (0,))),
            mm(grad_y, low_out, ((0,), (0,))),
            mm(cotangent, low_down, ((0,), (0,))),
        ],
        axis=1,
    ).astype(bf16)
    g_in_b = jnp.stack(grad_in_b).astype(bf16).reshape(4, RANK, ny, 2, share, sub_c)
    g_in_b = jnp.where(c == 0, g_in_b, jnp.flip(g_in_b, 3))
    g_in_b = g_in_b.transpose(3, 4, 2, 1, 0, 5).reshape(2, share, ny, 1, RANK, 4 * sub_c)
    g_in_b = jnp.pad(g_in_b, ((0, 0), (0, 0), (0, 0), (0, nx - 1), (0, 0), (0, 0)))
    g_out_a = mm(grad_low_out, merged_full, ((0,), (0,))).astype(bf16)
    g_out_a = g_out_a.reshape(RANK, nx, ny, 2, share, sub_c)
    g_out_a = jnp.where(c == 0, g_out_a, jnp.flip(g_out_a, 3)).transpose(3, 4, 2, 1, 0, 5)
    g_unit = jnp.stack(unit_grads)
    g_gu_b = (
        g_unit[:, :, : 2 * RANK]
        .reshape(n_chunk, ny, nx, 2, RANK, 2, per, sub_f)
        .transpose(5, 0, 6, 1, 2, 4, 3, 7)
        .reshape(2, share, ny, nx, RANK, 2 * sub_f)
    )
    g_down_a = (
        g_unit[:, :, 2 * RANK : 3 * RANK]
        .reshape(n_chunk, ny, nx, RANK, 2, per, sub_f)
        .transpose(4, 0, 5, 1, 2, 3, 6)
        .reshape(2, share, ny, nx, RANK, sub_f)
    )
    part_b = jnp.concatenate([g_in_b, g_out_a, g_gu_b, g_down_a], axis=-1)
    part_b = mm(reorder, part_b.reshape(count, RANK * n_cols), ((0,), (0,))).astype(bf16)
    part_f = mm(grad_forget_b.astype(bf16), head_pick, ((1,), (1,))).astype(bf16)
    part_f = part_f.reshape(RANK, n_tp, heads_t).transpose(1, 0, 2).reshape(1, n_tp, RANK * heads_t)
    part_f = jnp.broadcast_to(part_f, (n_fsdp, n_tp, RANK * heads_t)).reshape(count, RANK * heads_t)
    sent = jnp.concatenate([part_a.reshape(count, n_a), part_b, part_f], axis=1)
    sent = lax.all_to_all(sent, everyone, 0, 0, tiled=True)
    summed = mm(seq_hot, sent, ((0,), (0,)))
    sum_a = summed[:, :n_a].reshape(adapters, d_part, 9 * RANK)
    n_b = RANK * n_cols
    sum_b = summed[:, n_a : n_a + n_b].reshape(n_fsdp, rank_part, n_cols).astype(bf16)
    sum_f = summed[:, n_a + n_b :].reshape(ranks, heads_t)

    def by_feature(value, blocks):
        value = value.reshape(adapters, d_part, blocks, RANK)
        return value.transpose(1, 2, 0, 3).reshape(1, d_part, blocks * ranks)

    def by_rank(value):
        return value.transpose(0, 2, 1).reshape(1, ranks, d_part)

    out_in_a = by_feature(sum_a[:, :, : 5 * RANK], 5)
    out_mlp_a = by_feature(sum_a[:, :, 5 * RANK : 7 * RANK], 2)
    out_out_b = by_rank(sum_a[:, :, 7 * RANK : 8 * RANK])
    out_down_b = by_rank(sum_a[:, :, 8 * RANK :])
    out_forget = lax.dynamic_slice_in_dim(sum_f, (2 * z + c) * rank_part, rank_part, 0)[None]
    final = lax.all_to_all(sum_b, fsdp, 0, 0, tiled=True).astype(f32)
    at, cuts_b = 0, []
    for cut in cut_b:
        cuts_b.append(final[..., at : at + cut])
        at += cut
    out_in_b = (
        cuts_b[0].reshape(n_fsdp, rank_part, 4, sub_c).transpose(2, 1, 0, 3).reshape(
            1, 4, rank_part, cols_t
        )
    )
    out_out_a = cuts_b[1].transpose(0, 2, 1).reshape(1, cols_t, rank_part)
    out_gu_b = (
        cuts_b[2].reshape(n_fsdp, rank_part, 2, sub_f).transpose(2, 1, 0, 3).reshape(
            1, 2, rank_part, ff_t
        )
    )
    out_down_a = cuts_b[3].transpose(0, 2, 1).reshape(1, ff_t, rank_part)
    return (
        result, input_grad, out_in_a, out_in_b, out_forget, out_out_a, out_out_b, out_mlp_a,
        out_gu_b, out_down_a, out_down_b,
    )


def solution(mesh):
    n_fsdp, n_tp = mesh.shape["fsdp"], mesh.shape["tp"]
    fsdp, tp, both = ("z", "c"), ("y", "x"), ("z", "c", "y", "x")

    def run(*args):
        per_fsdp = args[3].shape[0] // n_fsdp
        sizes = (n_fsdp // 2, per_fsdp, n_tp // per_fsdp)
        devices = mesh.devices.reshape(sizes[0], 2, sizes[1], sizes[2])
        split = Mesh(devices, both)
        return jax.shard_map(
            functools.partial(on_device, sizes),
            mesh=split,
            in_specs=(
                P(both, None),
                P(both, None),
                P(fsdp, None),
                P(fsdp),
                P(None, both),
                P(None, fsdp, None, tp),
                P(None, fsdp, tp),
                P(None, tp),
                P(None, tp, fsdp),
                P(None, both),
                P(None, fsdp, None, tp),
                P(None, tp, fsdp),
                P(None, both, None),
                P(None, None, fsdp, tp),
                P(None, fsdp, tp),
                P(None, tp, fsdp),
                P(None, None, both),
                P(None, both, None),
                P(None, None, fsdp, tp),
                P(None, tp, fsdp),
                P(None, None, both),
            ),
            out_specs=(
                P(both, None),
                P(both, None),
                P(None, both, None),
                P(None, None, fsdp, tp),
                P(None, fsdp, tp),
                P(None, tp, fsdp),
                P(None, None, both),
                P(None, both, None),
                P(None, None, fsdp, tp),
                P(None, tp, fsdp),
                P(None, None, both),
            ),
            check_vma=False,
        )(*args)

    return run
```

time: 2120 us -> 842 us (0.40)
  waiting for transfers between devices: 1110 us -> 218 us
  blocking collectives: 380 us -> 0 us
  matrix products: 398 us -> 132 us
  Pallas kernels: 0 us -> 188 us
  starting transfers between devices: 1.4 us -> 105 us
  other arithmetic: 103 us -> 53.6 us
    reduce_scatter x16 -> x0, waiting for transfers between devices: 801 us -> none  [the longest x1 124 us: mlp_backward(): lax.psum_scatter(grad_normed, 'tp', scatter_dimension=0, tiled=True)]
    all_gather x11 -> x0, blocking collectives: 338 us -> none  [the longest x1 76.2 us: shared_pieces(): lax.all_gather(adapt_mlp_a[layer_index], ('fsdp', 'tp'), axis=0, tiled=True)]
    all_gather x11 -> x0, waiting for transfers between devices: 272 us -> none  [the longest x1 70.4 us: mlp_forward(): lax.all_gather(normed, 'tp', axis=0, tiled=True)]
    dot_general x51, matrix products: 398 us -> 132 us  [mm(): lax.dot_general(left, right, ((dims[0], dims[1]), ((), ())), preferred_el...]
    ppermute x0 -> x69, waiting for transfers between devices: none -> 210 us  [shift(): lax.ppermute(value, axis, [(i, (i + step) % size) for i in range(size)])]
    pallas_call x0 -> x14, Pallas kernels: none -> 188 us  [the longest x4 78.9 us: mlp_call(): pl.pallas_call(functools.partial(mlp_kernel, units, first, width), out_sh...]
    ppermute x0 -> x69, starting transfers between devices: none -> 78.3 us  [shift(): lax.ppermute(value, axis, [(i, (i + step) % size) for i in range(size)])]
    reduce_sum x7 -> x1, other arithmetic: 67.8 us -> 0.38 us  [norm_scale(): jnp.mean(hidden * hidden, axis=-1, keepdims=True) + epsilon]
  transfers between devices with their start and end apart: 28 -> 74, of which waited for: 21 -> 22; matrix products, arithmetic and copies ran while one was open for 25% -> 29% of each run, Pallas kernels for 0% -> 13%
where the time goes in v1:
time: 842 us; the launch traced here: 831 us
  waiting for transfers between devices  218 us (26%)
  Pallas kernels  188 us (22%)
  local copies, waits for them, and re-layouts  132 us (16%)
  matrix products  132 us (16%)
  starting transfers between devices  105 us (12%)
  other arithmetic  53.6 us (6%)
    ppermute x69, waiting for transfers between devices, shift(): lax.ppermute(value, axis, [(i, (i + step) % size) for i in range(size)])  210 us
    dot_general x51, matrix products, mm(): lax.dot_general(left, right, ((dims[0], dims[1]), ((), ())), preferred_el...  132 us
    pallas_call x4, Pallas kernels, mlp_call(): pl.pallas_call(functools.partial(mlp_kernel, units, first, width), out_sh...  78.9 us
    ppermute x69, starting transfers between devices, shift(): lax.ppermute(value, axis, [(i, (i + step) % size) for i in range(size)])  78.3 us
    pallas_call x1, Pallas kernels, attend_back(): prefetch_call(functools.partial(attend_back_kernel, length), (pairs,), [p...  56.1 us
    unnamed x236, local copies, waits for them, and re-layouts  33.7 us
    pallas_call x1, Pallas kernels, attend(): prefetch_call(functools.partial(attend_kernel, length), (pairs,), [pl.Blo...  32.3 us
  transfers between devices with their start and end apart: 74, of which 22 were waited for; matrix products, arithmetic and copies ran while one was open for 29% of the time, Pallas kernels for 13%

profile of v1, /device:TPU:0, one launch (start us, length us, event | category | flops | bytes accessed | tf_op | source)
XLA Modules:
  0.0 831.3 jit_solution(16544171497848357574)
XLA Ops:
  54.5 14.3 %collective-permute-done.9.refs_2_ = bf16[384,384]{1,0:T(8,128)(2,1)} collective-permute-done((bf16[384,384]{1,0:T(8,128)(2,1)S(1)}, bf16[384,384]{1,0:T(8,128)(2,1)}, u32[]{:S(2)}, u32[]{:S(2)}) %collective-permute-start.9) | collective-permute-done | bytes 294944 | tf_op jit(solution)/shard_map/ppermute | solution.py:32
  101.4 17.7 %collective-permute-done.57.refs_2_ = bf16[3,384,128]{2,1,0:T(8,128)(2,1)} collective-permute-done((bf16[3,384,128]{2,1,0:T(8,128)(2,1)S(1)}, bf16[3,384,128]{2,1,0:T(8,128)(2,1)}, u32[]{:S(2)}, u32[]{:S(2)}) %collective-permute-start.57) | collective-permute-done | bytes 294944 | tf_op jit(solution)/shard_map/ppermute | solution.py:32
  138.9 14.9 %collective-permute-done.47.refs_2_ = bf16[3,384,128]{2,1,0:T(8,128)(2,1)} collective-permute-done((bf16[3,384,128]{2,1,0:T(8,128)(2,1)}, bf16[3,384,128]{2,1,0:T(8,128)(2,1)}, u32[]{:S(2)}, u32[]{:S(2)}) %collective-permute-start.47) | collective-permute-done | bytes 294944 | tf_op jit(solution)/shard_map/ppermute | solution.py:32
  153.9 8.1 collective-permute-start.27
  167.3 14.1 %collective-permute-done.37.refs_2_ = bf16[3,384,128]{2,1,0:T(8,128)(2,1)} collective-permute-done((bf16[3,384,128]{2,1,0:T(8,128)(2,1)}, bf16[3,384,128]{2,1,0:T(8,128)(2,1)}, u32[]{:S(2)}, u32[]{:S(2)}) %collective-permute-start.37) | collective-permute-done | bytes 294944 | tf_op jit(solution)/shard_map/ppermute | solution.py:32
  185.7 19.9 %collective-permute-done.27.refs_2_ = bf16[3,384,128]{2,1,0:T(8,128)(2,1)} collective-permute-done((bf16[3,384,128]{2,1,0:T(8,128)(2,1)S(1)}, bf16[3,384,128]{2,1,0:T(8,128)(2,1)}, u32[]{:S(2)}, u32[]{:S(2)}) %collective-permute-start.27) | collective-permute-done | bytes 294944 | tf_op jit(solution)/shard_map/ppermute | solution.py:32
  260.6 25.3 %collective-permute-done.5 = bf16[1536,384]{1,0:T(8,128)(2,1)} collective-permute-done((bf16[1536,384]{1,0:T(8,128)(2,1)}, bf16[1536,384]{1,0:T(8,128)(2,1)}, u32[]{:S(2)}, u32[]{:S(2)}) %collective-permute-start.5) | collective-permute-done | bytes 1179680 | tf_op jit(solution)/shard_map/ppermute | solution.py:32
  298.7 8.0 add_bitcast_fusion.1
  311.3 7.5 fusion.25
  355.9 32.3 %attend.1 = (bf16[1024,768]{1,0:T(8,128)(2,1)}, f32[1024,768]{1,0:T(8,128)}, f32[1024,768]{1,0:T(8,128)}) custom-call(s32[3]{0:T(128)} %pad_add_fusion.starts_ref, bf16[2,1024,768]{2,1,0:T(8,128)(2,1)} %pad_maximum_fusion.1.q_ref.k_ref, bf16[2,1024,768]{2,1,0:T(8,128)(2,1)} %pad_maximum_fusion.1.q_ref.k_ref, f32[2,1024,768]{2,1,0:T(8,128)} %pad_maximum_fusion.v_ref.gate_ref, ...), custom_call_target="tpu_custom_call" | custom-call | flops 7549747200 | bytes 20447232 | tf_op jit(solution)/shard_map/attend/pallas_call | solution.py:338
  398.2 13.5 %collective-permute-done.14 = bf16[512,768]{1,0:T(8,128)(2,1)} collective-permute-done((bf16[512,768]{1,0:T(8,128)(2,1)}, bf16[512,768]{1,0:T(8,128)(2,1)}, u32[]{:S(2)}, u32[]{:S(2)}) %collective-permute-start.14) | collective-permute-done | bytes 786464 | tf_op jit(solution)/shard_map/ppermute | solution.py:32
  414.3 9.1 %collective-permute-done.30.refs_2_ = bf16[3,1536,128]{2,1,0:T(8,128)(2,1)} collective-permute-done((bf16[3,1536,128]{2,1,0:T(8,128)(2,1)S(1)}, bf16[3,1536,128]{2,1,0:T(8,128)(2,1)}, u32[]{:S(2)}, u32[]{:S(2)}) %collective-permute-start.30) | collective-permute-done | bytes 1179680 | tf_op jit(solution)/shard_map/ppermute | solution.py:32
  423.8 13.2 %collective-permute-done.29.refs_1_ = bf16[3,1536,128]{2,1,0:T(8,128)(2,1)} collective-permute-done((bf16[3,1536,128]{2,1,0:T(8,128)(2,1)S(1)}, bf16[3,1536,128]{2,1,0:T(8,128)(2,1)}, u32[]{:S(2)}, u32[]{:S(2)}) %collective-permute-start.29) | collective-permute-done | bytes 1179680 | tf_op jit(solution)/shard_map/ppermute | solution.py:32
  437.0 10.9 %collective-permute-done.61.refs_3_ = bf16[3,1536,128]{2,1,0:T(8,128)(2,1)} collective-permute-done((bf16[3,1536,128]{2,1,0:T(8,128)(2,1)}, bf16[3,1536,128]{2,1,0:T(8,128)(2,1)}, u32[]{:S(2)}, u32[]{:S(2)}) %collective-permute-start.61) | collective-permute-done | bytes 1179680 | tf_op jit(solution)/shard_map/ppermute | solution.py:32
  463.9 12.6 %collective-permute-done.41.refs_3_ = bf16[3,1536,128]{2,1,0:T(8,128)(2,1)S(1)} collective-permute-done((bf16[3,1536,128]{2,1,0:T(8,128)(2,1)}, bf16[3,1536,128]{2,1,0:T(8,128)(2,1)S(1)}, u32[]{:S(2)}, u32[]{:S(2)}) %collective-permute-start.41) | collective-permute-done | bytes 1179680 | tf_op jit(solution)/shard_map/ppermute | solution.py:32
  479.2 18.3 %feed_forward.4 = (f32[512,1536]{1,0:T(8,128)}, f32[512,1536]{1,0:T(8,128)}, f32[512,64]{1,0:T(8,128)}, bf16[4,64,256]{2,1,0:T(8,128)(2,1)}) custom-call(bf16[3,1536,128]{2,1,0:T(8,128)(2,1)} %assemble.13.refs_0_, bf16[3,1536,128]{2,1,0:T(8,128)(2,1)} %collective-permute-done.59.refs_1_, bf16[3,1536,128]{2,1,0:T(8,128)(2,1)} %collective-permute-done.60.refs_2_, ...), custom_call_target="tpu_custom_call" | custom-call | flops 9663676416 | bytes 25165824 | tf_op jit(solution)/shard_map/feed_forward/pallas_call | solution.py:211
  498.6 20.2 %feed_forward.5 = (f32[512,1536]{1,0:T(8,128)}, f32[512,1536]{1,0:T(8,128)}, f32[512,64]{1,0:T(8,128)}, bf16[4,64,256]{2,1,0:T(8,128)(2,1)}) custom-call(bf16[3,1536,128]{2,1,0:T(8,128)(2,1)} %assemble.12.refs_0_, bf16[3,1536,128]{2,1,0:T(8,128)(2,1)} %collective-permute-done.49.refs_1_, bf16[3,1536,128]{2,1,0:T(8,128)(2,1)} %collective-permute-done.50.refs_2_, ...), custom_call_target="tpu_custom_call" | custom-call | flops 9663676416 | bytes 25165824 | tf_op jit(solution)/shard_map/feed_forward/pallas_call | solution.py:211
  518.8 20.2 %feed_forward.6 = (f32[512,1536]{1,0:T(8,128)}, f32[512,1536]{1,0:T(8,128)}, f32[512,64]{1,0:T(8,128)}, bf16[4,64,256]{2,1,0:T(8,128)(2,1)}) custom-call(bf16[3,1536,128]{2,1,0:T(8,128)(2,1)} %assemble.11.refs_0_, bf16[3,1536,128]{2,1,0:T(8,128)(2,1)} %collective-permute-done.39.refs_1_, bf16[3,1536,128]{2,1,0:T(8,128)(2,1)} %collective-permute-done.40.refs_2_, ...), custom_call_target="tpu_custom_call" | custom-call | flops 9663676416 | bytes 25165824 | tf_op jit(solution)/shard_map/feed_forward/pallas_call | solution.py:211
  539.1 20.2 %feed_forward.7 = (f32[512,1536]{1,0:T(8,128)}, f32[512,1536]{1,0:T(8,128)}, f32[512,64]{1,0:T(8,128)}, bf16[4,64,256]{2,1,0:T(8,128)(2,1)}) custom-call(bf16[3,1536,128]{2,1,0:T(8,128)(2,1)} %assemble.10.refs_0_, bf16[3,1536,128]{2,1,0:T(8,128)(2,1)} %collective-permute-done.29.refs_1_, bf16[3,1536,128]{2,1,0:T(8,128)(2,1)} %collective-permute-done.30.refs_2_, ...), custom_call_target="tpu_custom_call" | custom-call | flops 9663676416 | bytes 25165824 | tf_op jit(solution)/shard_map/feed_forward/pallas_call | solution.py:211
  601.1 56.1 %attend_back.1 = (bf16[1024,768]{1,0:T(8,128)(2,1)}, bf16[1024,768]{1,0:T(8,128)(2,1)}, bf16[1024,768]{1,0:T(8,128)(2,1)}, bf16[1024,768]{1,0:T(8,128)(2,1)}, f32[1024,768]{1,0:T(8,128)}) custom-call(s32[3]{0:T(128)} %pad_add_fusion.starts_ref, bf16[2,1024,768]{2,1,0:T(8,128)(2,1)} %pad_maximum_fusion.1.q_ref.k_ref, ...), custom_call_target="tpu_custom_call" | custom-call | flops 18874368000 | bytes 26738688 | tf_op jit(solution)/shard_map/attend_back/pallas_call | solution.py:449
  717.9 7.5 fusion.18
  732.0 12.2 %add_convert_fusion = bf16[1024,1536]{1,0:T(8,128)(2,1)} fusion(f32[1024,1536]{1,0:T(8,128)S(1)} %bitcast.244, f32[1024,1536]{1,0:T(8,128)} %fusion.14, f32[1024,1536]{1,0:T(8,128)} %fusion.18, f32[1024,1536]{1,0:T(8,128)} %fusion.16, bf16[1536,768]{1,0:T(8,128)(2,1)} %copy-done.22, bf16[1024,768]{1,0:T(8,128)(2,1)} %get-tuple-element.53, ...), kind=kOutput, calls=%fused_computation.5 | convolution fusion | flops 2424569856 | bytes 33816576 | tf_op jit(solution)/shard_map/dot_general | solution.py:28
  769.9 8.4 %all-to-all-start.3 = ((bf16[32,2,8496]{2,1,0:T(2,128)(2,1)}), bf16[32,2,8496]{2,1,0:T(2,128)(2,1)}, u32[]{:S(2)}, u32[]{:S(2)}) async-start(bf16[32,2,8496]{2,1,0:T(2,128)(2,1)} %reshape.462), calls=%async_computation.3 | async-start | bytes 2195456 | tf_op jit(solution)/shard_map/all_to_all | solution.py:829
  783.2 11.4 %collective-permute-done.67 = bf16[512,1536]{1,0:T(8,128)(2,1)} collective-permute-done((bf16[512,1536]{1,0:T(8,128)(2,1)}, bf16[512,1536]{1,0:T(8,128)(2,1)}, u32[]{:S(2)}, u32[]{:S(2)}) %collective-permute-start.67) | collective-permute-done | bytes 1572896 | tf_op jit(solution)/shard_map/ppermute | solution.py:32
  (607 shorter events, 432.2 us)
Async XLA Ops:
  4.1 47.0 %collective-permute-start.25 = (bf16[3,192,512]{2,1,0:T(8,128)(2,1)}, bf16[3,192,512]{2,1,0:T(8,128)(2,1)}, u32[]{:S(2)}, u32[]{:S(2)}) collective-permute-start(bf16[3,192,512]{2,1,0:T(8,128)(2,1)} %get-tuple-element.134), channel_id=1, source_target_pairs={{0,4},{4,0},{1,5},{5,1},{2,6},{6,2},{3,7},{7,3},{8,12},{12,8},{9,1... | collective-permute-start | bytes 1769480 | tf_op jit(solution)/shard_map/ppermute | solution.py:32
  16.5 64.4 %all-to-all-start = ((bf16[32,2,676]{2,1,0:T(2,128)(2,1)}), bf16[32,2,676]{2,1,0:T(2,128)(2,1)}, u32[]{:S(2)}, u32[]{:S(2)}) async-start(bf16[32,2,676]{2,1,0:T(2,128)(2,1)} %reshape.458), calls=%async_computation | async-start | bytes 196608 | tf_op jit(solution)/shard_map/all_to_all | solution.py:522
  29.1 59.4 %collective-permute-start.19 = (bf16[4,192,384]{2,1,0:T(8,128)(2,1)}, bf16[4,192,384]{2,1,0:T(8,128)(2,1)}, u32[]{:S(2)}, u32[]{:S(2)}) collective-permute-start(bf16[4,192,384]{2,1,0:T(8,128)(2,1)} %assemble.9.refs_0_), channel_id=1, source_target_pairs={{0,1},{1,0},{2,3},{3,2},{4,5},{5,4},{6,7},{7,6},{8,9},{9,8},{10,11... | collective-permute-start | bytes 1769480 | tf_op jit(solution)/shard_map/ppermute | solution.py:32
  95.2 58.7 %collective-permute-start.47 = (bf16[3,384,128]{2,1,0:T(8,128)(2,1)}, bf16[3,384,128]{2,1,0:T(8,128)(2,1)}, u32[]{:S(2)}, u32[]{:S(2)}) collective-permute-start(bf16[3,384,128]{2,1,0:T(8,128)(2,1)} %get-tuple-element.130.refs_0_), channel_id=1, source_target_pairs={{0,16},{8,24},{16,0},{24,8},{1,17},{9,25},{17,1},{25,9},{2,18},{10... | collective-permute-start | bytes 884744 | tf_op jit(solution)/shard_map/ppermute | solution.py:32
  96.1 57.7 %collective-permute-start.48 = (bf16[3,384,128]{2,1,0:T(8,128)(2,1)}, bf16[3,384,128]{2,1,0:T(8,128)(2,1)}, u32[]{:S(2)}, u32[]{:S(2)}) collective-permute-start(bf16[3,384,128]{2,1,0:T(8,128)(2,1)} %get-tuple-element.130.refs_0_), channel_id=1, source_target_pairs={{0,24},{8,0},{16,8},{24,16},{1,25},{9,1},{17,9},{25,17},{2,26},{10... | collective-permute-start | bytes 884744 | tf_op jit(solution)/shard_map/ppermute | solution.py:32
  119.1 48.1 %collective-permute-start.36 = (bf16[3,384,128]{2,1,0:T(8,128)(2,1)}, bf16[3,384,128]{2,1,0:T(8,128)(2,1)}, u32[]{:S(2)}, u32[]{:S(2)}) collective-permute-start(bf16[3,384,128]{2,1,0:T(8,128)(2,1)} %get-tuple-element.131.refs_0_), channel_id=1, source_target_pairs={{0,8},{8,16},{16,24},{24,0},{1,9},{9,17},{17,25},{25,1},{2,10},{10... | collective-permute-start | bytes 884744 | tf_op jit(solution)/shard_map/ppermute | solution.py:32
  123.3 58.1 %collective-permute-start.37 = (bf16[3,384,128]{2,1,0:T(8,128)(2,1)}, bf16[3,384,128]{2,1,0:T(8,128)(2,1)}, u32[]{:S(2)}, u32[]{:S(2)}) collective-permute-start(bf16[3,384,128]{2,1,0:T(8,128)(2,1)} %get-tuple-element.131.refs_0_), channel_id=1, source_target_pairs={{0,16},{8,24},{16,0},{24,8},{1,17},{9,25},{17,1},{25,9},{2,18},{10... | collective-permute-start | bytes 884744 | tf_op jit(solution)/shard_map/ppermute | solution.py:32
  132.4 113.6 %all-to-all-start.2 = ((bf16[32,2,8448]{2,1,0:T(2,128)(2,1)}), bf16[32,2,8448]{2,1,0:T(2,128)(2,1)S(1)}, u32[]{:S(2)}, u32[]{:S(2)}) async-start(bf16[32,2,8448]{2,1,0:T(2,128)(2,1)} %reshape.460), calls=%async_computation.2 | async-start | bytes 2162688 | tf_op jit(solution)/shard_map/all_to_all | solution.py:636
  135.3 47.6 %collective-permute-start.38 = (bf16[3,384,128]{2,1,0:T(8,128)(2,1)}, bf16[3,384,128]{2,1,0:T(8,128)(2,1)S(1)}, u32[]{:S(2)}, u32[]{:S(2)}) collective-permute-start(bf16[3,384,128]{2,1,0:T(8,128)(2,1)} %get-tuple-element.131.refs_0_), channel_id=1, source_target_pairs={{0,24},{8,0},{16,8},{24,16},{1,25},{9,1},{17,9},{25,17},{2,26},{10... | collective-permute-start | bytes 884744 | tf_op jit(solution)/shard_map/ppermute | solution.py:32
  153.9 51.8 %collective-permute-start.27 = (bf16[3,384,128]{2,1,0:T(8,128)(2,1)S(1)}, bf16[3,384,128]{2,1,0:T(8,128)(2,1)}, u32[]{:S(2)}, u32[]{:S(2)}) collective-permute-start(bf16[3,384,128]{2,1,0:T(8,128)(2,1)S(1)} %get-tuple-element.132.refs_0_), channel_id=1, source_target_pairs={{0,16},{8,24},{16,0},{24,8},{1,17},{9,25},{17,1},{25,9},{2,18},{10... | collective-permute-start | bytes 884744 | tf_op jit(solution)/shard_map/ppermute | solution.py:32
  167.2 64.2 %collective-permute-start.12 = (bf16[1536,384]{1,0:T(8,128)(2,1)}, bf16[1536,384]{1,0:T(8,128)(2,1)}, u32[]{:S(2)}, u32[]{:S(2)}) collective-permute-start(bf16[1536,384]{1,0:T(8,128)(2,1)} %assemble.8), channel_id=1, source_target_pairs={{0,4},{4,0},{1,5},{5,1},{2,6},{6,2},{3,7},{7,3},{8,12},{12,8},{9,1... | collective-permute-start | bytes 3538952 | tf_op jit(solution)/shard_map/ppermute | solution.py:32
  181.4 51.7 %collective-permute-start.6 = (bf16[1536,384]{1,0:T(8,128)(2,1)}, bf16[1536,384]{1,0:T(8,128)(2,1)}, u32[]{:S(2)}, u32[]{:S(2)}) collective-permute-start(bf16[1536,384]{1,0:T(8,128)(2,1)} %assemble.7), channel_id=1, source_target_pairs={{0,4},{4,0},{1,5},{5,1},{2,6},{6,2},{3,7},{7,3},{8,12},{12,8},{9,1... | collective-permute-start | bytes 3538952 | tf_op jit(solution)/shard_map/ppermute | solution.py:32
  233.1 52.9 %collective-permute-start.5 = (bf16[1536,384]{1,0:T(8,128)(2,1)}, bf16[1536,384]{1,0:T(8,128)(2,1)}, u32[]{:S(2)}, u32[]{:S(2)}) collective-permute-start(bf16[1536,384]{1,0:T(8,128)(2,1)} %assemble.7), channel_id=1, source_target_pairs={{0,2},{2,0},{1,3},{3,1},{4,6},{6,4},{5,7},{7,5},{8,10},{10,8},{9,1... | collective-permute-start | bytes 3538952 | tf_op jit(solution)/shard_map/ppermute | solution.py:32
  238.4 109.4 %collective-permute-start.59 = (bf16[3,1536,128]{2,1,0:T(8,128)(2,1)}, bf16[3,1536,128]{2,1,0:T(8,128)(2,1)}, u32[]{:S(2)}, u32[]{:S(2)}) collective-permute-start(bf16[3,1536,128]{2,1,0:T(8,128)(2,1)} %assemble.13.refs_0_), channel_id=1, source_target_pairs={{0,1},{1,0},{2,3},{3,2},{4,5},{5,4},{6,7},{7,6},{8,9},{9,8},{10,11... | collective-permute-start | bytes 3538952 | tf_op jit(solution)/shard_map/ppermute | solution.py:32
  240.0 107.8 %collective-permute-start.60 = (bf16[3,1536,128]{2,1,0:T(8,128)(2,1)}, bf16[3,1536,128]{2,1,0:T(8,128)(2,1)}, u32[]{:S(2)}, u32[]{:S(2)}) collective-permute-start(bf16[3,1536,128]{2,1,0:T(8,128)(2,1)} %assemble.13.refs_0_), channel_id=1, source_target_pairs={{0,2},{2,0},{1,3},{3,1},{4,6},{6,4},{5,7},{7,5},{8,10},{10,8},{9,1... | collective-permute-start | bytes 3538952 | tf_op jit(solution)/shard_map/ppermute | solution.py:32
  257.7 90.8 %collective-permute-start.62 = (bf16[3,1536,128]{2,1,0:T(8,128)(2,1)}, bf16[3,1536,128]{2,1,0:T(8,128)(2,1)}, u32[]{:S(2)}, u32[]{:S(2)}) collective-permute-start(bf16[3,1536,128]{2,1,0:T(8,128)(2,1)} %assemble.13.refs_0_), channel_id=1, source_target_pairs={{0,4},{4,0},{1,5},{5,1},{2,6},{6,2},{3,7},{7,3},{8,12},{12,8},{9,1... | collective-permute-start | bytes 3538952 | tf_op jit(solution)/shard_map/ppermute | solution.py:32
  260.6 64.1 %collective-permute-start.13 = (bf16[1536,384]{1,0:T(8,128)(2,1)}, bf16[1536,384]{1,0:T(8,128)(2,1)}, u32[]{:S(2)}, u32[]{:S(2)}) collective-permute-start(bf16[1536,384]{1,0:T(8,128)(2,1)} %collective-permute-done.11), channel_id=1, source_target_pairs={{0,4},{4,0},{1,5},{5,1},{2,6},{6,2},{3,7},{7,3},{8,12},{12,8},{9,1... | collective-permute-start | bytes 3538952 | tf_op jit(solution)/shard_map/ppermute | solution.py:32
  285.9 49.3 %collective-permute-start.7 = (bf16[1536,384]{1,0:T(8,128)(2,1)}, bf16[1536,384]{1,0:T(8,128)(2,1)}, u32[]{:S(2)}, u32[]{:S(2)}) collective-permute-start(bf16[1536,384]{1,0:T(8,128)(2,1)} %collective-permute-done.5), channel_id=1, source_target_pairs={{0,4},{4,0},{1,5},{5,1},{2,6},{6,2},{3,7},{7,3},{8,12},{12,8},{9,1... | collective-permute-start | bytes 3538952 | tf_op jit(solution)/shard_map/ppermute | solution.py:32
  335.2 55.7 %collective-permute-start.49 = (bf16[3,1536,128]{2,1,0:T(8,128)(2,1)}, bf16[3,1536,128]{2,1,0:T(8,128)(2,1)}, u32[]{:S(2)}, u32[]{:S(2)}) collective-permute-start(bf16[3,1536,128]{2,1,0:T(8,128)(2,1)} %assemble.12.refs_0_), channel_id=1, source_target_pairs={{0,1},{1,0},{2,3},{3,2},{4,5},{5,4},{6,7},{7,6},{8,9},{9,8},{10,11... | collective-permute-start | bytes 3538952 | tf_op jit(solution)/shard_map/ppermute | solution.py:32
  347.8 48.0 %collective-permute-start.39 = (bf16[3,1536,128]{2,1,0:T(8,128)(2,1)}, bf16[3,1536,128]{2,1,0:T(8,128)(2,1)}, u32[]{:S(2)}, u32[]{:S(2)}) collective-permute-start(bf16[3,1536,128]{2,1,0:T(8,128)(2,1)} %assemble.11.refs_0_), channel_id=1, source_target_pairs={{0,1},{1,0},{2,3},{3,2},{4,5},{5,4},{6,7},{7,6},{8,9},{9,8},{10,11... | collective-permute-start | bytes 3538952 | tf_op jit(solution)/shard_map/ppermute | solution.py:32
  348.4 48.0 %collective-permute-start.40 = (bf16[3,1536,128]{2,1,0:T(8,128)(2,1)}, bf16[3,1536,128]{2,1,0:T(8,128)(2,1)}, u32[]{:S(2)}, u32[]{:S(2)}) collective-permute-start(bf16[3,1536,128]{2,1,0:T(8,128)(2,1)} %assemble.11.refs_0_), channel_id=1, source_target_pairs={{0,2},{2,0},{1,3},{3,1},{4,6},{6,4},{5,7},{7,5},{8,10},{10,8},{9,1... | collective-permute-start | bytes 3538952 | tf_op jit(solution)/shard_map/ppermute | solution.py:32
  396.4 51.5 %collective-permute-start.61 = (bf16[3,1536,128]{2,1,0:T(8,128)(2,1)}, bf16[3,1536,128]{2,1,0:T(8,128)(2,1)}, u32[]{:S(2)}, u32[]{:S(2)}) collective-permute-start(bf16[3,1536,128]{2,1,0:T(8,128)(2,1)} %collective-permute-done.59.refs_1_), channel_id=1, source_target_pairs={{0,2},{2,0},{1,3},{3,1},{4,6},{6,4},{5,7},{7,5},{8,10},{10,8},{9,1... | collective-permute-start | bytes 3538952 | tf_op jit(solution)/shard_map/ppermute | solution.py:32
  396.9 51.0 %collective-permute-start.63 = (bf16[3,1536,128]{2,1,0:T(8,128)(2,1)}, bf16[3,1536,128]{2,1,0:T(8,128)(2,1)}, u32[]{:S(2)}, u32[]{:S(2)}) collective-permute-start(bf16[3,1536,128]{2,1,0:T(8,128)(2,1)} %collective-permute-done.59.refs_1_), channel_id=1, source_target_pairs={{0,4},{4,0},{1,5},{5,1},{2,6},{6,2},{3,7},{7,3},{8,12},{12,8},{9,1... | collective-permute-start | bytes 3538952 | tf_op jit(solution)/shard_map/ppermute | solution.py:32
  694.1 58.4 %collective-permute-start.68 = (bf16[512,80]{0,1:T(8,128)(2,1)}, bf16[512,80]{0,1:T(8,128)(2,1)}, u32[]{:S(2)}, u32[]{:S(2)}) collective-permute-start(bf16[512,80]{0,1:T(8,128)(2,1)} %constant_dynamic-slice_fusion), channel_id=1, source_target_pairs={{0,1},{1,0},{2,3},{3,2},{4,5},{5,4},{6,7},{7,6},{8,9},{9,8},{10,11... | collective-permute-start | bytes 245768 | tf_op jit(solution)/shard_map/ppermute | solution.py:32
  (154 other events, 3534.1 us)

commit v2 on v1

--- a/solution.py
+++ b/solution.py
@@ -46,119 +46,188 @@
     return jnp.concatenate([high, mid, value - high - mid], 1).astype(bf16)
 
 
-def in_order(pieces, index, size):
+def in_order(pieces, index, size, axis=0):
     if size == 1:
         return pieces[0]
     if size == 2:
         return jnp.where(
-            index == 0, jnp.concatenate(pieces, 0), jnp.concatenate(pieces[::-1], 0)
+            index == 0, jnp.concatenate(pieces, axis), jnp.concatenate(pieces[::-1], axis)
         )
-    rows = pieces[0].shape[0]
-    out = jnp.zeros((size * rows,) + pieces[0].shape[1:], pieces[0].dtype)
-    for d, piece in enumerate(pieces):
-        out = lax.dynamic_update_slice_in_dim(out, piece, ((index - d) % size) * rows, 0)
-    return out
-
-
-def assemble_kernel(count, axis, width, at_ref, *refs):
-    pieces, out, buf, sem = refs[:count], refs[count], refs[count + 1], refs[count + 2]
-    copies = []
-    for d in range(count):
-        where = pl.multiple_of(lax.rem(at_ref[0] - d + count, count) * width, width)
-        spot = (slice(None),) * axis + (pl.ds(where, width),)
-        copies.append(pltpu.make_async_copy(pieces[d], buf.at[spot], sem.at[d]))
-    for copy in copies:
-        copy.start()
-    for copy in copies:
-        copy.wait()
-    last = pltpu.make_async_copy(buf, out, sem.at[count])
-    last.start()
-    last.wait()
-
-
-def assemble(pieces, index, axis):
-    count = len(pieces)
     shape = list(pieces[0].shape)
     width = shape[axis]
-    shape[axis] = width * count
-    size = 2 * functools.reduce(lambda a, b: a * b, shape)
+    shape[axis] = size * width
+    out = jnp.zeros(tuple(shape), pieces[0].dtype)
+    for d, piece in enumerate(pieces):
+        out = lax.dynamic_update_slice_in_dim(out, piece, ((index - d) % size) * width, axis)
+    return out
+
+
+def fetch_rows(gathered, buf, sem, shares, index, columns=None):
+    part = gathered.shape[-2]
+    for f in range(shares):
+        where = pl.ds(f * part, part)
+        if columns is None:
+            pltpu.make_async_copy(gathered.at[f, index], buf.at[index, where], sem.at[index]).start()
+            continue
+        for plane, start in enumerate(columns):
+            source = gathered.at[f, index, :, pl.ds(start, buf.shape[-1])]
+            spot = buf.at[index, plane, where] if len(buf.shape) == 4 else buf.at[index, where]
+            pltpu.make_async_copy(source, spot, sem.at[index]).start()
+
+
+def wait_rows(buf, sem, index):
+    pltpu.make_async_copy(buf.at[index], buf.at[index], sem.at[index]).wait()
+
+
+def project_kernel(shares, blocks, cols, gathered, x_ref, low_ref, up_ref, q_ref, k_ref, v_ref, gate_ref, wbuf, sem):
+    for b in range(blocks):
+        fetch_rows(gathered, wbuf, sem, shares, b)
+    for b in range(blocks):
+        wait_rows(wbuf, sem, b)
+
+        def step(i, carry):
+            rows = pl.ds(pl.multiple_of(i * BLOCK, BLOCK), BLOCK)
+            out = mm(x_ref[rows, :], wbuf[b], ((1,), (0,)))
+            out = out + mm(low_ref[rows, :], up_ref[b], ((1,), (0,)))
+            for j, ref in enumerate((q_ref, k_ref, v_ref, gate_ref)):
+                piece = out[:, j * cols : (j + 1) * cols]
+                ref[rows, b * cols : (b + 1) * cols] = piece.astype(ref.dtype)
+            return carry
+
+        lax.fori_loop(0, x_ref.shape[0] // BLOCK, step, 0)
+
+
+def project(gathered, normed, low, up):
+    shares, blocks, part, wide = gathered.shape
+    length, depth = normed.shape
+    cols = wide // 4
+    out = jax.ShapeDtypeStruct((length, blocks * cols), bf16)
     return pl.pallas_call(
-        functools.partial(assemble_kernel, count, axis, width),
-        out_shape=jax.ShapeDtypeStruct(tuple(shape), pieces[0].dtype),
-        grid_spec=pltpu.PrefetchScalarGridSpec(
-            num_scalar_prefetch=1,
-            grid=(1,),
-            in_specs=[ANY] * count,
-            out_specs=ANY,
-            scratch_shapes=[
-                pltpu.VMEM(tuple(shape), pieces[0].dtype),
-                pltpu.SemaphoreType.DMA((count + 1,)),
-            ],
+        functools.partial(project_kernel, shares, blocks, cols),
+        out_shape=(out, out, out, jax.ShapeDtypeStruct((length, blocks * cols), f32)),
+        in_specs=[ANY] + [WHOLE] * 3,
+        out_specs=(WHOLE,) * 4,
+        scratch_shapes=[
+            pltpu.VMEM((blocks, depth, wide), bf16),
+            pltpu.SemaphoreType.DMA((blocks,)),
+        ],
+        cost_estimate=pl.CostEstimate(
+            flops=2 * length * depth * blocks * wide,
+            bytes_accessed=2 * depth * blocks * wide + 12 * length * depth,
+            transcendentals=0,
         ),
-        cost_estimate=pl.CostEstimate(flops=0, bytes_accessed=2 * size, transcendentals=0),
         compiler_params=pltpu.CompilerParams(vmem_limit_bytes=VMEM_LIMIT),
-        name="assemble",
-    )(jnp.reshape(index, (1,)).astype(jnp.int32), *pieces)
-
-
-def out_weight_kernel(blocks, cols, at_ref, *refs):
-    mine, other = refs[:blocks], refs[blocks : 2 * blocks]
-    out, buf, sem = refs[2 * blocks :]
-    core = at_ref[0]
-    copies = []
-    for i in range(blocks):
-        for k, source in enumerate((mine[i], other[i])):
-            spot = buf.at[:, lax.rem(core + k, 2), :, pl.ds(i * cols, cols)]
-            copies.append(pltpu.make_async_copy(source, spot, sem.at[2 * i + k]))
-    for copy in copies:
-        copy.start()
-    for copy in copies:
-        copy.wait()
-    last = pltpu.make_async_copy(buf, out, sem.at[2 * blocks])
-    last.start()
-    last.wait()
-
-
-def out_weight(mine, other, core):
-    blocks = len(mine)
-    nz, rows, cols = mine[0].shape
-    if cols % LANES:
-        mine, other = jnp.concatenate(mine, 2), jnp.concatenate(other, 2)
-        return jnp.where(core == 0, jnp.stack([mine, other], 1), jnp.stack([other, mine], 1))
-    shape = (nz, 2, rows, blocks * cols)
-    size = 2 * nz * 2 * rows * blocks * cols
+        name="project",
+    )(gathered, normed, low, up)
+
+
+def project_back_kernel(
+    shares, blocks, cols, gathered, dq_ref, dk_ref, dv_ref, dgate_ref, tail_ref, wf_ref, low_ref, up_ref,
+    dx_ref, dlow_ref, dup_ref, wbuf, sem,
+):
+    for b in range(blocks):
+        fetch_rows(gathered, wbuf, sem, shares, b)
+    dup_ref[...] = jnp.zeros_like(dup_ref)
+    for b in range(blocks):
+        wait_rows(wbuf, sem, b)
+
+    def step(i, carry):
+        rows = pl.ds(pl.multiple_of(i * BLOCK, BLOCK), BLOCK)
+        total = mm(tail_ref[rows, :], wf_ref[...], ((1,), (1,)))
+        small = None
+        for b in range(blocks):
+            grad = jnp.concatenate(
+                [ref[rows, b * cols : (b + 1) * cols] for ref in (dq_ref, dk_ref, dv_ref, dgate_ref)], 1
+            )
+            total = total + mm(grad, wbuf[b], ((1,), (1,)))
+            part = mm(grad, up_ref[b], ((1,), (1,)))
+            small = part if small is None else small + part
+            dup_ref[b] += mm(low_ref[rows, :], grad, ((0,), (0,)))
+        dx_ref[rows, :] = total.astype(bf16)
+        dlow_ref[rows, :] = small.astype(bf16)
+        return carry
+
+    lax.fori_loop(0, dx_ref.shape[0] // BLOCK, step, 0)
+
+
+def project_back(gathered, dq, dk, dv, dgate, tail, wf, low, up):
+    shares, blocks, part, wide = gathered.shape
+    depth, length, ranks = shares * part, dq.shape[0], low.shape[1]
     return pl.pallas_call(
-        functools.partial(out_weight_kernel, blocks, cols),
-        out_shape=jax.ShapeDtypeStruct(shape, bf16),
-        grid_spec=pltpu.PrefetchScalarGridSpec(
-            num_scalar_prefetch=1,
-            grid=(1,),
-            in_specs=[ANY] * (2 * blocks),
-            out_specs=ANY,
-            scratch_shapes=[
-                pltpu.VMEM(shape, bf16),
-                pltpu.SemaphoreType.DMA((2 * blocks + 1,)),
-            ],
+        functools.partial(project_back_kernel, shares, blocks, wide // 4),
+        out_shape=(
+            jax.ShapeDtypeStruct((length, depth), bf16),
+            jax.ShapeDtypeStruct((length, ranks), bf16),
+            jax.ShapeDtypeStruct((blocks, ranks, wide), f32),
         ),
-        cost_estimate=pl.CostEstimate(flops=0, bytes_accessed=2 * size, transcendentals=0),
+        in_specs=[ANY] + [WHOLE] * 8,
+        out_specs=(WHOLE,) * 3,
+        scratch_shapes=[
+            pltpu.VMEM((blocks, depth, wide), bf16),
+            pltpu.SemaphoreType.DMA((blocks,)),
+        ],
+        cost_estimate=pl.CostEstimate(
+            flops=2 * length * depth * blocks * wide,
+            bytes_accessed=2 * depth * blocks * wide + 8 * length * depth,
+            transcendentals=0,
+        ),
         compiler_params=pltpu.CompilerParams(vmem_limit_bytes=VMEM_LIMIT),
-        name="out_weight",
-    )(jnp.reshape(core, (1,)).astype(jnp.int32), *mine, *other)
-
-
-def mlp_kernel(units, first, width, *refs):
-    own, oth = refs[:units], refs[units : 2 * units]
-    refs = refs[2 * units :]
-    xm_ref, gz_ref, low_ref, bu_ref = refs[:4]
-    refs = refs[4:]
+        name="project_back",
+    )(gathered, dq, dk, dv, dgate, tail, wf, low, up)
+
+
+def out_kernel(shares, ny, nx, cols, start, gathered, base_ref, merged_ref, out_ref, wbuf, sem):
+    for b in range(ny * nx):
+        fetch_rows(gathered, wbuf, sem, shares, b, (start,))
+    out_ref[...] = base_ref[...]
+    for b in range(ny * nx):
+        wait_rows(wbuf, sem, b)
+        at = (b % nx * ny + b // nx) * cols
+        out_ref[...] += mm(merged_ref[:, at : at + cols], wbuf[b, :, :cols], ((1,), (1,)))
+
+
+def out_back_kernel(shares, ny, nx, cols, start, gathered, grad_ref, low_ref, up_ref, out_ref, wbuf, sem):
+    for b in range(ny * nx):
+        fetch_rows(gathered, wbuf, sem, shares, b, (start,))
+    for b in range(ny * nx):
+        wait_rows(wbuf, sem, b)
+        at = (b % nx * ny + b // nx) * cols
+        out = mm(grad_ref[...], wbuf[b, :, :cols], ((1,), (0,)))
+        out = out + mm(low_ref[...], up_ref[:, at : at + cols], ((1,), (0,)))
+        out_ref[:, at : at + cols] = out.astype(bf16)
+
+
+def out_call(kernel, sizes, start, gathered, operands, out_shape, name):
+    ny, nx, cols = sizes
+    shares, blocks, part, total = gathered.shape
+    depth = shares * part
+    return pl.pallas_call(
+        functools.partial(kernel, shares, ny, nx, cols, start),
+        out_shape=out_shape,
+        in_specs=[ANY] + [WHOLE] * len(operands),
+        out_specs=WHOLE,
+        scratch_shapes=[
+            pltpu.VMEM((blocks, depth, total - start), bf16),
+            pltpu.SemaphoreType.DMA((blocks,)),
+        ],
+        cost_estimate=pl.CostEstimate(
+            flops=2 * out_shape.shape[0] * depth * blocks * cols,
+            bytes_accessed=2 * depth * blocks * cols + 8 * out_shape.shape[0] * depth,
+            transcendentals=0,
+        ),
+        compiler_params=pltpu.CompilerParams(vmem_limit_bytes=VMEM_LIMIT),
+        name=name,
+    )(gathered, *operands)
+
+
+def mlp_kernel(shares, units, first, width, *refs):
+    gathered, xm_ref, gz_ref, low_ref, bu_ref = refs[:5]
+    refs = refs[5:]
     if not first:
         prior, refs = refs[:3], refs[3:]
     out_ref, dx_ref, small_ref, grad_ref, wbuf, sem = refs
     for u in range(units):
-        for half, source in enumerate((own[u], oth[u])):
-            pltpu.make_async_copy(
-                source, wbuf.at[u, :, :, pl.ds(half * width, width)], sem.at[u, half]
-            ).start()
+        fetch_rows(gathered, wbuf, sem, shares, u, (0, width, 2 * width))
     if first:
         out_ref[...] = jnp.zeros_like(out_ref)
         dx_ref[...] = jnp.zeros_like(dx_ref)
@@ -173,9 +242,7 @@
     low_e, low_u, low_d = (jnp.where(lane == i, low_all, zero) for i in range(3))
 
     def step(u, carry):
-        for half in range(2):
-            spot = wbuf.at[u, :, :, pl.ds(half * width, width)]
-            pltpu.make_async_copy(spot, spot, sem.at[u, half]).wait()
+        wait_rows(wbuf, sem, u)
         bu = bu_ref[u]
         gate = mm(xm_ref[...], wbuf[u, 0], ((1,), (0,))) + mm(low_e, bu, ((1,), (0,)))
         up = mm(xm_ref[...], wbuf[u, 1], ((1,), (0,))) + mm(low_u, bu, ((1,), (0,)))
@@ -201,35 +268,35 @@
     lax.fori_loop(0, units, step, 0)
 
 
-def mlp_call(own, oth, xm, gz, low, bu, prior):
-    units = len(own)
-    three, depth, width = own[0].shape
-    rows = xm.shape[0]
+def mlp_call(gathered, xm, gz, low, bu, prior):
+    shares, units = gathered.shape[:2]
+    rows, depth = xm.shape
+    width = bu.shape[2]
     first = prior is None
     lanes = low.shape[1]
-    flops = units * 2 * rows * depth * 2 * width * 6
+    flops = units * 2 * rows * depth * width * 6
     return pl.pallas_call(
-        functools.partial(mlp_kernel, units, first, width),
+        functools.partial(mlp_kernel, shares, units, first, width),
         out_shape=(
             jax.ShapeDtypeStruct((rows, depth), f32),
             jax.ShapeDtypeStruct((rows, depth), f32),
             jax.ShapeDtypeStruct((rows, lanes), f32),
-            jax.ShapeDtypeStruct((units, lanes, 2 * width), bf16),
+            jax.ShapeDtypeStruct((units, lanes, width), bf16),
         ),
-        in_specs=[ANY] * (2 * units) + [WHOLE] * (4 + (0 if first else 3)),
+        in_specs=[ANY] + [WHOLE] * (4 + (0 if first else 3)),
         out_specs=(WHOLE,) * 4,
         scratch_shapes=[
-            pltpu.VMEM((units, three, depth, 2 * width), bf16),
-            pltpu.SemaphoreType.DMA((units, 2)),
+            pltpu.VMEM((units, 3, depth, width), bf16),
+            pltpu.SemaphoreType.DMA((units,)),
         ],
         cost_estimate=pl.CostEstimate(
             flops=flops,
-            bytes_accessed=units * 3 * depth * 2 * width * 2 + rows * depth * 20,
-            transcendentals=units * rows * 2 * width,
+            bytes_accessed=units * 3 * depth * width * 2 + rows * depth * 20,
+            transcendentals=units * rows * width,
         ),
         compiler_params=pltpu.CompilerParams(vmem_limit_bytes=VMEM_LIMIT),
         name="feed_forward",
-    )(*own, *oth, xm, gz, low, bu, *(() if first else prior))
+    )(gathered, xm, gz, low, bu, *(() if first else prior))
 
 
 def decay_lanes(cum, negate):
@@ -270,14 +337,14 @@
 def attend_kernel(length, starts_ref, q_ref, k_ref, v_ref, gate_ref, cum_ref, y_ref, o_ref, lse_ref, keys):
     starts = [starts_ref[i] for i in range(PIECES)]
     cum = cum_ref[...]
-    keys[:, :LANES] = k_ref[0]
+    keys[:, :LANES] = k_ref[...]
     keys[:, LANES:] = decay_lanes(cum, True)
-    values = v_ref[0].astype(bf16)
+    values = v_ref[...]
     for i in range(length // BLOCK):
         low, top = block_ranges(i, BLOCK, length)
         rows = slice(low, low + BLOCK)
         lane = lax.broadcasted_iota(jnp.int32, (BLOCK, LANES), 1)
-        queries = q_ref[0, rows, :] * jnp.asarray(HEAD**-0.5, bf16)
+        queries = q_ref[rows, :] * jnp.asarray(HEAD**-0.5, bf16)
         aug = decay_lanes(cum_ref[rows, :], False)
         row = low + lax.broadcasted_iota(jnp.int32, (BLOCK, 1), 0)
         col = low + lax.broadcasted_iota(jnp.int32, (1, top - low), 1)
@@ -307,7 +374,7 @@
         out = jnp.where(lane < HEAD, mixed[0], mixed[1])
         o_ref[rows, :] = out
         lse_ref[rows, :] = jnp.where(lane < HEAD, lse[0], lse[1])
-        y_ref[rows, :] = (out * jax.nn.sigmoid(gate_ref[0, rows, :])).astype(bf16)
+        y_ref[rows, :] = (out * jax.nn.sigmoid(gate_ref[rows, :])).astype(bf16)
 
 
 def prefetch_call(kernel, grid, in_specs, out_specs, out_shape, scratch, cost, name, scalars):
@@ -327,24 +394,15 @@
     )
 
 
-def attend(scalars, qk, vg, cum):
-    _, length, width = qk.shape
+def attend(scalars, q, k, v, gate, cum):
+    length, width = q.shape
     pairs = width // LANES
-    block = (1, length, LANES)
     flat = pl.BlockSpec((length, LANES), lambda p, s: (0, p))
-    first = lambda p, s: (s[PIECES], 0, p)
-    second = lambda p, s: (1 - s[PIECES], 0, p)
     area = length * length * pairs * 2
     return prefetch_call(
         functools.partial(attend_kernel, length),
         (pairs,),
-        [
-            pl.BlockSpec(block, first),
-            pl.BlockSpec(block, second),
-            pl.BlockSpec(block, first),
-            pl.BlockSpec(block, second),
-            flat,
-        ],
+        [flat] * 5,
         [flat, flat, flat],
         (
             jax.ShapeDtypeStruct((length, width), bf16),
@@ -357,7 +415,7 @@
         ),
         "attend",
         scalars,
-    )(scalars, qk, qk, vg, vg, cum)
+    )(scalars, q, k, v, gate, cum)
 
 
 def attend_back_kernel(
@@ -367,22 +425,22 @@
     starts = [starts_ref[i] for i in range(PIECES)]
     lane_all = lax.broadcasted_iota(jnp.int32, (length, LANES), 1)
     spot_all = lane_all % HEAD
-    keys[:, :LANES] = k_ref[0]
+    keys[:, :LANES] = k_ref[...]
     keys[:, LANES:] = jnp.where(
         (spot_all >= 6) & (spot_all < 9), jnp.asarray(1.0, bf16), decay_lanes(cum_ref[...], True)
     )
     for h in range(2):
-        summed[h] = jnp.where(lane_all // HEAD == h, k_ref[0], jnp.asarray(1.0, bf16))
-    vals[...] = v_ref[0].astype(bf16)
+        summed[h] = jnp.where(lane_all // HEAD == h, k_ref[...], jnp.asarray(1.0, bf16))
+    vals[...] = v_ref[...]
     dkeys[...] = jnp.zeros_like(dkeys)
     dvals[...] = jnp.zeros_like(dvals)
     for i in range(length // BLOCK):
         low, top = block_ranges(i, BLOCK, length)
         rows = slice(low, low + BLOCK)
         lane = lax.broadcasted_iota(jnp.int32, (BLOCK, LANES), 1)
-        queries = q_ref[0, rows, :] * jnp.asarray(HEAD**-0.5, bf16)
+        queries = q_ref[rows, :] * jnp.asarray(HEAD**-0.5, bf16)
         aug = decay_lanes(cum_ref[rows, :], False)
-        gate = jax.nn.sigmoid(gate_ref[0, rows, :])
+        gate = jax.nn.sigmoid(gate_ref[rows, :])
         mixed = o_ref[rows, :]
         dy = dy_ref[rows, :].astype(f32)
         dmix = (dy * gate).astype(bf16)
@@ -437,28 +495,16 @@
     dcum_ref[...] = dcol[...] - jnp.where(lane_all < HEAD, cols[:, 0:1], cols[:, HEAD : HEAD + 1])
 
 
-def attend_back(scalars, qk, vg, cum, mixed, lse, dy):
-    _, length, width = qk.shape
+def attend_back(scalars, q, k, v, gate, cum, mixed, lse, dy):
+    length, width = q.shape
     pairs = width // LANES
-    block = (1, length, LANES)
     flat = pl.BlockSpec((length, LANES), lambda p, s: (0, p))
-    first = lambda p, s: (s[PIECES], 0, p)
-    second = lambda p, s: (1 - s[PIECES], 0, p)
     area = length * length * pairs * 2
     out = jax.ShapeDtypeStruct((length, width), bf16)
     return prefetch_call(
         functools.partial(attend_back_kernel, length),
         (pairs,),
-        [
-            pl.BlockSpec(block, first),
-            pl.BlockSpec(block, second),
-            pl.BlockSpec(block, first),
-            pl.BlockSpec(block, second),
-            flat,
-            flat,
-            flat,
-            flat,
-        ],
+        [flat] * 8,
         [flat] * 5,
         (out, out, out, out, jax.ShapeDtypeStruct((length, width), f32)),
         [
@@ -474,7 +520,7 @@
         ),
         "attend_back",
         scalars,
-    )(scalars, qk, qk, vg, vg, cum, mixed, lse, dy)
+    )(scalars, q, k, v, gate, cum, mixed, lse, dy)
 
 
 def norm_scale(hidden):
@@ -543,62 +589,23 @@
     seq_of = jnp.broadcast_to(ids_all[:, :, None], (n_fsdp, ny, nx)).reshape(count)
     seq_hot = (seq_of[:, None] == jnp.arange(adapters)[None, :]).astype(bf16)
 
-    def z_gather(value, axis):
-        return assemble([shift(value, "z", nz, d) if d else value for d in range(nz)], z, axis)
-
-    def core_split(half0, half1):
-        keep, send = jnp.where(c == 0, half0, half1), jnp.where(c == 0, half1, half0)
-        got = shift(send, "c", 2, 1)
-        axis = keep.ndim - 2
-        return jnp.where(
-            c == 0, jnp.concatenate([keep, got], axis), jnp.concatenate([got, keep], axis)
-        )
-
-    def other_core(value):
-        return shift(value, "c", 2, 1)
-
-    w4 = w_in[0]
-    half0 = jnp.stack([w4[:, 0], w4[:, 2]])
-    half1 = jnp.stack([w4[:, 1], w4[:, 3]])
-    w4 = core_split(half0, half1)
-    chunks = []
-    for j in range(2):
-        mine = z_gather(w4[j], 0)
-        mine = [shift(mine, "y", ny, d) if d else mine for d in range(ny)]
-        chunks.append((mine, [other_core(piece) for piece in mine]))
-
-    wo = jnp.swapaxes(w_out[0], 0, 1)
-    wo = z_gather(wo[None], 0)
-    wo_mine = {}
-    for dx in range(nx):
-        moved = shift(wo, "x", nx, dx) if dx else wo
-        for dy in range(ny):
-            wo_mine[dx, dy] = shift(moved, "y", ny, dy) if dy else moved
-    wo_keys = [(dx, dy) for dx in range(nx) for dy in range(ny)]
-    wo_mine = [wo_mine[key] for key in wo_keys]
-    wo_all = out_weight(wo_mine, [other_core(piece) for piece in wo_mine], c)
-    wo_all = wo_all.reshape(depth, n_tp * cols_t)
-
-    w3 = jnp.stack([w_gate_up[0][:, 0], w_gate_up[0][:, 1], jnp.swapaxes(w_down[0], 0, 1)])
-    w3 = core_split(w3[..., : ff_t // 2], w3[..., ff_t // 2 :])
-    n_chunk = max(1, ff_t // 2 // LANES)
-    width = ff_t // 2 // n_chunk
-    ff_units = []
+    tokens_all = in_order(
+        [shift(tokens_in, "x", nx, d) if d else tokens_in for d in range(nx)], x, nx
+    )
+    w_all = lax.all_gather(w_in[0].reshape(d_fsdp, 4 * cols_t), ("z", "c", "y"))
+    w_all = w_all.reshape(n_fsdp, ny, d_fsdp, 4 * cols_t)
+    n_chunk = max(1, ff_t // (2 * BLOCK))
+    width = ff_t // n_chunk
+    w_gate, w_up = w_gate_up[0][:, 0], w_gate_up[0][:, 1]
+    w_down_t, w_out_t = jnp.swapaxes(w_down[0], 0, 1), jnp.swapaxes(w_out[0], 0, 1)
+    w_out_t = jnp.pad(w_out_t, ((0, 0), (0, -cols_t % LANES)))
+    ff_chunks = []
     for k in range(n_chunk):
-        mine = z_gather(w3[..., k * width : (k + 1) * width], 1)
-        placed = {}
-        if k % 2 == 0:
-            for dx in range(nx):
-                moved = shift(mine, "x", nx, dx) if dx else mine
-                for dy in range(ny):
-                    placed[dy, dx] = shift(moved, "y", ny, dy) if dy else moved
-        else:
-            for dy in range(ny):
-                moved = shift(mine, "y", ny, dy) if dy else mine
-                for dx in range(nx):
-                    placed[dy, dx] = shift(moved, "x", nx, dx) if dx else moved
-        order = [placed[dy, dx] for dy in range(ny) for dx in range(nx)]
-        ff_units.append((order, [other_core(piece) for piece in order]))
+        piece = [part[:, k * width : (k + 1) * width] for part in (w_gate, w_up, w_down_t)]
+        piece = jnp.concatenate(piece + ([] if k else [w_out_t]), axis=1)
+        piece = lax.all_gather(piece, everyone)
+        ff_chunks.append(piece.reshape(n_fsdp, n_tp, d_fsdp, piece.shape[-1]))
+    out_sizes, out_start = (ny, nx, cols_t), 3 * width
 
     sub_c, sub_f = cols_t // n_fsdp, ff_t // n_fsdp
     spread = jnp.concatenate(
@@ -638,54 +645,50 @@
     in_a, mlp_a = map_a[:, : 5 * RANK], map_a[:, 5 * RANK : 7 * RANK]
     out_b, down_b = map_a[:, 7 * RANK : 8 * RANK], map_a[:, 8 * RANK :]
 
-    share = n_fsdp // 2
-    r = jnp.arange(count)
-    r_c, r_s = r // (share * n_tp), (r // n_tp) % share
-    r_y, r_x = (r // nx) % ny, r % nx
-    r_true = (((c - r_c) % 2) * share + r_s) * n_tp + ((y - r_y) % ny) * nx + (x - r_x) % nx
-    reorder = (r_true[:, None] == r[None, :]).astype(bf16)
-    map_b = mm(reorder, chosen[:, n_a:], ((1,), (0,))).astype(bf16)
-    map_b = map_b.reshape(2, share, ny, nx, RANK, n_cols)
+    map_b = chosen[:, n_a:].reshape(n_fsdp, ny, nx, RANK, n_cols)
     cut_b = [4 * sub_c, sub_c, 2 * sub_f, sub_f]
     at, pieces_b = 0, []
     for cut in cut_b:
         pieces_b.append(map_b[..., at : at + cut])
         at += cut
-    in_b = pieces_b[0][:, :, :, 0].reshape(2, share, ny, RANK, 4, sub_c)
-    half_order_y = in_b.transpose(4, 3, 2, 0, 1, 5)
-    in_b = jnp.where(c == 0, half_order_y, jnp.flip(half_order_y, 3)).reshape(4, RANK, ny * cols_t)
-    out_a = pieces_b[1].transpose(4, 3, 2, 0, 1, 5)
-    out_a = jnp.where(c == 0, out_a, jnp.flip(out_a, 3)).reshape(RANK, n_tp * cols_t)
-    per = share // n_chunk
+    in_b = lax.dynamic_index_in_dim(pieces_b[0], x, 2, keepdims=False)
+    in_b = in_b.reshape(n_fsdp, ny, RANK, 4, sub_c).transpose(1, 3, 2, 0, 4)
+    in_b = in_b.reshape(ny, 4 * RANK, 1, cols_t)
+    own_rank = (jnp.arange(4 * RANK)[:, None] // RANK) == jnp.arange(4)[None, :]
+    up_in = jnp.where(own_rank[None, :, :, None], in_b, jnp.zeros_like(in_b))
+    up_in = up_in.reshape(ny, 4 * RANK, 4 * cols_t)
+    out_a = pieces_b[1].transpose(3, 2, 1, 0, 4).reshape(RANK, n_tp * cols_t)
+    per = n_fsdp // n_chunk
     gu_b = (
         pieces_b[2]
-        .reshape(2, n_chunk, per, ny, nx, RANK, 2, sub_f)
-        .transpose(1, 3, 4, 6, 5, 0, 2, 7)
-        .reshape(n_chunk, n_tp, 2 * RANK, 2 * width)
+        .reshape(n_chunk, per, ny, nx, RANK, 2, sub_f)
+        .transpose(0, 2, 3, 5, 4, 1, 6)
+        .reshape(n_chunk, n_tp, 2 * RANK, width)
     )
     down_a = (
         pieces_b[3]
-        .reshape(2, n_chunk, per, ny, nx, RANK, sub_f)
-        .transpose(1, 3, 4, 5, 0, 2, 6)
-        .reshape(n_chunk, n_tp, RANK, 2 * width)
+        .reshape(n_chunk, per, ny, nx, RANK, sub_f)
+        .transpose(0, 2, 3, 4, 1, 5)
+        .reshape(n_chunk, n_tp, RANK, width)
     )
     unit_b = jnp.concatenate([gu_b, down_a, jnp.zeros_like(down_a)], axis=2)
 
     hidden = tokens_in.astype(f32)
     inv_att = norm_scale(hidden)
     normed = (hidden * inv_att * gain_a).astype(bf16)
-    normed_all = in_order([shift(normed, "x", nx, d) if d else normed for d in range(nx)], x, nx)
+    hidden_all = tokens_all.astype(f32)
+    normed_all = (hidden_all * norm_scale(hidden_all) * gain_a).astype(bf16)
     low_in = mm(normed_all, in_a, ((1,), (0,))).astype(bf16)
-    la = [low_in[:, j * RANK : (j + 1) * RANK] for j in range(5)]
+    la, la_forget = low_in[:, : 4 * RANK], low_in[:, 4 * RANK :]
     local_heads = ny * heads_t
     lh = jnp.arange(local_heads)
-    true_head = (((y - lh // heads_t) % ny) * nx + x) * heads_t + lh % heads_t
+    true_head = ((lh // heads_t) * nx + x) * heads_t + lh % heads_t
     head_pick = (jnp.arange(n_tp * heads_t)[:, None] == true_head[None, :]).astype(bf16)
     wf = mm(forget_w, head_pick, ((1,), (0,))).astype(bf16)
     bf = mm(forget_b, head_pick, ((1,), (0,))).astype(bf16)
     bf = lax.dynamic_slice_in_dim(bf, my_id * RANK, RANK, 0)
     bias = mm(forget_bias, head_pick, ((1,), (0,)))
-    logits = mm(normed_all, wf, ((1,), (0,))) + mm(la[4], bf, ((1,), (0,))) + bias
+    logits = mm(normed_all, wf, ((1,), (0,))) + mm(la_forget, bf, ((1,), (0,))) + bias
     log_gate = -jnp.log1p(jnp.exp(-logits))
     order = jnp.arange(length)
     earlier = (order[None, :] <= order[:, None]).astype(bf16)
@@ -693,40 +696,31 @@
     cum = cum[:, :local_heads] + cum[:, local_heads : 2 * local_heads] + cum[:, 2 * local_heads :]
     cum = jnp.repeat(cum, HEAD, axis=1)
 
-    def core_pick(first, second):
-        return jnp.where(c == 0, first, second), jnp.where(c == 0, second, first)
-
-    def project(j, out_type):
-        mine, other = chunks[j]
-        la_pair = core_pick(la[2 * j], la[2 * j + 1])
-        in_b_pair = core_pick(in_b[2 * j], in_b[2 * j + 1])
-        out = []
-        for pieces, low, up in zip((mine, other), la_pair, in_b_pair):
-            weight = jnp.concatenate(pieces, 1)
-            out.append(
-                (mm(normed_all, weight, ((1,), (0,))) + mm(low, up, ((1,), (0,)))).astype(out_type)
-            )
-        return jnp.stack(out)
-
-    qk = project(0, bf16)
-    vg = project(1, f32)
+    q, k, v, gate = project(w_all, normed_all, la, up_in)
     my_starts = lax.dynamic_index_in_dim(piece_starts, y, 0, keepdims=False)
-    scalars = jnp.concatenate([my_starts, c[None].astype(jnp.int32)])
-    merged, mixed, lse = attend(scalars, qk, vg, cum)
+    merged, mixed, lse = attend(my_starts, q, k, v, gate, cum)
 
     def row_block(value, index):
         return lax.dynamic_slice_in_dim(value, index * rows, rows, 0)
 
-    merged_full = jnp.concatenate(
+    merged_full = in_order(
         [
             shift(row_block(merged, (x + d) % nx), "x", nx, d) if d else row_block(merged, x)
             for d in range(nx)
         ],
-        axis=1,
+        x,
+        nx,
+        1,
     )
     low_out = mm(merged_full, out_a, ((1,), (1,))).astype(bf16)
-    hidden1 = (
-        hidden + mm(merged_full, wo_all, ((1,), (1,))) + mm(low_out, out_b, ((1,), (1,)))
+    hidden1 = out_call(
+        out_kernel,
+        out_sizes,
+        out_start,
+        ff_chunks[0],
+        (hidden + mm(low_out, out_b, ((1,), (1,))), merged_full),
+        jax.ShapeDtypeStruct((rows, depth), f32),
+        "out_project",
     )
 
     inv_mlp = norm_scale(hidden1)
@@ -735,9 +729,8 @@
     grad_down = mm(cotangent, down_b, ((1,), (0,))).astype(bf16)
     low_all = jnp.concatenate([low_m, grad_down, jnp.zeros_like(grad_down)], axis=1)
     state, unit_grads = None, []
-    for k in range(n_chunk):
-        own, oth = ff_units[k]
-        *state, unit_grad = mlp_call(own, oth, normed_m, cotangent, low_all, unit_b[k], state)
+    for i in range(n_chunk):
+        *state, unit_grad = mlp_call(ff_chunks[i], normed_m, cotangent, low_all, unit_b[i], state)
         unit_grads.append(unit_grad)
     ff_out, grad_m, small_m = state
     low_down = small_m[:, 2 * RANK : 3 * RANK].astype(bf16)
@@ -748,38 +741,33 @@
 
     grad_y = grad1.astype(bf16)
     grad_low_out = mm(grad_y, out_b, ((1,), (0,))).astype(bf16)
-    grad_merged = (
-        mm(grad_y, wo_all, ((1,), (0,))) + mm(grad_low_out, out_a, ((1,), (0,)))
-    ).astype(bf16)
+    grad_merged = out_call(
+        out_back_kernel,
+        out_sizes,
+        out_start,
+        ff_chunks[0],
+        (grad_y, grad_low_out, out_a),
+        jax.ShapeDtypeStruct((rows, n_tp * cols_t), bf16),
+        "out_project_back",
+    )
     block = ny * cols_t
     grad_rows = []
     for d in range(nx):
-        part = grad_merged[:, d * block : (d + 1) * block]
-        grad_rows.append(shift(part, "x", nx, -d) if d else part)
-    grad_rows = [grad_rows[-d % nx] for d in range(nx)]
+        part = lax.dynamic_slice_in_dim(grad_merged, ((x + d) % nx) * block, block, 1)
+        grad_rows.append(shift(part, "x", nx, d) if d else part)
     grad_rows = in_order(grad_rows, x, nx)
-    dq, dk, dv, dgate, dcum = attend_back(scalars, qk, vg, cum, mixed, lse, grad_rows)
+    dq, dk, dv, dgate, dcum = attend_back(my_starts, q, k, v, gate, cum, mixed, lse, grad_rows)
     dcum = dcum[:, ::HEAD]
     dlog = mm(earlier, split_columns(dcum), ((0,), (0,)))
     dlog = dlog[:, :local_heads] + dlog[:, local_heads : 2 * local_heads] + dlog[:, 2 * local_heads :]
     dforget = (dlog * jax.nn.sigmoid(-logits)).astype(bf16)
 
-    grad_x, grad_la, grad_in_b = 0.0, [], []
-    pair_grads = ((dq, dk), (dv, dgate))
-    for j in range(2):
-        mine, other = chunks[j]
-        for pieces, grad in zip((mine, other), core_pick(*pair_grads[j])):
-            weight = jnp.concatenate(pieces, 1)
-            grad_x = grad_x + mm(grad, weight, ((1,), (1,)))
-        for i in range(2):
-            grad = pair_grads[j][i]
-            grad_la.append(mm(grad, in_b[2 * j + i], ((1,), (1,))))
-            grad_in_b.append(mm(la[2 * j + i], grad, ((0,), (0,))))
-    grad_x = grad_x + mm(dforget, wf, ((1,), (1,)))
-    grad_la.append(mm(dforget, bf, ((1,), (1,))))
-    grad_la = jnp.concatenate(grad_la, 1).astype(bf16)
-    grad_forget_b = mm(la[4], dforget, ((0,), (0,)))
-    grad_x = grad_x.astype(bf16)
+    lane_pad = ((0, 0), (0, -local_heads % LANES))
+    grad_x, grad_la, grad_up = project_back(
+        w_all, dq, dk, dv, dgate, jnp.pad(dforget, lane_pad), jnp.pad(wf, lane_pad), la, up_in
+    )
+    grad_la = jnp.concatenate([grad_la, mm(dforget, bf, ((1,), (1,))).astype(bf16)], 1)
+    grad_forget_b = mm(la_forget, dforget, ((0,), (0,)))
 
     def scatter_rows(value):
         total = row_block(value, x).astype(f32)
@@ -800,28 +788,28 @@
         ],
         axis=1,
     ).astype(bf16)
-    g_in_b = jnp.stack(grad_in_b).astype(bf16).reshape(4, RANK, ny, 2, share, sub_c)
-    g_in_b = jnp.where(c == 0, g_in_b, jnp.flip(g_in_b, 3))
-    g_in_b = g_in_b.transpose(3, 4, 2, 1, 0, 5).reshape(2, share, ny, 1, RANK, 4 * sub_c)
-    g_in_b = jnp.pad(g_in_b, ((0, 0), (0, 0), (0, 0), (0, nx - 1), (0, 0), (0, 0)))
+    g_in_b = grad_up.astype(bf16).reshape(ny, 4, RANK, 4, cols_t)
+    g_in_b = jnp.stack([g_in_b[:, i, :, i] for i in range(4)]).reshape(4, ny, RANK, n_fsdp, sub_c)
+    g_in_b = g_in_b.transpose(3, 1, 2, 0, 4).reshape(n_fsdp, ny, 1, RANK, 4 * sub_c)
+    own_x = (jnp.arange(nx) == x)[None, None, :, None, None]
+    g_in_b = jnp.where(own_x, g_in_b, jnp.zeros_like(g_in_b))
     g_out_a = mm(grad_low_out, merged_full, ((0,), (0,))).astype(bf16)
-    g_out_a = g_out_a.reshape(RANK, nx, ny, 2, share, sub_c)
-    g_out_a = jnp.where(c == 0, g_out_a, jnp.flip(g_out_a, 3)).transpose(3, 4, 2, 1, 0, 5)
+    g_out_a = g_out_a.reshape(RANK, nx, ny, n_fsdp, sub_c).transpose(3, 2, 1, 0, 4)
     g_unit = jnp.stack(unit_grads)
     g_gu_b = (
         g_unit[:, :, : 2 * RANK]
-        .reshape(n_chunk, ny, nx, 2, RANK, 2, per, sub_f)
-        .transpose(5, 0, 6, 1, 2, 4, 3, 7)
-        .reshape(2, share, ny, nx, RANK, 2 * sub_f)
+        .reshape(n_chunk, ny, nx, 2, RANK, per, sub_f)
+        .transpose(0, 5, 1, 2, 4, 3, 6)
+        .reshape(n_fsdp, ny, nx, RANK, 2 * sub_f)
     )
     g_down_a = (
         g_unit[:, :, 2 * RANK : 3 * RANK]
-        .reshape(n_chunk, ny, nx, RANK, 2, per, sub_f)
-        .transpose(4, 0, 5, 1, 2, 3, 6)
-        .reshape(2, share, ny, nx, RANK, sub_f)
+        .reshape(n_chunk, ny, nx, RANK, per, sub_f)
+        .transpose(0, 4, 1, 2, 3, 5)
+        .reshape(n_fsdp, ny, nx, RANK, sub_f)
     )
     part_b = jnp.concatenate([g_in_b, g_out_a, g_gu_b, g_down_a], axis=-1)
-    part_b = mm(reorder, part_b.reshape(count, RANK * n_cols), ((0,), (0,))).astype(bf16)
+    part_b = part_b.reshape(count, RANK * n_cols)
     part_f = mm(grad_forget_b.astype(bf16), head_pick, ((1,), (1,))).astype(bf16)
     part_f = part_f.reshape(RANK, n_tp, heads_t).transpose(1, 0, 2).reshape(1, n_tp, RANK * heads_t)
     part_f = jnp.broadcast_to(part_f, (n_fsdp, n_tp, RANK * heads_t)).reshape(count, RANK * heads_t)

time: 842 us -> 694 us (0.82)
  matrix products: 132 us -> 28.7 us
  starting transfers between devices: 105 us -> 27.7 us
  waiting for transfers between devices: 218 us -> 263 us
  local copies, waits for them, and re-layouts: 132 us -> 96.2 us
  Pallas kernels: 188 us -> 212 us
  between operations: 3.45 us -> 16.2 us
  other arithmetic: 53.6 us -> 44 us
    ppermute x69 -> x5, waiting for transfers between devices: 210 us -> 62.1 us  [shift(): lax.ppermute(value, axis, [(i, (i + step) % size) for i in range(size)])]
    all_gather x0 -> x3, waiting for transfers between devices: none -> 123 us  [the longest x2 123 us: on_device(): piece = lax.all_gather(piece, everyone)]
    dot_general x51 -> x25, matrix products: 132 us -> 28.7 us  [mm(): lax.dot_general(left, right, ((dims[0], dims[1]), ((), ())), preferred_el...]
    ppermute x69 -> x5, starting transfers between devices: 78.3 us -> 6.83 us  [shift(): lax.ppermute(value, axis, [(i, (i + step) % size) for i in range(size)])]
    all_to_all x1, waiting for transfers between devices: 0.01 us -> 38.7 us  [on_device(): chosen = lax.all_to_all(chosen, everyone, 0, 0, tiled=True)]
    pallas_call x14 -> x8, Pallas kernels: 188 us -> 212 us  [the longest x2 64.5 us: mlp_call(): pl.pallas_call(functools.partial(mlp_kernel, shares, units, first, width)...]
    all_to_all x1, waiting for transfers between devices: 4.15 us -> 20.9 us  [on_device(): sent = lax.all_to_all(sent, everyone, 0, 0, tiled=True)]
    all_to_all x1, waiting for transfers between devices: 0.01 us -> 10.7 us  [on_device(): spread = lax.all_to_all(spread, fsdp, 0, 0, tiled=True)]
  transfers between devices with their start and end apart: 74 -> 13, of which waited for: 22 -> 10; matrix products, arithmetic and copies ran while one was open for 29% -> 17% of each run, Pallas kernels for 13% -> 13%
where the time goes in v2:
time: 694 us; the launch traced here: 688 us
  waiting for transfers between devices  263 us (38%)
  Pallas kernels  212 us (31%)
  local copies, waits for them, and re-layouts  96.2 us (14%)
  other arithmetic  44 us (6%)
  matrix products  28.7 us (4%)
  starting transfers between devices  27.7 us (4%)
  between operations  16.2 us (2%)
    all_gather x2, waiting for transfers between devices, on_device(): piece = lax.all_gather(piece, everyone)  123 us
    pallas_call x2, Pallas kernels, mlp_call(): pl.pallas_call(functools.partial(mlp_kernel, shares, units, first, width)...  64.5 us
    ppermute x5, waiting for transfers between devices, shift(): lax.ppermute(value, axis, [(i, (i + step) % size) for i in range(size)])  62.1 us
    pallas_call x1, Pallas kernels, attend_back(): prefetch_call(functools.partial(attend_back_kernel, length), (pairs,), [f...  55.5 us
    all_to_all x1, waiting for transfers between devices, on_device(): chosen = lax.all_to_all(chosen, everyone, 0, 0, tiled=True)  38.7 us
    pallas_call x1, Pallas kernels, attend(): prefetch_call(functools.partial(attend_kernel, length), (pairs,), [flat]...  31.4 us
    dot_general x25, matrix products, mm(): lax.dot_general(left, right, ((dims[0], dims[1]), ((), ())), preferred_el...  28.7 us
    unnamed x160, local copies, waits for them, and re-layouts  27.3 us
  transfers between devices with their start and end apart: 13, of which 10 were waited for; matrix products, arithmetic and copies ran while one was open for 17% of the time, Pallas kernels for 13%

profile of v2, /device:TPU:0, one launch (start us, length us, event | category | flops | bytes accessed | tf_op | source)
XLA Modules:
  0.0 687.6 jit_solution(4004101494173941168)
XLA Ops:
  16.5 7.3 %all-to-all-start = ((bf16[32,2,676]{2,1,0:T(2,128)(2,1)}), bf16[32,2,676]{2,1,0:T(2,128)(2,1)S(1)}, u32[]{:S(2)}, u32[]{:S(2)}) async-start(bf16[32,2,676]{2,1,0:T(2,128)(2,1)} %reshape.418), calls=%async_computation | async-start | bytes 196608 | tf_op jit(solution)/shard_map/all_to_all | solution.py:568
  28.4 5.4 all-to-all-done
  38.4 10.7 %all-to-all-done.1 = bf16[8,16,624]{2,1,0:T(8,128)(2,1)S(1)} async-done(((bf16[8,16,624]{2,1,0:T(8,128)(2,1)}), bf16[8,16,624]{2,1,0:T(8,128)(2,1)S(1)}, u32[]{:S(2)}, u32[]{:S(2)}) %all-to-all-start.1) | async-done | bytes 159776 | tf_op jit(solution)/shard_map/all_to_all | solution.py:625
  71.3 3.7 fusion.3.x_ref
  75.0 38.7 %all-to-all-done.2 = bf16[32,2,8448]{2,1,0:T(2,128)(2,1)} async-done(((bf16[32,2,8448]{2,1,0:T(2,128)(2,1)}), bf16[32,2,8448]{2,1,0:T(2,128)(2,1)}, u32[]{:S(2)}, u32[]{:S(2)}) %all-to-all-start.2) | async-done | bytes 1081376 | tf_op jit(solution)/shard_map/all_to_all | solution.py:643
  113.7 5.8 reshape.421
  140.0 3.6 copy.349.cum_ref
  144.4 19.7 %project.1 = (bf16[1024,768]{1,0:T(8,128)(2,1)}, bf16[1024,768]{1,0:T(8,128)(2,1)}, bf16[1024,768]{1,0:T(8,128)(2,1)}, f32[1024,768]{1,0:T(8,128)}) custom-call(bf16[8,2,192,1536]{3,2,1,0:T(8,128)(2,1)} %bitcast.269, bf16[1024,1536]{1,0:T(8,128)(2,1)} %fusion.3.x_ref, bf16[1024,64]{1,0:T(8,128)(2,1)} %bitcast.222, ...), custom_call_target="tpu_custom_call" | custom-call | flops 9663676416 | bytes 28311552 | tf_op jit(solution)/shard_map/project/pallas_call | solution.py:105
  164.1 31.4 %attend.1 = (bf16[1024,768]{1,0:T(8,128)(2,1)}, f32[1024,768]{1,0:T(8,128)}, f32[1024,768]{1,0:T(8,128)}) custom-call(s32[2]{0:T(128)} %fusion.70.starts_ref, bf16[1024,768]{1,0:T(8,128)(2,1)} %get-tuple-element.34.q_ref, bf16[1024,768]{1,0:T(8,128)(2,1)} %get-tuple-element.35.k_ref, bf16[1024,768]{1,0:T(8,128)(2,1)} %get-tuple-element.36.v_ref, ...), custom_call_target="tpu_custom_call" | custom-call | flops 7549747200 | bytes 20447232 | tf_op jit(solution)/shard_map/attend/pallas_call | solution.py:402
  214.3 21.3 %collective-permute-done.1 = bf16[512,768]{1,0:T(8,128)(2,1)} collective-permute-done((bf16[512,768]{1,0:T(8,128)(2,1)}, bf16[512,768]{1,0:T(8,128)(2,1)}, u32[]{:S(2)}, u32[]{:S(2)}) %collective-permute-start.1) | collective-permute-done | bytes 786464 | tf_op jit(solution)/shard_map/ppermute | solution.py:32
  240.9 44.0 %all-gather.8.cloned.1.call-done = bf16[6144,1920]{1,0:T(8,128)(2,1)} async-done(((bf16[192,1920]{1,0:T(8,128)(2,1)}), bf16[6144,1920]{1,0:T(8,128)(2,1)}) %all-gather.8.cloned.1.call-update) | async-done | bytes 23592976 | tf_op jit(solution)/shard_map/all_gather | solution.py:606
  284.9 9.2 %out_project.1 = f32[512,1536]{1,0:T(8,128)} custom-call(bf16[8,4,192,1920]{3,2,1,0:T(8,128)(2,1)} %bitcast.208, f32[512,1536]{1,0:T(8,128)} %convert_add_fusion.base_ref, bf16[512,1536]{1,0:T(8,128)(2,1)} %copy-done.5), custom_call_target="tpu_custom_call" | custom-call | flops 2415919104 | bytes 11010048 | tf_op jit(solution)/shard_map/out_project/pallas_call | solution.py:204
  300.6 31.3 %feed_forward.2 = (f32[512,1536]{1,0:T(8,128)}, f32[512,1536]{1,0:T(8,128)}, f32[512,64]{1,0:T(8,128)}, bf16[4,64,512]{2,1,0:T(8,128)(2,1)}) custom-call(bf16[8,4,192,1920]{3,2,1,0:T(8,128)(2,1)} %bitcast.209, bf16[512,1536]{1,0:T(8,128)(2,1)} %copy-done.11, bf16[512,1536]{1,0:T(8,128)(2,1)} %refs_2_.3, bf16[512,64]{1,0:T(8,128)(2,1)} %maximum_maximum_fusion.1.refs_3_, ...), custom_call_target="tpu_custom_call" | custom-call | flops 19327352832 | bytes 34603008 | tf_op jit(solution)/shard_map/feed_forward/pallas_call | solution.py:278
  331.9 79.0 %all-gather.10.cloned.1.call-done = bf16[6144,1536]{1,0:T(8,128)(2,1)} async-done(((bf16[192,1536]{1,0:T(8,128)(2,1)}), bf16[6144,1536]{1,0:T(8,128)(2,1)}) %all-gather.10.cloned.1.call-update) | async-done | bytes 18874384 | tf_op jit(solution)/shard_map/all_gather | solution.py:606
  410.9 33.2 %feed_forward.3 = (f32[512,1536]{1,0:T(8,128)}, f32[512,1536]{1,0:T(8,128)}, f32[512,64]{1,0:T(8,128)}, bf16[4,64,512]{2,1,0:T(8,128)(2,1)}) custom-call(bf16[8,4,192,1536]{3,2,1,0:T(8,128)(2,1)} %bitcast.268, bf16[512,1536]{1,0:T(8,128)(2,1)} %copy-done.11, bf16[512,1536]{1,0:T(8,128)(2,1)} %refs_2_.3, bf16[512,64]{1,0:T(8,128)(2,1)} %maximum_maximum_fusion.1.refs_3_, ...), custom_call_target="tpu_custom_call" | custom-call | flops 19327352832 | bytes 34603008 | tf_op jit(solution)/shard_map/feed_forward/pallas_call | solution.py:278
  457.5 8.4 %out_project_back.1 = bf16[512,1536]{1,0:T(8,128)(2,1)} custom-call(bf16[8,4,192,1920]{3,2,1,0:T(8,128)(2,1)} %bitcast.210, bf16[512,1536]{1,0:T(8,128)(2,1)} %copy-done.7, bf16[512,16]{1,0:T(8,128)(2,1)} %convolution_convert_fusion.8.low_ref, bf16[16,1536]{1,0:T(8,128)(2,1)} %reshape.379.up_ref), custom_call_target="tpu_custom_call" | custom-call | flops 2415919104 | bytes 11010048 | tf_op jit(solution)/shard_map/out_project_back/pallas_call | solution.py:204
  471.5 15.9 %collective-permute-done.2 = bf16[512,768]{1,0:T(8,128)(2,1)S(1)} collective-permute-done((bf16[512,768]{1,0:T(8,128)(2,1)S(1)}, bf16[512,768]{1,0:T(8,128)(2,1)S(1)}, u32[]{:S(2)}, u32[]{:S(2)}) %collective-permute-start.2) | collective-permute-done | bytes 786464 | tf_op jit(solution)/shard_map/ppermute | solution.py:32
  489.2 55.5 %attend_back.1 = (bf16[1024,768]{1,0:T(8,128)(2,1)}, bf16[1024,768]{1,0:T(8,128)(2,1)}, bf16[1024,768]{1,0:T(8,128)(2,1)}, bf16[1024,768]{1,0:T(8,128)(2,1)}, f32[1024,768]{1,0:T(8,128)}) custom-call(s32[2]{0:T(128)} %fusion.70.starts_ref, bf16[1024,768]{1,0:T(8,128)(2,1)} %get-tuple-element.34.q_ref, bf16[1024,768]{1,0:T(8,128)(2,1)} %get-tuple-element.35.k_ref, ...), custom_call_target="tpu_custom_call" | custom-call | flops 18874368000 | bytes 26738688 | tf_op jit(solution)/shard_map/attend_back/pallas_call | solution.py:504
  544.7 4.5 slice.205
  551.8 22.9 %project_back.1 = (bf16[1024,1536]{1,0:T(8,128)(2,1)}, bf16[1024,64]{1,0:T(8,128)(2,1)}, f32[2,64,1536]{2,1,0:T(8,128)}) custom-call(bf16[8,2,192,1536]{3,2,1,0:T(8,128)(2,1)} %bitcast.270, bf16[1024,768]{1,0:T(8,128)(2,1)} %get-tuple-element.47.dq_ref, bf16[1024,768]{1,0:T(8,128)(2,1)} %get-tuple-element.48.dk_ref, ...), custom_call_target="tpu_custom_call" | custom-call | flops 9663676416 | bytes 22020096 | tf_op jit(solution)/shard_map/project_back/pallas_call | solution.py:156
  591.2 24.9 %collective-permute-done.4 = bf16[512,80]{1,0:T(8,128)(2,1)} collective-permute-done((bf16[512,80]{1,0:T(8,128)(2,1)}, bf16[512,80]{1,0:T(8,128)(2,1)}, u32[]{:S(2)}, u32[]{:S(2)}) %collective-permute-start.4) | collective-permute-done | bytes 81952 | tf_op jit(solution)/shard_map/ppermute | solution.py:32
  617.2 4.7 fusion.7
  636.1 6.6 fusion.10
  642.6 20.9 %all-to-all-done.3 = bf16[32,2,8496]{2,1,0:T(2,128)(2,1)S(1)} async-done(((bf16[32,2,8496]{2,1,0:T(2,128)(2,1)}), bf16[32,2,8496]{2,1,0:T(2,128)(2,1)S(1)}, u32[]{:S(2)}, u32[]{:S(2)}) %all-to-all-start.3) | async-done | bytes 1087520 | tf_op jit(solution)/shard_map/all_to_all | solution.py:817
  (379 shorter events, 162.8 us)
Async XLA Ops:
  7.2 50.6 %copy-start = (s32[2,2]{1,0:T(2,128)S(1)}, s32[2,2]{1,0:T(2,128)}, u32[]{:S(2)}) copy-start(s32[2,2]{1,0:T(2,128)} %param.23) | copy-start | bytes 52
  7.2 137.2 %all-gather.6.cloned.1.call-start = ((), (), s32[]{:S(2)}) async-start(), calls=%async_computation.5 | async-start | bytes 10027008 | tf_op jit(solution)/shard_map/all_gather | solution.py:595
  9.6 275.3 %all-gather.8.cloned.1.call-start = ((), (), s32[]{:S(2)}) async-start(), calls=%async_computation.6 | async-start | bytes 24330240 | tf_op jit(solution)/shard_map/all_gather | solution.py:606
  11.3 16.5 %copy-start.51 = (bf16[1,128,48]{1,2,0:T(8,128)(2,1)S(1)}, bf16[1,128,48]{1,2,0:T(8,128)(2,1)}, u32[]{:S(2)}) copy-start(bf16[1,128,48]{1,2,0:T(8,128)(2,1)} %param.41) | copy-start | bytes 36868
  11.3 16.7 %copy-start.48 = (bf16[1,48,256]{2,1,0:T(8,128)(2,1)S(1)}, bf16[1,48,256]{2,1,0:T(8,128)(2,1)}, u32[]{:S(2)}) copy-start(bf16[1,48,256]{2,1,0:T(8,128)(2,1)} %param.38) | copy-start | bytes 73732
  11.3 16.8 %copy-start.44 = (bf16[1,48,640]{2,1,0:T(8,128)(2,1)S(1)}, bf16[1,48,640]{2,1,0:T(8,128)(2,1)}, u32[]{:S(2)}) copy-start(bf16[1,48,640]{2,1,0:T(8,128)(2,1)} %param.33) | copy-start | bytes 184324
  12.3 398.6 %all-gather.10.cloned.1.call-start = ((), (), s32[]{:S(2)}) async-start(), calls=%async_computation.7 | async-start | bytes 19464192 | tf_op jit(solution)/shard_map/all_gather | solution.py:606
  16.5 17.3 %all-to-all-start = ((bf16[32,2,676]{2,1,0:T(2,128)(2,1)}), bf16[32,2,676]{2,1,0:T(2,128)(2,1)S(1)}, u32[]{:S(2)}, u32[]{:S(2)}) async-start(bf16[32,2,676]{2,1,0:T(2,128)(2,1)} %reshape.418), calls=%async_computation | async-start | bytes 196608 | tf_op jit(solution)/shard_map/all_to_all | solution.py:568
  23.8 44.9 %collective-permute-start = (bf16[512,1536]{1,0:T(8,128)(2,1)S(1)}, bf16[512,1536]{1,0:T(8,128)(2,1)}, u32[]{:S(2)}, u32[]{:S(2)}) collective-permute-start(bf16[512,1536]{1,0:T(8,128)(2,1)S(1)} %copy-done.3), channel_id=1, source_target_pairs={{0,1},{1,0},{2,3},{3,2},{4,5},{5,4},{6,7},{7,6},{8,9},{9,8},{10,11... | collective-permute-start | bytes 4718600 | tf_op jit(solution)/shard_map/ppermute | solution.py:32
  33.8 15.4 %all-to-all-start.1 = ((bf16[8,16,624]{2,1,0:T(8,128)(2,1)}), bf16[8,16,624]{2,1,0:T(8,128)(2,1)S(1)}, u32[]{:S(2)}, u32[]{:S(2)}) async-start(bf16[8,16,624]{2,1,0:T(8,128)(2,1)} %pad_maximum_fusion.5), calls=%async_computation.1 | async-start | bytes 327680 | tf_op jit(solution)/shard_map/all_to_all | solution.py:625
  54.2 59.6 %all-to-all-start.2 = ((bf16[32,2,8448]{2,1,0:T(2,128)(2,1)}), bf16[32,2,8448]{2,1,0:T(2,128)(2,1)}, u32[]{:S(2)}, u32[]{:S(2)}) async-start(bf16[32,2,8448]{2,1,0:T(2,128)(2,1)} %reshape.420), calls=%async_computation.2 | async-start | bytes 2162688 | tf_op jit(solution)/shard_map/all_to_all | solution.py:643
  68.5 66.6 %copy-start.54 = (f32[12]{0:T(128)}, f32[12]{0:T(128)S(1)}, u32[]{:S(2)}) copy-start(f32[12]{0:T(128)S(1)} %convolution_bitcast_fusion) | copy-start | bytes 148
  68.7 64.4 %copy-start.45 = (bf16[128,12]{1,0:T(8,128)(2,1)}, bf16[128,12]{1,0:T(8,128)(2,1)S(1)}, u32[]{:S(2)}) copy-start(bf16[128,12]{1,0:T(8,128)(2,1)S(1)} %fusion.59) | copy-start | bytes 9220
  198.4 37.3 %collective-permute-start.1 = (bf16[512,768]{1,0:T(8,128)(2,1)}, bf16[512,768]{1,0:T(8,128)(2,1)}, u32[]{:S(2)}, u32[]{:S(2)}) collective-permute-start(bf16[512,768]{1,0:T(8,128)(2,1)} %get-tuple-element.131), channel_id=1, source_target_pairs={{0,1},{1,0},{2,3},{3,2},{4,5},{5,4},{6,7},{7,6},{8,9},{9,8},{10,11... | collective-permute-start | bytes 2359304 | tf_op jit(solution)/shard_map/ppermute | solution.py:32
  213.3 24.8 %copy-start.35 = (bf16[16,1536]{1,0:T(8,128)(2,1)S(1)}, bf16[16,1536]{1,0:T(8,128)(2,1)}, u32[]{:S(2)}) copy-start(bf16[16,1536]{1,0:T(8,128)(2,1)} %reshape.379.up_ref) | copy-start | bytes 147460
  213.5 25.1 %copy-start.14 = (bf16[1536,144]{1,0:T(8,128)(2,1)S(1)}, bf16[1536,144]{1,0:T(8,128)(2,1)}, u32[]{:S(2)}) copy-start(bf16[1536,144]{1,0:T(8,128)(2,1)} %copy-done.13) | copy-start | bytes 1327108
  467.6 19.8 %collective-permute-start.2 = (bf16[512,768]{1,0:T(8,128)(2,1)S(1)}, bf16[512,768]{1,0:T(8,128)(2,1)S(1)}, u32[]{:S(2)}, u32[]{:S(2)}) collective-permute-start(bf16[512,768]{1,0:T(8,128)(2,1)S(1)} %get-tuple-element.129), channel_id=1, source_target_pairs={{0,1},{1,0},{2,3},{3,2},{4,5},{5,4},{6,7},{7,6},{8,9},{9,8},{10,11... | collective-permute-start | bytes 2359304 | tf_op jit(solution)/shard_map/ppermute | solution.py:32
  577.3 39.8 %collective-permute-start.3 = (bf16[512,1536]{1,0:T(8,128)(2,1)}, bf16[512,1536]{1,0:T(8,128)(2,1)}, u32[]{:S(2)}, u32[]{:S(2)}) collective-permute-start(bf16[512,1536]{1,0:T(8,128)(2,1)} %constant_dynamic-slice_fusion), channel_id=1, source_target_pairs={{0,1},{1,0},{2,3},{3,2},{4,5},{5,4},{6,7},{7,6},{8,9},{9,8},{10,11... | collective-permute-start | bytes 4718600 | tf_op jit(solution)/shard_map/ppermute | solution.py:32
  584.4 32.8 %copy-start.4 = (bf16[512,1536]{1,0:T(8,128)(2,1)S(1)}, bf16[512,1536]{1,0:T(8,128)(2,1)}, u32[]{:S(2)}) copy-start(bf16[512,1536]{1,0:T(8,128)(2,1)} %param.21) | copy-start | bytes 4718596
  584.4 32.8 %copy-start.17 = (bf16[1536,144]{1,0:T(8,128)(2,1)S(1)}, bf16[1536,144]{1,0:T(8,128)(2,1)}, u32[]{:S(2)}) copy-start(bf16[1536,144]{1,0:T(8,128)(2,1)} %copy-done.13) | copy-start | bytes 1327108
  586.9 29.2 %collective-permute-start.4 = (bf16[512,80]{1,0:T(8,128)(2,1)}, bf16[512,80]{1,0:T(8,128)(2,1)}, u32[]{:S(2)}, u32[]{:S(2)}) collective-permute-start(bf16[512,80]{1,0:T(8,128)(2,1)} %fusion.43), channel_id=1, source_target_pairs={{0,1},{1,0},{2,3},{3,2},{4,5},{5,4},{6,7},{7,6},{8,9},{9,8},{10,11... | collective-permute-start | bytes 245768 | tf_op jit(solution)/shard_map/ppermute | solution.py:32
  633.0 30.5 %all-to-all-start.3 = ((bf16[32,2,8496]{2,1,0:T(2,128)(2,1)}), bf16[32,2,8496]{2,1,0:T(2,128)(2,1)S(1)}, u32[]{:S(2)}, u32[]{:S(2)}) async-start(bf16[32,2,8496]{2,1,0:T(2,128)(2,1)} %reshape.422), calls=%async_computation.3 | async-start | bytes 2195456 | tf_op jit(solution)/shard_map/all_to_all | solution.py:817
  642.6 22.6 %copy-start.53 = (s32[32]{0:T(128)S(1)}, s32[32]{0:T(128)}, u32[]{:S(2)}) copy-start(s32[32]{0:T(128)} %copy-done.52) | copy-start | bytes 388
  666.7 10.5 %all-to-all-start.4 = ((bf16[8,16,624]{2,1,0:T(8,128)(2,1)}), bf16[8,16,624]{2,1,0:T(8,128)(2,1)S(1)}, u32[]{:S(2)}, u32[]{:S(2)}) async-start(bf16[8,16,624]{2,1,0:T(8,128)(2,1)} %convert_element_type.178), calls=%async_computation.4 | async-start | bytes 327680 | tf_op jit(solution)/shard_map/all_to_all | solution.py:836
  (53 other events, 301.3 us)
Sparse Core Ops, SparseCore 0:
  10.3 110.0 all-gather.5
  123.3 161.5 all-gather.7
  287.8 122.9 all-gather.9

commit v3 on v2

--- a/solution.py
+++ b/solution.py
@@ -62,13 +62,10 @@
     return out
 
 
-def fetch_rows(gathered, buf, sem, shares, index, columns=None):
+def fetch_rows(gathered, buf, sem, shares, index, columns):
     part = gathered.shape[-2]
     for f in range(shares):
         where = pl.ds(f * part, part)
-        if columns is None:
-            pltpu.make_async_copy(gathered.at[f, index], buf.at[index, where], sem.at[index]).start()
-            continue
         for plane, start in enumerate(columns):
             source = gathered.at[f, index, :, pl.ds(start, buf.shape[-1])]
             spot = buf.at[index, plane, where] if len(buf.shape) == 4 else buf.at[index, where]
@@ -79,9 +76,23 @@
     pltpu.make_async_copy(buf.at[index], buf.at[index], sem.at[index]).wait()
 
 
-def project_kernel(shares, blocks, cols, gathered, x_ref, low_ref, up_ref, q_ref, k_ref, v_ref, gate_ref, wbuf, sem):
-    for b in range(blocks):
-        fetch_rows(gathered, wbuf, sem, shares, b)
+def fetch_placed(place, sources, buf, sem):
+    blocks = buf.shape[0]
+    nz, part, _ = sources[0].shape
+    for dy in range(blocks):
+        block = lax.rem(place[2] - dy + blocks, blocks)
+        for dc in range(2):
+            core = lax.rem(place[1] + dc, 2)
+            for dz in range(nz):
+                share = 2 * lax.rem(place[0] - dz + nz, nz) + core
+                spot = buf.at[block, pl.ds(pl.multiple_of(share * part, part), part)]
+                pltpu.make_async_copy(sources[2 * dy + dc].at[dz], spot, sem.at[block]).start()
+
+
+def project_kernel(blocks, cols, place, *refs):
+    sources, refs = refs[: 2 * blocks], refs[2 * blocks :]
+    x_ref, low_ref, up_ref, q_ref, k_ref, v_ref, gate_ref, wbuf, sem = refs
+    fetch_placed(place, sources, wbuf, sem)
     for b in range(blocks):
         wait_rows(wbuf, sem, b)
 
@@ -97,36 +108,53 @@
         lax.fori_loop(0, x_ref.shape[0] // BLOCK, step, 0)
 
 
-def project(gathered, normed, low, up):
-    shares, blocks, part, wide = gathered.shape
-    length, depth = normed.shape
-    cols = wide // 4
-    out = jax.ShapeDtypeStruct((length, blocks * cols), bf16)
+def placed_call(kernel, operands, place, sources, out_shape, flops, moved, name):
+    blocks = len(sources) // 2
+    nz, part, wide = sources[0].shape
     return pl.pallas_call(
-        functools.partial(project_kernel, shares, blocks, cols),
-        out_shape=(out, out, out, jax.ShapeDtypeStruct((length, blocks * cols), f32)),
-        in_specs=[ANY] + [WHOLE] * 3,
-        out_specs=(WHOLE,) * 4,
-        scratch_shapes=[
-            pltpu.VMEM((blocks, depth, wide), bf16),
-            pltpu.SemaphoreType.DMA((blocks,)),
-        ],
+        functools.partial(kernel, blocks, wide // 4),
+        out_shape=out_shape,
+        grid_spec=pltpu.PrefetchScalarGridSpec(
+            num_scalar_prefetch=1,
+            grid=(1,),
+            in_specs=[ANY] * len(sources) + [WHOLE] * len(operands),
+            out_specs=(WHOLE,) * len(out_shape),
+            scratch_shapes=[
+                pltpu.VMEM((blocks, 2 * nz * part, wide), bf16),
+                pltpu.SemaphoreType.DMA((blocks,)),
+            ],
+        ),
         cost_estimate=pl.CostEstimate(
-            flops=2 * length * depth * blocks * wide,
-            bytes_accessed=2 * depth * blocks * wide + 12 * length * depth,
+            flops=flops,
+            bytes_accessed=4 * blocks * nz * part * wide + moved,
             transcendentals=0,
         ),
         compiler_params=pltpu.CompilerParams(vmem_limit_bytes=VMEM_LIMIT),
-        name="project",
-    )(gathered, normed, low, up)
-
-
-def project_back_kernel(
-    shares, blocks, cols, gathered, dq_ref, dk_ref, dv_ref, dgate_ref, tail_ref, wf_ref, low_ref, up_ref,
-    dx_ref, dlow_ref, dup_ref, wbuf, sem,
-):
-    for b in range(blocks):
-        fetch_rows(gathered, wbuf, sem, shares, b)
+        name=name,
+    )(place, *sources, *operands)
+
+
+def project(place, sources, normed, low, up):
+    length, depth = normed.shape
+    wide = len(sources) // 2 * sources[0].shape[2]
+    out = jax.ShapeDtypeStruct((length, wide // 4), bf16)
+    return placed_call(
+        project_kernel,
+        (normed, low, up),
+        place,
+        sources,
+        (out, out, out, jax.ShapeDtypeStruct((length, wide // 4), f32)),
+        2 * length * depth * wide,
+        12 * length * depth,
+        "project",
+    )
+
+
+def project_back_kernel(blocks, cols, place, *refs):
+    sources, refs = refs[: 2 * blocks], refs[2 * blocks :]
+    dq_ref, dk_ref, dv_ref, dgate_ref, tail_ref, wf_ref, low_ref, up_ref = refs[:8]
+    dx_ref, dlow_ref, dup_ref, wbuf, sem = refs[8:]
+    fetch_placed(place, sources, wbuf, sem)
     dup_ref[...] = jnp.zeros_like(dup_ref)
     for b in range(blocks):
         wait_rows(wbuf, sem, b)
@@ -150,30 +178,23 @@
     lax.fori_loop(0, dx_ref.shape[0] // BLOCK, step, 0)
 
 
-def project_back(gathered, dq, dk, dv, dgate, tail, wf, low, up):
-    shares, blocks, part, wide = gathered.shape
-    depth, length, ranks = shares * part, dq.shape[0], low.shape[1]
-    return pl.pallas_call(
-        functools.partial(project_back_kernel, shares, blocks, wide // 4),
-        out_shape=(
+def project_back(place, sources, dq, dk, dv, dgate, tail, wf, low, up):
+    length, ranks = low.shape
+    depth, blocks, wide = wf.shape[0], len(sources) // 2, sources[0].shape[2]
+    return placed_call(
+        project_back_kernel,
+        (dq, dk, dv, dgate, tail, wf, low, up),
+        place,
+        sources,
+        (
             jax.ShapeDtypeStruct((length, depth), bf16),
             jax.ShapeDtypeStruct((length, ranks), bf16),
             jax.ShapeDtypeStruct((blocks, ranks, wide), f32),
         ),
-        in_specs=[ANY] + [WHOLE] * 8,
-        out_specs=(WHOLE,) * 3,
-        scratch_shapes=[
-            pltpu.VMEM((blocks, depth, wide), bf16),
-            pltpu.SemaphoreType.DMA((blocks,)),
-        ],
-        cost_estimate=pl.CostEstimate(
-            flops=2 * length * depth * blocks * wide,
-            bytes_accessed=2 * depth * blocks * wide + 8 * length * depth,
-            transcendentals=0,
-        ),
-        compiler_params=pltpu.CompilerParams(vmem_limit_bytes=VMEM_LIMIT),
-        name="project_back",
-    )(gathered, dq, dk, dv, dgate, tail, wf, low, up)
+        2 * length * depth * blocks * wide,
+        8 * length * depth,
+        "project_back",
+    )
 
 
 def out_kernel(shares, ny, nx, cols, start, gathered, base_ref, merged_ref, out_ref, wbuf, sem):
@@ -592,8 +613,12 @@
     tokens_all = in_order(
         [shift(tokens_in, "x", nx, d) if d else tokens_in for d in range(nx)], x, nx
     )
-    w_all = lax.all_gather(w_in[0].reshape(d_fsdp, 4 * cols_t), ("z", "c", "y"))
-    w_all = w_all.reshape(n_fsdp, ny, d_fsdp, 4 * cols_t)
+    w_own = w_in[0].reshape(1, d_fsdp, 4 * cols_t)
+    w_own = jnp.concatenate([shift(w_own, "z", nz, d) if d else w_own for d in range(nz)], 0)
+    w_all = [shift(w_own, "y", ny, d) if d else w_own for d in range(ny)]
+    w_all = [[piece, shift(piece, "c", 2, 1)] for piece in w_all]
+    w_all = [piece for pair in w_all for piece in pair]
+    place = jnp.stack([z, c, y]).astype(jnp.int32)
     n_chunk = max(1, ff_t // (2 * BLOCK))
     width = ff_t // n_chunk
     w_gate, w_up = w_gate_up[0][:, 0], w_gate_up[0][:, 1]
@@ -696,7 +721,7 @@
     cum = cum[:, :local_heads] + cum[:, local_heads : 2 * local_heads] + cum[:, 2 * local_heads :]
     cum = jnp.repeat(cum, HEAD, axis=1)
 
-    q, k, v, gate = project(w_all, normed_all, la, up_in)
+    q, k, v, gate = project(place, w_all, normed_all, la, up_in)
     my_starts = lax.dynamic_index_in_dim(piece_starts, y, 0, keepdims=False)
     merged, mixed, lse = attend(my_starts, q, k, v, gate, cum)
 
@@ -764,7 +789,7 @@
 
     lane_pad = ((0, 0), (0, -local_heads % LANES))
     grad_x, grad_la, grad_up = project_back(
-        w_all, dq, dk, dv, dgate, jnp.pad(dforget, lane_pad), jnp.pad(wf, lane_pad), la, up_in
+        place, w_all, dq, dk, dv, dgate, jnp.pad(dforget, lane_pad), jnp.pad(wf, lane_pad), la, up_in
     )
     grad_la = jnp.concatenate([grad_la, mm(dforget, bf, ((1,), (1,))).astype(bf16)], 1)
     grad_forget_b = mm(la_forget, dforget, ((0,), (0,)))

time: 694 us -> 645 us (0.929)
  waiting for transfers between devices: 263 us -> 195 us
  starting transfers between devices: 27.7 us -> 36.5 us
    all_gather x2, waiting for transfers between devices: 123 us -> 14.7 us  [on_device(): piece = lax.all_gather(piece, everyone)]
    ppermute x5 -> x11, waiting for transfers between devices: 62.1 us -> 140 us  [shift(): lax.ppermute(value, axis, [(i, (i + step) % size) for i in range(size)])]
    all_to_all x1, waiting for transfers between devices: 38.7 us -> 6.03 us  [on_device(): chosen = lax.all_to_all(chosen, everyone, 0, 0, tiled=True)]
    ppermute x5 -> x11, starting transfers between devices: 6.83 us -> 14.7 us  [shift(): lax.ppermute(value, axis, [(i, (i + step) % size) for i in range(size)])]
    unnamed x160 -> x157, local copies, waits for them, and re-layouts: 27.3 us -> 33.1 us
  transfers between devices with their start and end apart: 13 -> 18, of which waited for: 10 -> 11; matrix products, arithmetic and copies ran while one was open for 17% -> 19% of each run, Pallas kernels for 13% -> 15%
where the time goes in v3:
time: 645 us; the launch traced here: 639 us
  Pallas kernels  214 us (33%)
  waiting for transfers between devices  195 us (30%)
  local copies, waits for them, and re-layouts  103 us (16%)
  other arithmetic  45.1 us (7%)
  starting transfers between devices  36.5 us (6%)
  matrix products  28.4 us (4%)
  between operations  16.4 us (3%)
    ppermute x11, waiting for transfers between devices, shift(): lax.ppermute(value, axis, [(i, (i + step) % size) for i in range(size)])  140 us
    pallas_call x2, Pallas kernels, mlp_call(): pl.pallas_call(functools.partial(mlp_kernel, shares, units, first, width)...  64.5 us
    pallas_call x1, Pallas kernels, attend_back(): prefetch_call(functools.partial(attend_back_kernel, length), (pairs,), [f...  55.5 us
    pallas_call x2, Pallas kernels, placed_call(): pl.pallas_call(functools.partial(kernel, blocks, wide // 4), out_shape=ou...  44.2 us
    unnamed x157, local copies, waits for them, and re-layouts  33.1 us
    pallas_call x1, Pallas kernels, attend(): prefetch_call(functools.partial(attend_kernel, length), (pairs,), [flat]...  31.4 us
    dot_general x25, matrix products, mm(): lax.dot_general(left, right, ((dims[0], dims[1]), ((), ())), preferred_el...  28.4 us
    all_to_all x1, waiting for transfers between devices, on_device(): sent = lax.all_to_all(sent, everyone, 0, 0, tiled=True)  20.9 us
  transfers between devices with their start and end apart: 18, of which 11 were waited for; matrix products, arithmetic and copies ran while one was open for 19% of the time, Pallas kernels for 15%

profile of v3, /device:TPU:0, one launch (start us, length us, event | category | flops | bytes accessed | tf_op | source)
XLA Modules:
  0.0 638.8 jit_solution(6614648999771871431)
XLA Ops:
  23.0 4.4 all-to-all-start
  30.1 5.1 collective-permute-done
  36.1 51.5 %collective-permute-done.1 = bf16[1,192,1536]{2,1,0:T(8,128)(2,1)} collective-permute-done((bf16[1,192,1536]{2,1,0:T(8,128)(2,1)S(1)}, bf16[1,192,1536]{2,1,0:T(8,128)(2,1)}, u32[]{:S(2)}, u32[]{:S(2)}) %collective-permute-start.1) | collective-permute-done | bytes 589856 | tf_op jit(solution)/shard_map/ppermute | solution.py:32
  97.7 7.3 %all-to-all-start.1 = ((bf16[8,16,624]{2,1,0:T(8,128)(2,1)}), bf16[8,16,624]{2,1,0:T(8,128)(2,1)S(1)}, u32[]{:S(2)}, u32[]{:S(2)}) async-start(bf16[8,16,624]{2,1,0:T(8,128)(2,1)} %pad_maximum_fusion.5), calls=%async_computation.1 | async-start | bytes 327680 | tf_op jit(solution)/shard_map/all_to_all | solution.py:650
  106.8 10.9 %all-to-all-done.1 = bf16[8,16,624]{2,1,0:T(8,128)(2,1)S(1)} async-done(((bf16[8,16,624]{2,1,0:T(8,128)(2,1)}), bf16[8,16,624]{2,1,0:T(8,128)(2,1)S(1)}, u32[]{:S(2)}, u32[]{:S(2)}) %all-to-all-start.1) | async-done | bytes 159776 | tf_op jit(solution)/shard_map/all_to_all | solution.py:650
  140.2 30.8 %collective-permute-done.4.refs_2_ = bf16[4,192,1536]{2,1,0:T(8,128)(2,1)} collective-permute-done((bf16[4,192,1536]{2,1,0:T(8,128)(2,1)}, bf16[4,192,1536]{2,1,0:T(8,128)(2,1)}, u32[]{:S(2)}, u32[]{:S(2)}) %collective-permute-start.4) | collective-permute-done | bytes 2359328 | tf_op jit(solution)/shard_map/ppermute | solution.py:32
  174.7 6.0 all-to-all-done.2
  180.8 5.7 reshape.417
  210.9 20.6 %project.1 = (bf16[1024,768]{1,0:T(8,128)(2,1)}, bf16[1024,768]{1,0:T(8,128)(2,1)}, bf16[1024,768]{1,0:T(8,128)(2,1)}, f32[1024,768]{1,0:T(8,128)}) custom-call(s32[3]{0:T(128)} %pad_add_fusion.place, bf16[4,192,1536]{2,1,0:T(8,128)(2,1)} %constant_dynamic-update-slice_fusion.refs_0_, bf16[4,192,1536]{2,1,0:T(8,128)(2,1)} %collective-permute-done.3.refs_1_, ...), custom_call_target="tpu_custom_call" | custom-call | flops 9663676416 | bytes 28311552 | tf_op jit(solution)/shard_map/project/pallas_call | solution.py:114
  231.6 31.4 %attend.1 = (bf16[1024,768]{1,0:T(8,128)(2,1)}, f32[1024,768]{1,0:T(8,128)}, f32[1024,768]{1,0:T(8,128)}) custom-call(s32[2]{0:T(128)} %fusion.70.starts_ref, bf16[1024,768]{1,0:T(8,128)(2,1)} %get-tuple-element.34.q_ref, bf16[1024,768]{1,0:T(8,128)(2,1)} %get-tuple-element.35.k_ref, bf16[1024,768]{1,0:T(8,128)(2,1)} %get-tuple-element.36.v_ref, ...), custom_call_target="tpu_custom_call" | custom-call | flops 7549747200 | bytes 20447232 | tf_op jit(solution)/shard_map/attend/pallas_call | solution.py:423
  281.8 12.1 %collective-permute-done.7 = bf16[512,768]{1,0:T(8,128)(2,1)} collective-permute-done((bf16[512,768]{1,0:T(8,128)(2,1)}, bf16[512,768]{1,0:T(8,128)(2,1)}, u32[]{:S(2)}, u32[]{:S(2)}) %collective-permute-start.7) | collective-permute-done | bytes 786464 | tf_op jit(solution)/shard_map/ppermute | solution.py:32
  299.2 9.7 %out_project.1 = f32[512,1536]{1,0:T(8,128)} custom-call(bf16[8,4,192,1920]{3,2,1,0:T(8,128)(2,1)} %bitcast.210, f32[512,1536]{1,0:T(8,128)} %convert_add_fusion.base_ref, bf16[512,1536]{1,0:T(8,128)(2,1)} %copy-done.5), custom_call_target="tpu_custom_call" | custom-call | flops 2415919104 | bytes 11010048 | tf_op jit(solution)/shard_map/out_project/pallas_call | solution.py:225
  314.9 31.3 %feed_forward.2 = (f32[512,1536]{1,0:T(8,128)}, f32[512,1536]{1,0:T(8,128)}, f32[512,64]{1,0:T(8,128)}, bf16[4,64,512]{2,1,0:T(8,128)(2,1)}) custom-call(bf16[8,4,192,1920]{3,2,1,0:T(8,128)(2,1)} %bitcast.211, bf16[512,1536]{1,0:T(8,128)(2,1)} %copy-done.11, bf16[512,1536]{1,0:T(8,128)(2,1)} %refs_2_.3, bf16[512,64]{1,0:T(8,128)(2,1)} %maximum_maximum_fusion.1.refs_3_, ...), custom_call_target="tpu_custom_call" | custom-call | flops 19327352832 | bytes 34603008 | tf_op jit(solution)/shard_map/feed_forward/pallas_call | solution.py:299
  346.2 14.7 %all-gather.7.cloned.1.call-done = bf16[6144,1536]{1,0:T(8,128)(2,1)} async-done(((bf16[192,1536]{1,0:T(8,128)(2,1)}), bf16[6144,1536]{1,0:T(8,128)(2,1)}) %all-gather.7.cloned.1.call-update) | async-done | bytes 18874384 | tf_op jit(solution)/shard_map/all_gather | solution.py:631
  360.9 33.2 %feed_forward.3 = (f32[512,1536]{1,0:T(8,128)}, f32[512,1536]{1,0:T(8,128)}, f32[512,64]{1,0:T(8,128)}, bf16[4,64,512]{2,1,0:T(8,128)(2,1)}) custom-call(bf16[8,4,192,1536]{3,2,1,0:T(8,128)(2,1)} %bitcast.270, bf16[512,1536]{1,0:T(8,128)(2,1)} %copy-done.11, bf16[512,1536]{1,0:T(8,128)(2,1)} %refs_2_.3, bf16[512,64]{1,0:T(8,128)(2,1)} %maximum_maximum_fusion.1.refs_3_, ...), custom_call_target="tpu_custom_call" | custom-call | flops 19327352832 | bytes 34603008 | tf_op jit(solution)/shard_map/feed_forward/pallas_call | solution.py:299
  407.6 8.4 %out_project_back.1 = bf16[512,1536]{1,0:T(8,128)(2,1)} custom-call(bf16[8,4,192,1920]{3,2,1,0:T(8,128)(2,1)} %bitcast.212, bf16[512,1536]{1,0:T(8,128)(2,1)} %copy-done.7, bf16[512,16]{1,0:T(8,128)(2,1)} %convolution_convert_fusion.8.low_ref, bf16[16,1536]{1,0:T(8,128)(2,1)} %reshape.375.up_ref), custom_call_target="tpu_custom_call" | custom-call | flops 2415919104 | bytes 11010048 | tf_op jit(solution)/shard_map/out_project_back/pallas_call | solution.py:225
  421.6 15.9 %collective-permute-done.8 = bf16[512,768]{1,0:T(8,128)(2,1)S(1)} collective-permute-done((bf16[512,768]{1,0:T(8,128)(2,1)S(1)}, bf16[512,768]{1,0:T(8,128)(2,1)S(1)}, u32[]{:S(2)}, u32[]{:S(2)}) %collective-permute-start.8) | collective-permute-done | bytes 786464 | tf_op jit(solution)/shard_map/ppermute | solution.py:32
  439.3 55.5 %attend_back.1 = (bf16[1024,768]{1,0:T(8,128)(2,1)}, bf16[1024,768]{1,0:T(8,128)(2,1)}, bf16[1024,768]{1,0:T(8,128)(2,1)}, bf16[1024,768]{1,0:T(8,128)(2,1)}, f32[1024,768]{1,0:T(8,128)}) custom-call(s32[2]{0:T(128)} %fusion.70.starts_ref, bf16[1024,768]{1,0:T(8,128)(2,1)} %get-tuple-element.34.q_ref, bf16[1024,768]{1,0:T(8,128)(2,1)} %get-tuple-element.35.k_ref, ...), custom_call_target="tpu_custom_call" | custom-call | flops 18874368000 | bytes 26738688 | tf_op jit(solution)/shard_map/attend_back/pallas_call | solution.py:525
  494.8 4.5 slice.205
  501.9 23.5 %project_back.1 = (bf16[1024,1536]{1,0:T(8,128)(2,1)}, bf16[1024,64]{1,0:T(8,128)(2,1)}, f32[2,64,1536]{2,1,0:T(8,128)}) custom-call(s32[3]{0:T(128)} %pad_add_fusion.place, bf16[4,192,1536]{2,1,0:T(8,128)(2,1)} %constant_dynamic-update-slice_fusion.refs_0_, bf16[4,192,1536]{2,1,0:T(8,128)(2,1)} %collective-permute-done.3.refs_1_, ...), custom_call_target="tpu_custom_call" | custom-call | flops 9663676416 | bytes 22020096 | tf_op jit(solution)/shard_map/project_back/pallas_call | solution.py:114
  542.0 24.9 %collective-permute-done.10 = bf16[512,80]{1,0:T(8,128)(2,1)} collective-permute-done((bf16[512,80]{1,0:T(8,128)(2,1)}, bf16[512,80]{1,0:T(8,128)(2,1)}, u32[]{:S(2)}, u32[]{:S(2)}) %collective-permute-start.10) | collective-permute-done | bytes 81952 | tf_op jit(solution)/shard_map/ppermute | solution.py:32
  568.0 4.7 fusion.7
  586.9 6.6 %fusion.10 = f32[512,1536]{1,0:T(8,128)} fusion(f32[512,1536]{1,0:T(8,128)} %get-tuple-element.126, bf16[512,1536]{1,0:T(8,128)(2,1)S(1)} %copy-done.4, f32[512]{0:T(512)S(1)} %broadcast_multiply_fusion, f32[512]{0:T(512)S(1)} %get-tuple-element.155, f32[512]{0:T(512)S(1)} %get-tuple-element.154, f32[1536]{0:T(1024)S(1)} %reshape.404, ...), kind=kLoop, calls=%fused_computation.20 | loop fusion | flops 8650752 | bytes 14168068 | tf_op jit(solution)/shard_map/add | solution.py:805
  593.4 20.9 %all-to-all-done.3 = bf16[32,2,8496]{2,1,0:T(2,128)(2,1)S(1)} async-done(((bf16[32,2,8496]{2,1,0:T(2,128)(2,1)}), bf16[32,2,8496]{2,1,0:T(2,128)(2,1)S(1)}, u32[]{:S(2)}, u32[]{:S(2)}) %all-to-all-start.3) | async-done | bytes 1087520 | tf_op jit(solution)/shard_map/all_to_all | solution.py:842
  (387 shorter events, 182.7 us)
Async XLA Ops:
  7.2 97.8 %copy-start = (s32[2,2]{1,0:T(2,128)S(1)}, s32[2,2]{1,0:T(2,128)}, u32[]{:S(2)}) copy-start(s32[2,2]{1,0:T(2,128)} %param.23) | copy-start | bytes 52
  7.2 292.0 %all-gather.5.cloned.1.call-start = ((), (), s32[]{:S(2)}) async-start(), calls=%async_computation.5 | async-start | bytes 24330240 | tf_op jit(solution)/shard_map/all_gather | solution.py:631
  10.8 350.1 %all-gather.7.cloned.1.call-start = ((), (), s32[]{:S(2)}) async-start(), calls=%async_computation.6 | async-start | bytes 19464192 | tf_op jit(solution)/shard_map/all_gather | solution.py:631
  12.0 23.2 %collective-permute-start = (bf16[1,192,1536]{2,1,0:T(8,128)(2,1)S(1)}, bf16[1,192,1536]{2,1,0:T(8,128)(2,1)S(1)}, u32[]{:S(2)}, u32[]{:S(2)}) collective-permute-start(bf16[1,192,1536]{2,1,0:T(8,128)(2,1)S(1)} %reshape_squeeze.33), channel_id=1, source_target_pairs={{0,8},{8,16},{16,24},{24,0},{1,9},{9,17},{17,25},{25,1},{2,10},{10... | collective-permute-start | bytes 1769480 | tf_op jit(solution)/shard_map/ppermute | solution.py:32
  15.1 74.5 %collective-permute-start.2 = (bf16[1,192,1536]{2,1,0:T(8,128)(2,1)S(1)}, bf16[1,192,1536]{2,1,0:T(8,128)(2,1)S(1)}, u32[]{:S(2)}, u32[]{:S(2)}) collective-permute-start(bf16[1,192,1536]{2,1,0:T(8,128)(2,1)S(1)} %reshape_squeeze.33), channel_id=1, source_target_pairs={{0,24},{8,0},{16,8},{24,16},{1,25},{9,1},{17,9},{25,17},{2,26},{10... | collective-permute-start | bytes 1769480 | tf_op jit(solution)/shard_map/ppermute | solution.py:32
  17.2 70.4 %collective-permute-start.1 = (bf16[1,192,1536]{2,1,0:T(8,128)(2,1)S(1)}, bf16[1,192,1536]{2,1,0:T(8,128)(2,1)}, u32[]{:S(2)}, u32[]{:S(2)}) collective-permute-start(bf16[1,192,1536]{2,1,0:T(8,128)(2,1)S(1)} %reshape_squeeze.33), channel_id=1, source_target_pairs={{0,16},{8,24},{16,0},{24,8},{1,17},{9,25},{17,1},{25,9},{2,18},{10... | collective-permute-start | bytes 1769480 | tf_op jit(solution)/shard_map/ppermute | solution.py:32
  21.3 72.9 %copy-start.43 = (bf16[1,2,16,1024]{3,2,1,0:T(8,128)(2,1)S(1)}, bf16[1,2,16,1024]{3,2,1,0:T(8,128)(2,1)}, u32[]{:S(2)}) copy-start(bf16[1,2,16,1024]{3,2,1,0:T(8,128)(2,1)} %param.39) | copy-start | bytes 196612
  23.0 74.7 %all-to-all-start = ((bf16[32,2,676]{2,1,0:T(2,128)(2,1)}), bf16[32,2,676]{2,1,0:T(2,128)(2,1)S(1)}, u32[]{:S(2)}, u32[]{:S(2)}) async-start(bf16[32,2,676]{2,1,0:T(2,128)(2,1)} %reshape.414), calls=%async_computation | async-start | bytes 196608 | tf_op jit(solution)/shard_map/all_to_all | solution.py:589
  27.4 110.2 %collective-permute-start.6 = (bf16[512,1536]{1,0:T(8,128)(2,1)S(1)}, bf16[512,1536]{1,0:T(8,128)(2,1)}, u32[]{:S(2)}, u32[]{:S(2)}) collective-permute-start(bf16[512,1536]{1,0:T(8,128)(2,1)S(1)} %copy-done.3), channel_id=1, source_target_pairs={{0,1},{1,0},{2,3},{3,2},{4,5},{5,4},{6,7},{7,6},{8,9},{9,8},{10,11... | collective-permute-start | bytes 4718600 | tf_op jit(solution)/shard_map/ppermute | solution.py:32
  29.2 67.1 %copy-start.47 = (bf16[1,128,48]{1,2,0:T(8,128)(2,1)S(1)}, bf16[1,128,48]{1,2,0:T(8,128)(2,1)}, u32[]{:S(2)}) copy-start(bf16[1,128,48]{1,2,0:T(8,128)(2,1)} %param.37) | copy-start | bytes 36868
  29.2 68.0 %copy-start.46 = (bf16[1,48,256]{2,1,0:T(8,128)(2,1)S(1)}, bf16[1,48,256]{2,1,0:T(8,128)(2,1)}, u32[]{:S(2)}) copy-start(bf16[1,48,256]{2,1,0:T(8,128)(2,1)} %param.38) | copy-start | bytes 73732
  90.4 80.6 %collective-permute-start.4 = (bf16[4,192,1536]{2,1,0:T(8,128)(2,1)}, bf16[4,192,1536]{2,1,0:T(8,128)(2,1)}, u32[]{:S(2)}, u32[]{:S(2)}) collective-permute-start(bf16[4,192,1536]{2,1,0:T(8,128)(2,1)} %constant_dynamic-update-slice_fusion.refs_0_), channel_id=1, source_target_pairs={{0,2},{2,0},{1,3},{3,1},{4,6},{6,4},{5,7},{7,5},{8,10},{10,8},{9,1... | collective-permute-start | bytes 7077896 | tf_op jit(solution)/shard_map/ppermute | solution.py:32
  97.7 20.0 %all-to-all-start.1 = ((bf16[8,16,624]{2,1,0:T(8,128)(2,1)}), bf16[8,16,624]{2,1,0:T(8,128)(2,1)S(1)}, u32[]{:S(2)}, u32[]{:S(2)}) async-start(bf16[8,16,624]{2,1,0:T(8,128)(2,1)} %pad_maximum_fusion.5), calls=%async_computation.1 | async-start | bytes 327680 | tf_op jit(solution)/shard_map/all_to_all | solution.py:650
  122.7 58.1 %all-to-all-start.2 = ((bf16[32,2,8448]{2,1,0:T(2,128)(2,1)}), bf16[32,2,8448]{2,1,0:T(2,128)(2,1)}, u32[]{:S(2)}, u32[]{:S(2)}) async-start(bf16[32,2,8448]{2,1,0:T(2,128)(2,1)} %reshape.416), calls=%async_computation.2 | async-start | bytes 2162688 | tf_op jit(solution)/shard_map/all_to_all | solution.py:668
  137.1 64.5 %copy-start.50 = (f32[12]{0:T(128)}, f32[12]{0:T(128)S(1)}, u32[]{:S(2)}) copy-start(f32[12]{0:T(128)S(1)} %convolution_bitcast_fusion) | copy-start | bytes 148
  137.3 62.4 %copy-start.45 = (bf16[128,12]{1,0:T(8,128)(2,1)}, bf16[128,12]{1,0:T(8,128)(2,1)S(1)}, u32[]{:S(2)}) copy-start(bf16[128,12]{1,0:T(8,128)(2,1)S(1)} %fusion.59) | copy-start | bytes 9220
  137.3 73.6 %collective-permute-start.3 = (bf16[4,192,1536]{2,1,0:T(8,128)(2,1)}, bf16[4,192,1536]{2,1,0:T(8,128)(2,1)}, u32[]{:S(2)}, u32[]{:S(2)}) collective-permute-start(bf16[4,192,1536]{2,1,0:T(8,128)(2,1)} %constant_dynamic-update-slice_fusion.refs_0_), channel_id=1, source_target_pairs={{0,4},{4,0},{1,5},{5,1},{2,6},{6,2},{3,7},{7,3},{8,12},{12,8},{9,1... | collective-permute-start | bytes 7077896 | tf_op jit(solution)/shard_map/ppermute | solution.py:32
  171.0 39.9 %collective-permute-start.5 = (bf16[4,192,1536]{2,1,0:T(8,128)(2,1)}, bf16[4,192,1536]{2,1,0:T(8,128)(2,1)}, u32[]{:S(2)}, u32[]{:S(2)}) collective-permute-start(bf16[4,192,1536]{2,1,0:T(8,128)(2,1)} %collective-permute-done.4.refs_2_), channel_id=1, source_target_pairs={{0,4},{4,0},{1,5},{5,1},{2,6},{6,2},{3,7},{7,3},{8,12},{12,8},{9,1... | collective-permute-start | bytes 7077896 | tf_op jit(solution)/shard_map/ppermute | solution.py:32
  265.9 28.0 %collective-permute-start.7 = (bf16[512,768]{1,0:T(8,128)(2,1)}, bf16[512,768]{1,0:T(8,128)(2,1)}, u32[]{:S(2)}, u32[]{:S(2)}) collective-permute-start(bf16[512,768]{1,0:T(8,128)(2,1)} %get-tuple-element.131), channel_id=1, source_target_pairs={{0,1},{1,0},{2,3},{3,2},{4,5},{5,4},{6,7},{7,6},{8,9},{9,8},{10,11... | collective-permute-start | bytes 2359304 | tf_op jit(solution)/shard_map/ppermute | solution.py:32
  417.7 19.8 %collective-permute-start.8 = (bf16[512,768]{1,0:T(8,128)(2,1)S(1)}, bf16[512,768]{1,0:T(8,128)(2,1)S(1)}, u32[]{:S(2)}, u32[]{:S(2)}) collective-permute-start(bf16[512,768]{1,0:T(8,128)(2,1)S(1)} %get-tuple-element.129), channel_id=1, source_target_pairs={{0,1},{1,0},{2,3},{3,2},{4,5},{5,4},{6,7},{7,6},{8,9},{9,8},{10,11... | collective-permute-start | bytes 2359304 | tf_op jit(solution)/shard_map/ppermute | solution.py:32
  528.1 39.9 %collective-permute-start.9 = (bf16[512,1536]{1,0:T(8,128)(2,1)}, bf16[512,1536]{1,0:T(8,128)(2,1)}, u32[]{:S(2)}, u32[]{:S(2)}) collective-permute-start(bf16[512,1536]{1,0:T(8,128)(2,1)} %constant_dynamic-slice_fusion), channel_id=1, source_target_pairs={{0,1},{1,0},{2,3},{3,2},{4,5},{5,4},{6,7},{7,6},{8,9},{9,8},{10,11... | collective-permute-start | bytes 4718600 | tf_op jit(solution)/shard_map/ppermute | solution.py:32
  537.7 29.3 %collective-permute-start.10 = (bf16[512,80]{1,0:T(8,128)(2,1)}, bf16[512,80]{1,0:T(8,128)(2,1)}, u32[]{:S(2)}, u32[]{:S(2)}) collective-permute-start(bf16[512,80]{1,0:T(8,128)(2,1)} %fusion.43), channel_id=1, source_target_pairs={{0,1},{1,0},{2,3},{3,2},{4,5},{5,4},{6,7},{7,6},{8,9},{9,8},{10,11... | collective-permute-start | bytes 245768 | tf_op jit(solution)/shard_map/ppermute | solution.py:32
  583.8 30.5 %all-to-all-start.3 = ((bf16[32,2,8496]{2,1,0:T(2,128)(2,1)}), bf16[32,2,8496]{2,1,0:T(2,128)(2,1)S(1)}, u32[]{:S(2)}, u32[]{:S(2)}) async-start(bf16[32,2,8496]{2,1,0:T(2,128)(2,1)} %reshape.418), calls=%async_computation.3 | async-start | bytes 2195456 | tf_op jit(solution)/shard_map/all_to_all | solution.py:842
  617.5 10.5 %all-to-all-start.4 = ((bf16[8,16,624]{2,1,0:T(8,128)(2,1)}), bf16[8,16,624]{2,1,0:T(8,128)(2,1)S(1)}, u32[]{:S(2)}, u32[]{:S(2)}) async-start(bf16[8,16,624]{2,1,0:T(8,128)(2,1)} %convert_element_type.178), calls=%async_computation.4 | async-start | bytes 327680 | tf_op jit(solution)/shard_map/all_to_all | solution.py:861
  (55 other events, 456.2 us)
Sparse Core Ops, SparseCore 0:
  11.0 215.5 all-gather.4
  229.4 131.4 all-gather.6
